TPU v7x, 32 devices: a whole 2x2x4 slice. The times are simulated.
32 devices in a mesh: dp: 8 (over z, x), tensor: 4 (over y, core).
Axes of the slice: x: 2, y: 2, z: 4, core: 2. Of those that a mesh axis runs over, the one named last changes fastest.
Arguments:
- block_input: bfloat16 [8, 512, 2048], P('dp'), may hold values from -6 to 6
- out_grad: bfloat16 [8, 512, 2048], P('dp'), may hold values from -6 to 6
- seg_ids: int32 [8, 512], P('dp'), may hold values from 0 to 5, never falling along the last dimension, each value on 1 to 400 neighbouring positions
- slot_live: int32 [8], P('dp'), may hold values 0 or 1
- norm_gain: float32 [2048], replicated, may hold values from 0.5 to 1.5
- z_weight: float32 [2048, 4096], P('dp', 'tensor'), may hold values from -0.125 to 0.125
- x_weight: float32 [2048, 4096], P('dp', 'tensor'), may hold values from -0.125 to 0.125
- bc_weight: float32 [2048, 256], P('dp'), may hold values from -0.125 to 0.125
- dt_weight: float32 [2048, 64], P('dp', 'tensor'), may hold values from -0.125 to 0.125
- conv_x: float32 [4, 4096], P(None, 'tensor'), may hold values from -3 to 3
- conv_bc: float32 [4, 256], replicated, may hold values from -3 to 3
- head_params: float32 [3, 64], P(None, 'tensor'), may hold values from -5 to 3, as said below
- gated_gain: float32 [4096], P('tensor'), may hold values from 0.5 to 1.5
- out_weight: float32 [2048, 4096], P('dp', 'tensor'), may hold values from -0.09375 to 0.09375
- norm_gain_sq: float32 [2048], replicated, may hold values from 64 to 1024
- z_rows: float32 [2048], P('dp'), may hold values from 32 to 8192, as said below
- z_cols: float32 [4096], P('tensor'), may hold values from 64 to 1024
- x_rows: float32 [2048], P('dp'), may hold values from 32 to 8192, as said below
- x_cols: float32 [4096], P('tensor'), may hold values from 64 to 1024
- bc_rows: float32 [2048], P('dp'), may hold values from 32 to 8192, as said below
- bc_cols: float32 [256], replicated, may hold values from 64 to 1024
- dt_rows: float32 [2048], P('dp'), may hold values from 32 to 8192, as said below
- dt_cols: float32 [64], P('tensor'), may hold values from 64 to 1024
- conv_x_sq: float32 [4, 4096], P(None, 'tensor'), may hold values from 64 to 1024
- conv_bc_sq: float32 [4, 256], replicated, may hold values from 64 to 1024
- head_sq: float32 [3, 64], P(None, 'tensor'), may hold values from 64 to 1024
- gated_gain_sq: float32 [4096], P('tensor'), may hold values from 64 to 1024
- out_rows: float32 [2048], P('dp'), may hold values from 32 to 8192, as said below
- out_cols: float32 [4096], P('tensor'), may hold values from 64 to 1024
Outputs:
- output: bfloat16 [8, 512, 2048], P('dp')
- input_grad: bfloat16 [8, 512, 2048], P('dp')
- norm_gain_grad: float32 [2048], replicated
- norm_gain_update: float32 [2048], replicated
- norm_gain_sq_new: float32 [2048], replicated
- z_grad: float32 [2048, 4096], P('dp', 'tensor')
- z_update: float32 [2048, 4096], P('dp', 'tensor')
- z_rows_new: float32 [2048], P('dp')
- z_cols_new: float32 [4096], P('tensor')
- x_grad: float32 [2048, 4096], P('dp', 'tensor')
- x_update: float32 [2048, 4096], P('dp', 'tensor')
- x_rows_new: float32 [2048], P('dp')
- x_cols_new: float32 [4096], P('tensor')
- bc_grad: float32 [2048, 256], P('dp')
- bc_update: float32 [2048, 256], P('dp')
- bc_rows_new: float32 [2048], P('dp')
- bc_cols_new: float32 [256], replicated
- dt_grad: float32 [2048, 64], P('dp', 'tensor')
- dt_update: float32 [2048, 64], P('dp', 'tensor')
- dt_rows_new: float32 [2048], P('dp')
- dt_cols_new: float32 [64], P('tensor')
- conv_x_grad: float32 [4, 4096], P(None, 'tensor')
- conv_x_update: float32 [4, 4096], P(None, 'tensor')
- conv_x_sq_new: float32 [4, 4096], P(None, 'tensor')
- conv_bc_grad: float32 [4, 256], replicated
- conv_bc_update: float32 [4, 256], replicated
- conv_bc_sq_new: float32 [4, 256], replicated
- head_grad: float32 [3, 64], P(None, 'tensor')
- head_update: float32 [3, 64], P(None, 'tensor')
- head_sq_new: float32 [3, 64], P(None, 'tensor')
- gated_gain_grad: float32 [4096], P('tensor')
- gated_gain_update: float32 [4096], P('tensor')
- gated_gain_sq_new: float32 [4096], P('tensor')
- out_grad_w: float32 [2048, 4096], P('dp', 'tensor')
- out_update: float32 [2048, 4096], P('dp', 'tensor')
- out_rows_new: float32 [2048], P('dp')
- out_cols_new: float32 [4096], P('tensor')
Inputs may be any that keep to these rules, and one draw needn't show every extreme that they name: `seg_ids`: in each slot the document numbers never fall and take all 6 values; each document has 1 to 400 tokens, one exactly 400. `head_params`: row 0 holds step size offsets, row 1 logarithms of decay rates, row 2 skip gains. `z_rows`: positive. `x_rows`: positive. `bc_rows`: positive. `dt_rows`: positive. `out_rows`: positive.
All inputs are finite; a program needn't handle non-finite values. No bound on the sum of `slot_live` on one device may be relied on, other than what follows from the above.
Results may differ from a plain program's by a relative error of at most 0.0044.
The roundings to bfloat16 on the way count: a program that leaves them out, or rounds other values in their place, can miss the bound.
Values may be sent and summed in bfloat16 or wider, within the bound.
No kernel may reach another device: no remote copies, remote signals or barrier semaphores. Data moves between devices by JAX's collectives and lax.ppermute only.
A program may use at most 192 MiB of HBM per device.

v0:
```python
import jax
import jax.numpy as jnp
from jax import lax
from jax.sharding import PartitionSpec as P

D = 2048
HEADS = 64
STATE = 128
INNER = 4096
KCONV = 4
STRETCH = 256


norm_eps = 1e-05
decay_rate = 0.5
tiny_eps = 1e-30
unit_eps = 1e-06
vector_rate = 0.05


def shift_down(values, offset):
    padding = jnp.zeros((offset,) + values.shape[1:], values.dtype)
    return jnp.concatenate([padding, values[:-offset]], axis=0)


def causal_conv(values, taps, segment):
    result = taps[0] * values
    for offset in range(1, taps.shape[0]):
        same_doc = jnp.concatenate(
            [jnp.zeros((offset,), jnp.bool_), segment[offset:] == segment[:-offset]]
        )
        result = result + taps[offset] * shift_down(values, offset) * same_doc[:, None].astype(
            values.dtype
        )
    return result


def state_scan(heads_x, step_size, decay_coef, b_mat, c_mat, segment):
    length, head_count, head_width = heads_x.shape
    blocks = length // STRETCH
    highest = lax.Precision.HIGHEST
    x_blocks = heads_x.reshape(blocks, STRETCH, head_count, head_width).transpose(0, 2, 3, 1)
    dt_blocks = step_size.reshape(blocks, STRETCH, head_count).transpose(0, 2, 1)
    b_blocks = b_mat.reshape(blocks, STRETCH, -1).transpose(0, 2, 1)
    c_blocks = c_mat.reshape(blocks, STRETCH, -1).transpose(0, 2, 1)
    doc_blocks = segment.reshape(blocks, STRETCH)

    def advance(carried, block_data):
        memory, prev_doc = carried
        block_x, block_dt, block_b, block_c, block_doc = block_data
        log_decay = jnp.cumsum(block_dt * decay_coef[:, None], axis=1)
        places = jnp.arange(STRETCH)
        visible = (places[:, None] >= places[None, :]) & (block_doc[:, None] == block_doc[None, :])
        visible = visible[None, :, :]
        log_gaps = log_decay[:, :, None] - log_decay[:, None, :]
        kernel = jnp.where(visible, jnp.exp(jnp.where(visible, log_gaps, 0.0)), 0.0)
        intersection = jnp.dot(block_c.T, block_b, precision=highest)
        mixing = intersection[None, :, :] * kernel * block_dt[:, None, :]
        inside = jnp.einsum("hts,hps->hpt", mixing, block_x, precision=highest)
        keep_prev = (block_doc == prev_doc).astype(block_x.dtype)
        carry_in = jnp.einsum("nt,hpn->hpt", block_c, memory, precision=highest)
        carry_in = carry_in * (jnp.exp(log_decay) * keep_prev[None, :])[:, None, :]
        last_doc = block_doc[-1]
        tail_weight = jnp.exp(log_decay[:, -1:] - log_decay) * block_dt
        tail_weight = tail_weight * (block_doc == last_doc).astype(block_x.dtype)[None, :]
        fresh_state = jnp.einsum("hs,hps,ns->hpn", tail_weight, block_x, block_b, precision=highest)
        kept_share = (jnp.exp(log_decay[:, -1]) * (last_doc == prev_doc).astype(block_x.dtype))[
            :, None, None
        ]
        return ((fresh_state + memory * kept_share, last_doc), inside + carry_in)

    initial = (
        jnp.zeros((head_count, head_width, b_mat.shape[1]), heads_x.dtype),
        jnp.array(-1, jnp.int32),
    )
    _, outputs = lax.scan(
        jax.checkpoint(advance), initial, (x_blocks, dt_blocks, b_blocks, c_blocks, doc_blocks)
    )
    return outputs.transpose(0, 3, 1, 2).reshape(heads_x.shape)


def mixer(gate_z, x_raw, bc_raw, dt_raw, conv_x, conv_bc, head_params, gated_gain, segment):
    head_count = dt_raw.shape[1]
    x_conv = jax.nn.silu(causal_conv(x_raw, conv_x, segment))
    bc_conv = jax.nn.silu(causal_conv(bc_raw, conv_bc, segment))
    half_width = bc_conv.shape[1] // 2
    step_size = jax.nn.softplus(dt_raw + head_params[0])
    decay_coef = -jnp.exp(head_params[1])
    heads_x = x_conv.reshape(x_conv.shape[0], head_count, -1)
    scanned = state_scan(
        heads_x, step_size, decay_coef, bc_conv[:, :half_width], bc_conv[:, half_width:], segment
    )
    scanned = scanned + head_params[2][None, :, None] * heads_x
    gated_values = scanned.reshape(x_conv.shape) * jax.nn.silu(gate_z)
    return (gated_values * gated_gain, jnp.sum(gated_values * gated_values, axis=1))


def norm_input(values, gain):
    mean_square = jnp.mean(values * values, axis=1, keepdims=True)
    return values * lax.rsqrt(mean_square + norm_eps) * gain


def rows_times(left, right):
    return lax.dot_general(
        left, right, (((1,), (1,)), ((), ())), preferred_element_type=jnp.float32
    )


def tokens_out(left, right):
    return lax.dot_general(
        left, right, (((0,), (0,)), ((), ())), preferred_element_type=jnp.float32
    )


def mix_state(old_state, fresh_term):
    return decay_rate * old_state + (1.0 - decay_rate) * fresh_term


def normalized(unit, square_total, entries):
    return unit * lax.rsqrt(square_total / entries + unit_eps)


def shards(
    block_input,
    out_grad,
    seg_ids,
    slot_live,
    norm_gain,
    z_weight,
    x_weight,
    bc_weight,
    dt_weight,
    conv_x,
    conv_bc,
    head_params,
    gated_gain,
    out_weight,
    norm_gain_sq,
    z_rows,
    z_cols,
    x_rows,
    x_cols,
    bc_rows,
    bc_cols,
    dt_rows,
    dt_cols,
    conv_x_sq,
    conv_bc_sq,
    head_sq,
    gated_gain_sq,
    out_rows,
    out_cols,
):
    data_count = lax.axis_size("dp")
    tensor_count = lax.axis_size("tensor")
    full_copies = data_count * tensor_count
    block_in = block_input[0].astype(jnp.float32)
    segment = seg_ids[0]
    live_flag = slot_live[0].astype(jnp.float32)
    low_z, low_x, low_bc, low_dt, low_out = (
        lax.all_gather(z_weight.astype(jnp.bfloat16), "dp", axis=0, tiled=True),
        lax.all_gather(x_weight.astype(jnp.bfloat16), "dp", axis=0, tiled=True),
        lax.all_gather(bc_weight.astype(jnp.bfloat16), "dp", axis=0, tiled=True),
        lax.all_gather(dt_weight.astype(jnp.bfloat16), "dp", axis=0, tiled=True),
        lax.all_gather(out_weight.astype(jnp.bfloat16), "dp", axis=0, tiled=True),
    )
    normed, norm_pull = jax.vjp(norm_input, block_in, norm_gain)
    normed_low = normed.astype(jnp.bfloat16)
    gate_z = jnp.dot(normed_low, low_z, preferred_element_type=jnp.float32)
    x_raw = jnp.dot(normed_low, low_x, preferred_element_type=jnp.float32)
    bc_raw = jnp.dot(normed_low, low_bc, preferred_element_type=jnp.float32)
    dt_raw = jnp.dot(normed_low, low_dt, preferred_element_type=jnp.float32)

    def local_mixer(gate_in, x_in_raw, bc_in_raw, dt_in_raw, taps_x, taps_bc, per_head, gain_inner):
        return mixer(
            gate_in, x_in_raw, bc_in_raw, dt_in_raw, taps_x, taps_bc, per_head, gain_inner, segment
        )

    (scaled, squares), mixer_pull = jax.vjp(
        local_mixer, gate_z, x_raw, bc_raw, dt_raw, conv_x, conv_bc, head_params, gated_gain
    )
    scaled_low = scaled.astype(jnp.bfloat16)
    projected, total_squares = lax.psum((rows_times(scaled_low, low_out), squares), "tensor")
    inv_rms = lax.rsqrt(total_squares / INNER + norm_eps)
    output = (block_in + inv_rms[:, None] * projected).astype(jnp.bfloat16)
    cotangent = out_grad[0].astype(jnp.float32) * live_flag
    proj_grad = (cotangent * inv_rms[:, None]).astype(jnp.bfloat16)
    rms_grad = jnp.sum(cotangent * projected, axis=1)
    squares_grad = rms_grad * -0.5 * inv_rms * inv_rms * inv_rms / INNER
    out_part = tokens_out(proj_grad, scaled_low)
    scaled_grad = jnp.dot(proj_grad, low_out, preferred_element_type=jnp.float32)
    (
        z_grad_raw,
        x_grad_raw,
        bc_grad_part,
        dt_grad_raw,
        convx_slot,
        convbc_part,
        head_slot,
        gated_slot,
    ) = mixer_pull((scaled_grad, squares_grad))
    z_low = z_grad_raw.astype(jnp.bfloat16)
    x_low = x_grad_raw.astype(jnp.bfloat16)
    dt_low = dt_grad_raw.astype(jnp.bfloat16)
    input_part = rows_times(z_low, low_z) + rows_times(x_low, low_x) + rows_times(dt_low, low_dt)
    input_total, bc_total, convbc_slot = lax.psum((input_part, bc_grad_part, convbc_part), "tensor")
    bc_low = bc_total.astype(jnp.bfloat16)
    normed_grad = input_total + rows_times(bc_low, low_bc)
    block_grad, gain_slot = norm_pull(normed_grad)
    input_grad = (cotangent + block_grad).astype(jnp.bfloat16)
    z_part = tokens_out(normed_low, z_low)
    x_part = tokens_out(normed_low, x_low)
    bc_part = tokens_out(normed_low, bc_low)
    dt_part = tokens_out(normed_low, dt_low)
    z_share, x_share, bc_share, dt_share, out_share = (
        lax.psum_scatter(z_part, "dp", scatter_dimension=0, tiled=True),
        lax.psum_scatter(x_part, "dp", scatter_dimension=0, tiled=True),
        lax.psum_scatter(bc_part, "dp", scatter_dimension=0, tiled=True),
        lax.psum_scatter(dt_part, "dp", scatter_dimension=0, tiled=True),
        lax.psum_scatter(out_part, "dp", scatter_dimension=0, tiled=True),
    )
    z_square = z_share * z_share + tiny_eps
    x_square = x_share * x_share + tiny_eps
    bc_square = bc_share * bc_share + tiny_eps
    dt_square = dt_share * dt_share + tiny_eps
    out_square = out_share * out_share + tiny_eps
    z_row_sum, x_row_sum, dt_row_sum, out_row_sum = lax.psum(
        (
            jnp.sum(z_square, axis=1),
            jnp.sum(x_square, axis=1),
            jnp.sum(dt_square, axis=1),
            jnp.sum(out_square, axis=1),
        ),
        "tensor",
    )
    bc_row_sum = jnp.sum(bc_square, axis=1)
    (
        z_col_sum,
        x_col_sum,
        bc_col_sum,
        dt_col_sum,
        out_col_sum,
        norm_total,
        gated_total,
        convx_total,
        convbc_total,
        head_total,
    ) = lax.psum(
        (
            jnp.sum(z_square, axis=0),
            jnp.sum(x_square, axis=0),
            jnp.sum(bc_square, axis=0),
            jnp.sum(dt_square, axis=0),
            jnp.sum(out_square, axis=0),
            gain_slot,
            gated_slot,
            convx_slot,
            convbc_slot,
            head_slot,
        ),
        "dp",
    )
    z_rows_new = mix_state(z_rows, z_row_sum / INNER)
    x_rows_new = mix_state(x_rows, x_row_sum / INNER)
    bc_rows_new = mix_state(bc_rows, bc_row_sum / (2 * STATE))
    dt_rows_new = mix_state(dt_rows, dt_row_sum / HEADS)
    out_rows_new = mix_state(out_rows, out_row_sum / INNER)
    z_cols_new = mix_state(z_cols, z_col_sum / D)
    x_cols_new = mix_state(x_cols, x_col_sum / D)
    bc_cols_new = mix_state(bc_cols, bc_col_sum / D)
    dt_cols_new = mix_state(dt_cols, dt_col_sum / D)
    out_cols_new = mix_state(out_cols, out_col_sum / D)
    norm_second = mix_state(norm_gain_sq, norm_total * norm_total + tiny_eps)
    gated_second = mix_state(gated_gain_sq, gated_total * gated_total + tiny_eps)
    convx_second = mix_state(conv_x_sq, convx_total * convx_total + tiny_eps)
    convbc_second = mix_state(conv_bc_sq, convbc_total * convbc_total + tiny_eps)
    head_second = mix_state(head_sq, head_total * head_total + tiny_eps)
    norm_unit = norm_total * lax.rsqrt(norm_second)
    gated_unit = gated_total * lax.rsqrt(gated_second)
    convx_unit = convx_total * lax.rsqrt(convx_second)
    convbc_unit = convbc_total * lax.rsqrt(convbc_second)
    head_unit = head_total * lax.rsqrt(head_second)
    z_unit = z_share * lax.rsqrt(z_rows_new[:, None] * z_cols_new[None, :])
    x_unit = x_share * lax.rsqrt(x_rows_new[:, None] * x_cols_new[None, :])
    bc_unit = bc_share * lax.rsqrt(bc_rows_new[:, None] * bc_cols_new[None, :])
    dt_unit = dt_share * lax.rsqrt(dt_rows_new[:, None] * dt_cols_new[None, :])
    out_unit = out_share * lax.rsqrt(out_rows_new[:, None] * out_cols_new[None, :])
    (
        z_total,
        x_total,
        bc_total_sq,
        dt_total,
        out_total,
        norm_sq_total,
        gated_sq_total,
        convx_sq_total,
        convbc_sq_total,
        head_sq_total,
    ) = lax.psum(
        (
            jnp.sum(z_unit * z_unit),
            jnp.sum(x_unit * x_unit),
            jnp.sum(bc_unit * bc_unit) / tensor_count,
            jnp.sum(dt_unit * dt_unit),
            jnp.sum(out_unit * out_unit),
            jnp.sum(norm_unit * norm_unit) / full_copies,
            jnp.sum(gated_unit * gated_unit) / data_count,
            jnp.sum(convx_unit * convx_unit) / data_count,
            jnp.sum(convbc_unit * convbc_unit) / full_copies,
            jnp.sum(head_unit * head_unit) / data_count,
        ),
        ("dp", "tensor"),
    )
    in_rate = D ** (-0.5)
    out_rate = INNER ** (-0.5)
    z_upd = -in_rate * normalized(z_unit, z_total, D * INNER)
    x_upd = -in_rate * normalized(x_unit, x_total, D * INNER)
    bc_upd = -in_rate * normalized(bc_unit, bc_total_sq, D * 2 * STATE)
    dt_upd = -in_rate * normalized(dt_unit, dt_total, D * HEADS)
    out_upd = -out_rate * normalized(out_unit, out_total, D * INNER)
    norm_upd = -vector_rate * normalized(norm_unit, norm_sq_total, D)
    gated_upd = -vector_rate * normalized(gated_unit, gated_sq_total, INNER)
    convx_upd = -vector_rate * normalized(convx_unit, convx_sq_total, KCONV * INNER)
    convbc_upd = -vector_rate * normalized(convbc_unit, convbc_sq_total, KCONV * 2 * STATE)
    head_upd = -vector_rate * normalized(head_unit, head_sq_total, 3 * HEADS)
    return (
        output[None],
        input_grad[None],
        norm_total,
        norm_upd,
        norm_second,
        z_share,
        z_upd,
        z_rows_new,
        z_cols_new,
        x_share,
        x_upd,
        x_rows_new,
        x_cols_new,
        bc_share,
        bc_upd,
        bc_rows_new,
        bc_cols_new,
        dt_share,
        dt_upd,
        dt_rows_new,
        dt_cols_new,
        convx_total,
        convx_upd,
        convx_second,
        convbc_total,
        convbc_upd,
        convbc_second,
        head_total,
        head_upd,
        head_second,
        gated_total,
        gated_upd,
        gated_second,
        out_share,
        out_upd,
        out_rows_new,
        out_cols_new,
    )


def solution(mesh):
    in_specs = (
        P("dp", None, None),
        P("dp", None, None),
        P("dp", None),
        P("dp"),
        P(),
        P("dp", "tensor"),
        P("dp", "tensor"),
        P("dp", None),
        P("dp", "tensor"),
        P(None, "tensor"),
        P(),
        P(None, "tensor"),
        P("tensor"),
        P("dp", "tensor"),
        P(),
        P("dp"),
        P("tensor"),
        P("dp"),
        P("tensor"),
        P("dp"),
        P(),
        P("dp"),
        P("tensor"),
        P(None, "tensor"),
        P(),
        P(None, "tensor"),
        P("tensor"),
        P("dp"),
        P("tensor"),
    )
    out_specs = (
        P("dp", None, None),
        P("dp", None, None),
        P(),
        P(),
        P(),
        P("dp", "tensor"),
        P("dp", "tensor"),
        P("dp"),
        P("tensor"),
        P("dp", "tensor"),
        P("dp", "tensor"),
        P("dp"),
        P("tensor"),
        P("dp", None),
        P("dp", None),
        P("dp"),
        P(),
        P("dp", "tensor"),
        P("dp", "tensor"),
        P("dp"),
        P("tensor"),
        P(None, "tensor"),
        P(None, "tensor"),
        P(None, "tensor"),
        P(),
        P(),
        P(),
        P(None, "tensor"),
        P(None, "tensor"),
        P(None, "tensor"),
        P("tensor"),
        P("tensor"),
        P("tensor"),
        P("dp", "tensor"),
        P("dp", "tensor"),
        P("dp"),
        P("tensor"),
    )
    return jax.shard_map(shards, mesh=mesh, in_specs=in_specs, out_specs=out_specs, check_vma=False)
```

profile of v0, /device:TPU:0, one launch (start us, length us, event | category | flops | bytes accessed | tf_op | source)
XLA Modules:
  0.0 1280.2 jit_solution(9074550535017207405)
XLA Ops:
  15.5 32.5 %all_gather.16 = bf16[2048,16]{0,1:T(8,128)(2,1)S(1)} all-gather(bf16[256,16]{0,1:T(8,128)(2,1)S(1)} %convert_element_type.127), channel_id=1, replica_groups=mesh['dp'=8,'tensor'=4] {'dp'}, dimensions={0}, use_global_device_ids=true | all-gather | bytes 73728 | tf_op jit(solution)/shard_map/all_gather | solution.py:164
  59.6 68.4 %all-gather.5.cloned.1.call-done = bf16[2048,1024]{1,0:T(8,128)(2,1)} async-done(((bf16[256,1024]{1,0:T(8,128)(2,1)}), bf16[2048,1024]{1,0:T(8,128)(2,1)}) %all-gather.5.cloned.1.call-update) | async-done | bytes 4194320 | tf_op jit(solution)/shard_map/all_gather | solution.py:162
  128.0 5.1 fusion.148
  148.3 38.9 %while.46 = (s32[]{:T(128)}, f32[16,64,128]{2,1,0:T(8,128)S(1)}, s32[]{:T(128)}, f32[2,16,64,256]{3,2,1,0:T(8,128)}, f32[2,16,64,128]{3,2,1,0:T(8,128)}, /*index...) while((s32[]{:T(128)}, f32[16,64,128]{2,1,0:T(8,128)S(1)}, ...), condition=%wide.region_4.5_spmd.clone, body=%wide.region_1.4_spmd.clone.sunk | while | flops 1718707200 | bytes 9435327 | solution.py:76
  150.5 7.1 fusion.246
  170.0 7.1 fusion.246
  192.0 5.3 reshape.651
  202.1 9.0 multiply_reduce_fusion.10
  211.1 64.9 %all-gather.11.cloned.1.call-done = bf16[2048,1024]{1,0:T(8,128)(2,1)} async-done(((bf16[256,1024]{1,0:T(8,128)(2,1)}), bf16[2048,1024]{1,0:T(8,128)(2,1)}) %all-gather.11.cloned.1.call-update) | async-done | bytes 4194320 | tf_op jit(solution)/shard_map/all_gather | solution.py:165
  276.0 7.2 fusion.120
  283.9 5.7 psum.203
  289.6 77.8 %all-reduce.36.cloned.1.call-done = f32[512,2048]{1,0:T(8,128)} async-done(((f32[512,2048]{1,0:T(8,128)}), f32[512,2048]{1,0:T(8,128)}) %all-reduce.36.cloned.1.call-update) | async-done | bytes 4194320 | tf_op jit(solution)/shard_map/psum | solution.py:183
  367.4 5.4 fusion.95
  374.1 8.4 multiply_reduce_fusion.5
  390.5 82.3 %while.47 = (s32[]{:T(128)}, f32[16]{0:T(128)}, f32[16,64,128]{2,1,0:T(8,128)}, f32[2,16,64,256]{3,2,1,0:T(8,128)}, f32[2,16,256]{2,1,0:T(8,128)}, /*index=5*/f3...) while((s32[]{:T(128)}, f32[16]{0:T(128)}, ...), condition=%wide.region_22.23_spmd.clone, body=%wide.region_9.22_spmd.clone.sunk | while | flops 3951219712 | bytes 44425100 | solution.py:76
  406.6 7.6 fusion.269
  422.7 5.8 fusion.273
  448.1 7.6 fusion.269
  464.1 5.9 fusion.273
  477.4 7.3 fusion.113
  490.1 5.0 reshape.652
  504.5 5.6 fusion.153
  511.9 5.6 fusion.152
  541.1 149.4 %reduce-scatter.14.cloned.1.call-done = f32[256,1024]{1,0:T(8,128)} async-done(((f32[2048,1024]{1,0:T(8,128)}), f32[256,1024]{1,0:T(8,128)}) %reduce-scatter.14.cloned.1.call-update) | async-done | bytes 1048592 | tf_op jit(solution)/shard_map/reduce_scatter | solution.py:220
  692.0 149.3 %reduce-scatter.8.cloned.1.call-done = f32[256,1024]{1,0:T(8,128)} async-done(((f32[2048,1024]{1,0:T(8,128)}), f32[256,1024]{1,0:T(8,128)}) %reduce-scatter.8.cloned.1.call-update) | async-done | bytes 1048592 | tf_op jit(solution)/shard_map/reduce_scatter | solution.py:217
  842.8 149.3 %reduce-scatter.6.cloned.1.call-done = f32[256,1024]{1,0:T(8,128)} async-done(((f32[2048,1024]{1,0:T(8,128)}), f32[256,1024]{1,0:T(8,128)}) %reduce-scatter.6.cloned.1.call-update) | async-done | bytes 1048592 | tf_op jit(solution)/shard_map/reduce_scatter | solution.py:216
  993.6 25.1 %all-reduce.39 = (bf16[512,256]{1,0:T(8,128)(2,1)S(1)}, f32[4,256]{1,0:T(4,128)}, f32[256]{0:T(256)S(1)}, f32[256]{0:T(256)S(1)}, f32[256]{0:T(256)S(1)}, /*index=5*/f32[256]{0:T(256)S(1)}) all-reduce(f32[512,256]{1,0:T(8,128)S(1)} %copy-done.27, f32[4,256]{1,0:T(4,128)S(1)} %pad_add_fusion.1, ...), channel_id=1, replica_groups=mesh['dp'=8,'tensor'=4] {'tensor'}, use_global_device_ids=true, to_apply=%region_24.25 | all-reduce | flops 133120 | bytes 802816 | tf_op jit(solution)/shard_map/psum | solution.py:206
  1022.4 62.2 %all-reduce.38.cloned.1.call-done = f32[512,2048]{1,0:T(8,128)} async-done(((f32[512,2048]{1,0:T(8,128)}), f32[512,2048]{1,0:T(8,128)}) %all-reduce.38.cloned.1.call-update) | async-done | bytes 4194320 | tf_op jit(solution)/shard_map/psum | solution.py:206
  1084.6 5.8 fusion.89
  1090.4 67.4 %reduce-scatter.10.cloned.1.call-done = f32[256,256]{1,0:T(8,128)} async-done(((f32[2048,256]{1,0:T(8,128)}), f32[256,256]{1,0:T(8,128)}) %reduce-scatter.10.cloned.1.call-update) | async-done | bytes 262160 | tf_op jit(solution)/shard_map/reduce_scatter | solution.py:218
  1158.9 35.9 %all-reduce.30 = (f32[2048]{0:T(1024)S(1)}, f32[1024]{0:T(1024)S(1)}, f32[1024]{0:T(1024)S(1)}, f32[256]{0:T(256)S(1)}, f32[16]{0:T(128)S(1)}, /*index=5*/f32[4,...) all-reduce(f32[2048]{0:T(1024)S(1)} %get-tuple-element.764, ...), channel_id=1, replica_groups=mesh['dp'=8,'tensor'=4] {'dp'}, use_global_device_ids=true, to_apply=%region_27.28 | all-reduce | flops 11584 | bytes 92672 | tf_op jit(solution)/shard_map/psum | solution.py:248
  1221.0 37.3 %all-reduce.29 = (f32[]{:T(128)}, f32[]{:T(128)}, f32[]{:T(128)}, f32[]{:T(128)}, f32[]{:T(128)}, /*index=5*/f32[]{:T(128)}, f32[]{:T(128)}, f32[]{:T(128)}, f32[]{:T(128)}, f32[]{:T(128)}) all-reduce(f32[]{:T(128)S(6)} %div.98, f32[]{:T(128)} %multiply_reduce_fusion.13, ...), channel_id=1, replica_groups=mesh['dp'=8,'tensor'=4] {'dp','tensor'}, use_global_device_ids=true, to_apply=%region_29.30 | all-reduce | flops 10 | bytes 80 | tf_op jit(solution)/shard_map/psum | solution.py:299
  (592 shorter events, 210.8 us)
Async XLA Ops:
  7.2 46.6 %all-gather.7.cloned.1.call-start = ((), (), s32[]{:S(2)}) async-start(), calls=%async_computation.6 | async-start | bytes 1179648 | tf_op jit(solution)/shard_map/all_gather | solution.py:163
  9.0 119.0 %all-gather.5.cloned.1.call-start = ((), (), s32[]{:S(2)}) async-start(), calls=%async_computation.5 | async-start | bytes 4718592 | tf_op jit(solution)/shard_map/all_gather | solution.py:162
  11.2 190.9 %all-gather.9.cloned.1.call-start = ((), (), s32[]{:S(2)}) async-start(), calls=%async_computation.7 | async-start | bytes 4718592 | tf_op jit(solution)/shard_map/all_gather | solution.py:161
  12.2 263.8 %all-gather.11.cloned.1.call-start = ((), (), s32[]{:S(2)}) async-start(), calls=%async_computation.8 | async-start | bytes 4718592 | tf_op jit(solution)/shard_map/all_gather | solution.py:165
  14.4 353.0 %all-reduce.36.cloned.1.call-start = ((), (), s32[]{:S(2)}) async-start(), calls=%async_computation.9 | async-start | bytes 8388608 | tf_op jit(solution)/shard_map/psum | solution.py:183
  15.4 117.7 %copy-start.62 = (f32[512]{0:T(512)}, f32[512]{0:T(512)S(1)}, u32[]{:S(2)}) copy-start(f32[512]{0:T(512)S(1)} %pad_convert_fusion) | copy-start | bytes 6148
  15.4 117.7 %copy-start.68 = (f32[1,1024]{1,0:T(1,128)}, f32[1,1024]{1,0:T(1,128)S(1)}, u32[]{:S(2)}) copy-start(f32[1,1024]{1,0:T(1,128)S(1)} %get-tuple-element.924) | copy-start | bytes 12292
  15.5 117.7 %copy-start.70 = (f32[1,1024]{1,0:T(1,128)}, f32[1,1024]{1,0:T(1,128)S(1)}, u32[]{:S(2)}) copy-start(f32[1,1024]{1,0:T(1,128)S(1)} %get-tuple-element.926) | copy-start | bytes 12292
  15.5 117.7 %copy-start.72 = (f32[1,1024]{1,0:T(1,128)}, f32[1,1024]{1,0:T(1,128)S(1)}, u32[]{:S(2)}) copy-start(f32[1,1024]{1,0:T(1,128)S(1)} %get-tuple-element.925) | copy-start | bytes 12292
  15.5 117.7 %copy-start.74 = (f32[1,1024]{1,0:T(1,128)}, f32[1,1024]{1,0:T(1,128)S(1)}, u32[]{:S(2)}) copy-start(f32[1,1024]{1,0:T(1,128)S(1)} %get-tuple-element.927) | copy-start | bytes 12292
  53.1 319.7 %copy-start.87 = (f32[1024]{0:T(1024)}, f32[1024]{0:T(1024)S(1)}, u32[]{:S(2)}) copy-start(f32[1024]{0:T(1024)S(1)} %mul.1361) | copy-start | bytes 12292
  53.2 80.0 %copy-start.64 = (f32[512]{0:T(512)}, f32[512]{0:T(512)S(1)}, u32[]{:S(2)}) copy-start(f32[512]{0:T(512)S(1)} %get-tuple-element.939) | copy-start | bytes 6148
  53.2 80.0 %copy-start.66 = (f32[512]{0:T(512)}, f32[512]{0:T(512)S(1)}, u32[]{:S(2)}) copy-start(f32[512]{0:T(512)S(1)} %get-tuple-element.940) | copy-start | bytes 6148
  202.1 73.9 %copy-start.118 = (f32[1024]{0:T(1024)S(1)}, f32[1024]{0:T(1024)}, u32[]{:S(2)}) copy-start(f32[1024]{0:T(1024)} %param.45) | copy-start | bytes 12292
  283.2 256.6 %reduce-scatter.12.cloned.1.call-start = ((), (), s32[]{:S(2)}) async-start(), calls=%async_computation.14 | async-start | bytes 147456 | tf_op jit(solution)/shard_map/reduce_scatter | solution.py:219
  289.6 83.2 %copy-start.83 = (f32[512]{0:T(512)}, f32[512]{0:T(512)S(1)}, u32[]{:S(2)}) copy-start(f32[512]{0:T(512)S(1)} %add_rsqrt_fusion) | copy-start | bytes 6148
  477.3 213.2 %reduce-scatter.14.cloned.1.call-start = ((), (), s32[]{:S(2)}) async-start(), calls=%async_computation.15 | async-start | bytes 9437184 | tf_op jit(solution)/shard_map/reduce_scatter | solution.py:220
  484.7 356.6 %reduce-scatter.8.cloned.1.call-start = ((), (), s32[]{:S(2)}) async-start(), calls=%async_computation.12 | async-start | bytes 9437184 | tf_op jit(solution)/shard_map/reduce_scatter | solution.py:217
  510.1 482.0 %reduce-scatter.6.cloned.1.call-start = ((), (), s32[]{:S(2)}) async-start(), calls=%async_computation.11 | async-start | bytes 9437184 | tf_op jit(solution)/shard_map/reduce_scatter | solution.py:216
  517.6 567.0 %all-reduce.38.cloned.1.call-start = ((), (), s32[]{:S(2)}) async-start(), calls=%async_computation.10 | async-start | bytes 8388608 | tf_op jit(solution)/shard_map/psum | solution.py:206
  531.4 626.4 %reduce-scatter.10.cloned.1.call-start = ((), (), s32[]{:S(2)}) async-start(), calls=%async_computation.13 | async-start | bytes 2359296 | tf_op jit(solution)/shard_map/reduce_scatter | solution.py:218
  535.2 458.3 %copy-start.27 = (f32[512,256]{1,0:T(8,128)S(1)}, f32[512,256]{1,0:T(8,128)}, u32[]{:S(2)}) copy-start(f32[512,256]{1,0:T(8,128)} %get-tuple-element.919) | copy-start | bytes 1572868
  1022.3 246.0 %copy-start.99 = (f32[256]{0:T(256)}, f32[256]{0:T(256)S(1)}, u32[]{:S(2)}) copy-start(f32[256]{0:T(256)S(1)} %multiply_add_fusion.14) | copy-start | bytes 3076
  1022.3 247.2 %copy-start.112 = (f32[256]{0:T(256)}, f32[256]{0:T(256)S(1)}, u32[]{:S(2)}) copy-start(f32[256]{0:T(256)S(1)} %multiply_add_fusion.15) | copy-start | bytes 3076
  1022.3 248.7 %copy-start.100 = (f32[256]{0:T(256)}, f32[256]{0:T(256)S(1)}, u32[]{:S(2)}) copy-start(f32[256]{0:T(256)S(1)} %multiply_add_fusion.18) | copy-start | bytes 3076
  1022.4 249.9 %copy-start.101 = (f32[256]{0:T(256)}, f32[256]{0:T(256)S(1)}, u32[]{:S(2)}) copy-start(f32[256]{0:T(256)S(1)} %multiply_add_fusion.19) | copy-start | bytes 3076
  1022.4 172.5 %copy-start.113 = (f32[2048]{0:T(1024)S(1)}, f32[2048]{0:T(1024)}, u32[]{:S(2)}) copy-start(f32[2048]{0:T(1024)} %param.47) | copy-start | bytes 24580
  1022.4 175.7 %copy-start.89 = (f32[4,1024]{1,0:T(4,128)S(1)}, f32[4,1024]{1,0:T(4,128)}, u32[]{:S(2)}) copy-start(f32[4,1024]{1,0:T(4,128)} %param.56) | copy-start | bytes 49156
  1022.4 187.5 %copy-start.16 = (f32[256,1024]{1,0:T(8,128)S(1)}, f32[256,1024]{1,0:T(8,128)}, u32[]{:S(2)}) copy-start(f32[256,1024]{1,0:T(8,128)} %reduce-scatter.14.cloned.1.call-done) | copy-start | bytes 3145732
  1022.4 188.6 %copy-start.51 = (f32[256,16]{0,1:T(8,128)S(1)}, f32[256,16]{0,1:T(8,128)}, u32[]{:S(2)}) copy-start(f32[256,16]{0,1:T(8,128)} %reduce-scatter.12.cloned.1.call-done) | copy-start | bytes 49156
  1194.8 72.2 %copy-start.58 = (f32[4,1024]{1,0:T(4,128)}, f32[4,1024]{1,0:T(4,128)S(1)}, u32[]{:S(2)}) copy-start(f32[4,1024]{1,0:T(4,128)S(1)} %get-tuple-element.847) | copy-start | bytes 49156
  1194.8 72.8 %copy-start.79 = (f32[2048]{0:T(1024)}, f32[2048]{0:T(1024)S(1)}, u32[]{:S(2)}) copy-start(f32[2048]{0:T(1024)S(1)} %get-tuple-element.842) | copy-start | bytes 24580
  (143 other events, 2044.8 us)
Sparse Core Ops, SparseCore 0:
  10.7 43.0 all-gather.6
  56.6 71.3 all-gather.4
  130.7 71.3 all-gather.8
  204.6 71.3 all-gather.10
  283.3 84.0 all-reduce.35
  477.4 62.3 reduce-scatter.11
  544.0 146.4 reduce-scatter.13
  694.7 146.5 reduce-scatter.7
  845.5 146.5 reduce-scatter.5
  994.3 90.2 all-reduce.37
  1089.3 68.4 reduce-scatter.9
where the time goes:
time: 1290 us; the launch traced here: 1280 us
  waiting for transfers between devices  799 us (62%)
  matrix products  139 us (11%)
  blocking collectives  136 us (11%)
  other arithmetic  97 us (8%)
  local copies, waits for them, and re-layouts  75 us (6%)
  between operations  26.7 us (2%)
    reduce_scatter x1, waiting for transfers between devices, shards(): lax.psum_scatter(out_part, 'dp', scatter_dimension=0, tiled=True)  149 us
    reduce_scatter x1, waiting for transfers between devices, shards(): lax.psum_scatter(x_part, 'dp', scatter_dimension=0, tiled=True)  149 us
    reduce_scatter x1, waiting for transfers between devices, shards(): lax.psum_scatter(z_part, 'dp', scatter_dimension=0, tiled=True)  149 us
    psum x1, waiting for transfers between devices, shards(): lax.psum((rows_times(scaled_low, low_out), squares), 'tensor')  77.8 us
    all_gather x1, waiting for transfers between devices, shards(): lax.all_gather(x_weight.astype(jnp.bfloat16), 'dp', axis=0, tiled=True)  68.4 us
    reduce_scatter x1, waiting for transfers between devices, shards(): lax.psum_scatter(bc_part, 'dp', scatter_dimension=0, tiled=True)  67.4 us
    all_gather x1, waiting for transfers between devices, shards(): lax.all_gather(out_weight.astype(jnp.bfloat16), 'dp', axis=0, tiled=True)  64.9 us
    psum x1, waiting for transfers between devices, shards(): lax.psum((input_part, bc_grad_part, convbc_part), 'tensor')  62.2 us
  transfers between devices with their start and end apart: 11, of which 11 were waited for; matrix products, arithmetic and copies ran while one was open for 12% of the time, Pallas kernels for 0%

commit v1 on v0

--- a/solution.py
+++ b/solution.py
@@ -118,6 +118,128 @@
 
 def normalized(unit, square_total, entries):
     return unit * lax.rsqrt(square_total / entries + unit_eps)
+
+
+def swap(value, axis, bit):
+    size = lax.axis_size(axis)
+    return lax.ppermute(value, axis, [(place, place ^ bit) for place in range(size)])
+
+
+def add_over(value, axis, bits):
+    for bit in bits:
+        value = value + swap(value, axis, bit)
+    return value
+
+
+PAIR = 2
+
+
+def dp_bits():
+    count = lax.axis_size("dp")
+    rest = [1 << place for place in reversed(range(count.bit_length() - 1)) if 1 << place != PAIR]
+    return [PAIR] + rest
+
+
+def block_masks():
+    bits = dp_bits()
+    return [
+        sum(bit for place, bit in enumerate(bits) if (number >> place) & 1)
+        for number in range(lax.axis_size("dp"))
+    ]
+
+
+def place_of(offset):
+    return sum(
+        ((offset // bit) % 2) << place for place, bit in enumerate(dp_bits())
+    )
+
+
+def to_relative(values, mine):
+    blocks = lax.axis_size("dp")
+    width = values.shape[-1] // blocks
+    return jnp.concatenate(
+        [
+            lax.dynamic_slice_in_dim(values, (mine ^ mask) * width, width, values.ndim - 1)
+            for mask in block_masks()
+        ],
+        axis=-1,
+    )
+
+
+def from_relative(values, mine):
+    blocks = lax.axis_size("dp")
+    width = values.shape[-1] // blocks
+    return jnp.concatenate(
+        [
+            lax.dynamic_slice_in_dim(values, place_of(mine ^ block) * width, width, values.ndim - 1)
+            for block in range(blocks)
+        ],
+        axis=-1,
+    )
+
+
+def halves(values, half, axis):
+    width = values.shape[axis] // 2
+    mine = lax.dynamic_slice_in_dim(values, half * width, width, axis)
+    other = lax.dynamic_slice_in_dim(values, (1 - half) * width, width, axis)
+    return mine, other
+
+
+def join_halves(mine, other, half, axis):
+    return jnp.where(
+        half == 0,
+        jnp.concatenate([mine, other], axis=axis),
+        jnp.concatenate([other, mine], axis=axis),
+    )
+
+
+def gather_rows(weight, half):
+    mine, other = halves(weight.astype(jnp.bfloat16), half, 1)
+    held = jnp.concatenate([mine, swap(other, "dp", PAIR)], axis=0)
+    for bit in dp_bits()[1:]:
+        held = jnp.concatenate([held, swap(held, "dp", bit)], axis=0)
+    return held
+
+
+def reduce_rows(terms, half):
+    held = terms
+    for bit in reversed(dp_bits()[1:]):
+        rows = held.shape[0] // 2
+        held = held[:rows] + swap(held[rows:].astype(jnp.bfloat16), "dp", bit).astype(jnp.float32)
+    rows = held.shape[0] // 2
+    other = swap(held[rows:].astype(jnp.bfloat16), "dp", PAIR).astype(jnp.float32)
+    return join_halves(held[:rows], other, half, 1)
+
+
+def reduce_small(terms, axis):
+    held = terms
+    for bit in reversed(dp_bits()):
+        rows = held.shape[axis] // 2
+        low = lax.slice_in_dim(held, 0, rows, axis=axis)
+        high = lax.slice_in_dim(held, rows, 2 * rows, axis=axis)
+        held = low + swap(high, "dp", bit)
+    return held
+
+
+def share_tokens(terms, tensor_at, kind):
+    held = terms
+    for bit in (1, 2):
+        mine, other = halves(held, (tensor_at // bit) % 2, 1)
+        held = mine + swap(other.astype(kind), "tensor", bit).astype(jnp.float32)
+    return held[0], swap(held[1].astype(kind), "dp", PAIR).astype(jnp.float32)
+
+
+def flip_pairs(values):
+    blocks = lax.axis_size("dp")
+    width = values.shape[-1] // blocks
+    pieces = [values[..., (place ^ 1) * width : ((place ^ 1) + 1) * width] for place in range(blocks)]
+    return jnp.concatenate(pieces, axis=-1)
+
+
+def whole_tokens(values, tensor_at):
+    for bit in (2, 1):
+        values = join_halves(values, swap(values, "tensor", bit), (tensor_at // bit) % 2, 0)
+    return values
 
 
 def shards(
@@ -152,43 +274,109 @@
     out_cols,
 ):
     data_count = lax.axis_size("dp")
-    tensor_count = lax.axis_size("tensor")
-    full_copies = data_count * tensor_count
-    block_in = block_input[0].astype(jnp.float32)
-    segment = seg_ids[0]
-    live_flag = slot_live[0].astype(jnp.float32)
-    low_z, low_x, low_bc, low_dt, low_out = (
-        lax.all_gather(z_weight.astype(jnp.bfloat16), "dp", axis=0, tiled=True),
-        lax.all_gather(x_weight.astype(jnp.bfloat16), "dp", axis=0, tiled=True),
-        lax.all_gather(bc_weight.astype(jnp.bfloat16), "dp", axis=0, tiled=True),
-        lax.all_gather(dt_weight.astype(jnp.bfloat16), "dp", axis=0, tiled=True),
-        lax.all_gather(out_weight.astype(jnp.bfloat16), "dp", axis=0, tiled=True),
-    )
-    normed, norm_pull = jax.vjp(norm_input, block_in, norm_gain)
-    normed_low = normed.astype(jnp.bfloat16)
-    gate_z = jnp.dot(normed_low, low_z, preferred_element_type=jnp.float32)
-    x_raw = jnp.dot(normed_low, low_x, preferred_element_type=jnp.float32)
-    bc_raw = jnp.dot(normed_low, low_bc, preferred_element_type=jnp.float32)
-    dt_raw = jnp.dot(normed_low, low_dt, preferred_element_type=jnp.float32)
+    data_at = lax.axis_index("dp")
+    tensor_at = lax.axis_index("tensor")
+    half = (data_at // PAIR) % 2
+    core = tensor_at % 2
+    row_count = z_weight.shape[0]
+    quarter = row_count // 4
+    slot_tokens = block_input.shape[1]
+    f32, bf16 = jnp.float32, jnp.bfloat16
+
+    def pair_tokens(values):
+        mine, _ = halves(values, core, 0)
+        far = swap(mine, "dp", PAIR)
+        near = swap(far, "tensor", 1)
+        return jnp.stack([values, join_halves(far, near, core, 0)])
+
+    whole_numbers = jnp.concatenate(
+        [seg_ids[0], jnp.broadcast_to(slot_live, (128,))]
+    ).reshape(-1, 128)
+    far_numbers = swap(whole_numbers, "dp", PAIR)
+    segments = jnp.stack([seg_ids[0], far_numbers[:-1].reshape(-1)])
+    live = jnp.stack([slot_live[0], far_numbers[-1, 0]]).astype(f32)
+
+    both_in = pair_tokens(block_input[0])
+    dt_rows_low = dt_weight.astype(bf16).T
+    bc_mine = lax.dynamic_slice_in_dim(bc_weight.astype(bf16), tensor_at * quarter, quarter, 0)
+    small = jnp.concatenate([bc_mine.reshape(-1, 128), dt_rows_low.reshape(-1, 128)], axis=0)[None]
+    for bit in dp_bits():
+        small = jnp.concatenate([small, swap(small, "dp", bit)], axis=0)
+    bc_piece_rows = quarter * bc_weight.shape[1] // 128
+    low_dt = (
+        small[:, bc_piece_rows:].reshape(data_count, dt_weight.shape[1], row_count).transpose(1, 0, 2)
+    ).reshape(dt_weight.shape[1], -1)
+    low_dt, _ = halves(low_dt, half, 0)
+    bc_held = small[:, :bc_piece_rows].reshape(data_count, quarter, -1)
+    bc_held = join_halves(bc_held, swap(bc_held, "tensor", 1), core, 1)
+    bc_held = join_halves(bc_held, swap(bc_held, "tensor", 2), tensor_at // 2, 1)
+    low_bc = bc_held.reshape(data_count * row_count, -1)
+
+    low_x = gather_rows(x_weight, half)
+    low_z = gather_rows(z_weight, half)
+    low_out = gather_rows(out_weight, half)
+    both_grad = pair_tokens(out_grad[0])
+
+    taps_x, _ = halves(conv_x, half, 1)
+    per_head, _ = halves(head_params, half, 1)
+    gain_inner, _ = halves(gated_gain, half, 0)
+
+    gain_rel = to_relative(norm_gain, data_at)
+    in_rel = to_relative(both_in, data_at).astype(f32)
+    mean_square = jnp.mean(in_rel * in_rel, axis=-1, keepdims=True)
+    normed_low = (in_rel * lax.rsqrt(mean_square + norm_eps) * gain_rel).astype(bf16)
+    normed_flat = normed_low.reshape(-1, normed_low.shape[-1])
+    tokens = normed_flat.shape[0]
+
+    def per_slot(values):
+        return values.reshape(2, slot_tokens, -1)
+
+    x_raw = per_slot(jnp.dot(normed_flat, low_x, preferred_element_type=f32))
+    bc_raw = per_slot(jnp.dot(normed_flat, low_bc, preferred_element_type=f32))
+    dt_raw = per_slot(rows_times(normed_flat, low_dt))
+    gate_z = per_slot(jnp.dot(normed_flat, low_z, preferred_element_type=f32))
 
     def local_mixer(gate_in, x_in_raw, bc_in_raw, dt_in_raw, taps_x, taps_bc, per_head, gain_inner):
-        return mixer(
-            gate_in, x_in_raw, bc_in_raw, dt_in_raw, taps_x, taps_bc, per_head, gain_inner, segment
+        return jax.vmap(mixer, in_axes=(0, 0, 0, 0, None, None, None, None, 0))(
+            gate_in, x_in_raw, bc_in_raw, dt_in_raw, taps_x, taps_bc, per_head, gain_inner, segments
         )
 
     (scaled, squares), mixer_pull = jax.vjp(
-        local_mixer, gate_z, x_raw, bc_raw, dt_raw, conv_x, conv_bc, head_params, gated_gain
-    )
-    scaled_low = scaled.astype(jnp.bfloat16)
-    projected, total_squares = lax.psum((rows_times(scaled_low, low_out), squares), "tensor")
+        local_mixer, gate_z, x_raw, bc_raw, dt_raw, taps_x, conv_bc, per_head, gain_inner
+    )
+    scaled_low = scaled.astype(bf16).reshape(tokens, -1)
+
+    def all_heads(values):
+        values = add_over(values, "tensor", (1, 2))
+        far = swap(values[1], "dp", PAIR)
+        mine = values[0] + far
+        return jnp.stack([mine, swap(mine, "dp", PAIR)])
+
+    def all_heads_once(values):
+        values = add_over(values, "tensor", (1, 2))
+        return values + swap(values, "dp", PAIR)[::-1]
+
+    total_squares = all_heads_once(squares)
+    projected = per_slot(rows_times(scaled_low, low_out))
     inv_rms = lax.rsqrt(total_squares / INNER + norm_eps)
-    output = (block_in + inv_rms[:, None] * projected).astype(jnp.bfloat16)
-    cotangent = out_grad[0].astype(jnp.float32) * live_flag
-    proj_grad = (cotangent * inv_rms[:, None]).astype(jnp.bfloat16)
-    rms_grad = jnp.sum(cotangent * projected, axis=1)
+    cot_rel = to_relative(both_grad, data_at).astype(f32) * live[:, None, None]
+    proj_grad = (cot_rel * inv_rms[:, :, None]).astype(bf16).reshape(tokens, -1)
+    rms_grad = all_heads_once(jnp.sum(cot_rel * projected, axis=-1))
     squares_grad = rms_grad * -0.5 * inv_rms * inv_rms * inv_rms / INNER
+    scaled_grad = per_slot(jnp.dot(proj_grad, low_out, preferred_element_type=f32))
     out_part = tokens_out(proj_grad, scaled_low)
-    scaled_grad = jnp.dot(proj_grad, low_out, preferred_element_type=jnp.float32)
+    out_share = reduce_rows(out_part, half)
+
+    share = slot_tokens // 4
+    share_at = (core * 2 + tensor_at // 2) * share
+    own, far = share_tokens(projected, tensor_at, bf16)
+    projected_mine = own + flip_pairs(far)
+    inv_mine = lax.dynamic_slice_in_dim(inv_rms[0], share_at, share, 0)
+    in_mine = lax.dynamic_slice_in_dim(in_rel[0], share_at, share, 0)
+    cot_mine = lax.dynamic_slice_in_dim(cot_rel[0], share_at, share, 0)
+    output_mine = (in_mine + inv_mine[:, None] * projected_mine).astype(bf16)
+    output = whole_tokens(from_relative(output_mine, data_at), tensor_at)
+
     (
         z_grad_raw,
         x_grad_raw,
@@ -199,66 +387,99 @@
         head_slot,
         gated_slot,
     ) = mixer_pull((scaled_grad, squares_grad))
-    z_low = z_grad_raw.astype(jnp.bfloat16)
-    x_low = x_grad_raw.astype(jnp.bfloat16)
-    dt_low = dt_grad_raw.astype(jnp.bfloat16)
-    input_part = rows_times(z_low, low_z) + rows_times(x_low, low_x) + rows_times(dt_low, low_dt)
-    input_total, bc_total, convbc_slot = lax.psum((input_part, bc_grad_part, convbc_part), "tensor")
-    bc_low = bc_total.astype(jnp.bfloat16)
-    normed_grad = input_total + rows_times(bc_low, low_bc)
+    z_low = z_grad_raw.astype(bf16).reshape(tokens, -1)
+    x_low = x_grad_raw.astype(bf16).reshape(tokens, -1)
+    dt_low = dt_grad_raw.astype(bf16).reshape(tokens, -1)
+    z_share = reduce_rows(tokens_out(normed_flat, z_low), half)
+    x_share = reduce_rows(tokens_out(normed_flat, x_low), half)
+    input_part = per_slot(
+        rows_times(z_low, low_z)
+        + rows_times(x_low, low_x)
+        + jnp.dot(dt_low, low_dt, preferred_element_type=f32)
+    )
+    bc_own, bc_far = share_tokens(bc_grad_part, tensor_at, f32)
+    bc_low_mine = (bc_own + bc_far).astype(bf16)
+    own, far = share_tokens(input_part, tensor_at, bf16)
+    normed_grad = own + flip_pairs(far) + rows_times(bc_low_mine, low_bc)
+
+    _, norm_pull = jax.vjp(norm_input, in_mine, gain_rel)
     block_grad, gain_slot = norm_pull(normed_grad)
-    input_grad = (cotangent + block_grad).astype(jnp.bfloat16)
-    z_part = tokens_out(normed_low, z_low)
-    x_part = tokens_out(normed_low, x_low)
-    bc_part = tokens_out(normed_low, bc_low)
-    dt_part = tokens_out(normed_low, dt_low)
-    z_share, x_share, bc_share, dt_share, out_share = (
-        lax.psum_scatter(z_part, "dp", scatter_dimension=0, tiled=True),
-        lax.psum_scatter(x_part, "dp", scatter_dimension=0, tiled=True),
-        lax.psum_scatter(bc_part, "dp", scatter_dimension=0, tiled=True),
-        lax.psum_scatter(dt_part, "dp", scatter_dimension=0, tiled=True),
-        lax.psum_scatter(out_part, "dp", scatter_dimension=0, tiled=True),
-    )
+    input_grad = whole_tokens(
+        from_relative((cot_mine + block_grad).astype(bf16), data_at), tensor_at
+    )
+
+    bc_low = whole_tokens(bc_low_mine, tensor_at)
+    bc_rows_part = tokens_out(normed_low[0], bc_low).reshape(data_count, row_count, -1)
+    bc_rows_part = lax.dynamic_slice_in_dim(bc_rows_part, tensor_at * quarter, quarter, 1)
+    dt_rows_part = tokens_out(dt_low, normed_flat).reshape(-1, data_count, row_count)
+    small_part = jnp.concatenate(
+        [
+            bc_rows_part.reshape(data_count, -1, 128),
+            dt_rows_part.transpose(1, 0, 2).reshape(data_count, -1, 128),
+        ],
+        axis=1,
+    )
+    held = small_part
+    for bit in reversed(dp_bits()[1:]):
+        count = held.shape[0] // 2
+        held = held[:count] + swap(held[count:], "dp", bit)
+    far = swap(held[1], "dp", PAIR)
+    bc_share = (held[0, :bc_piece_rows] + far[:bc_piece_rows]).reshape(quarter, -1)
+    dt_mine = held[0, bc_piece_rows:].reshape(-1, row_count)
+    dt_other = far[bc_piece_rows:].reshape(-1, row_count)
+    dt_share = join_halves(dt_mine, dt_other, half, 0).T
+    bc_share = join_halves(bc_share, swap(bc_share, "tensor", 1), core, 0)
+    bc_share = join_halves(bc_share, swap(bc_share, "tensor", 2), tensor_at // 2, 0)
+
     z_square = z_share * z_share + tiny_eps
     x_square = x_share * x_share + tiny_eps
     bc_square = bc_share * bc_share + tiny_eps
     dt_square = dt_share * dt_share + tiny_eps
     out_square = out_share * out_share + tiny_eps
-    z_row_sum, x_row_sum, dt_row_sum, out_row_sum = lax.psum(
-        (
+    row_sums = jnp.stack(
+        [
             jnp.sum(z_square, axis=1),
             jnp.sum(x_square, axis=1),
             jnp.sum(dt_square, axis=1),
             jnp.sum(out_square, axis=1),
-        ),
-        "tensor",
-    )
+        ]
+    )
+    z_row_sum, x_row_sum, dt_row_sum, out_row_sum = add_over(row_sums, "tensor", (1, 2))
     bc_row_sum = jnp.sum(bc_square, axis=1)
-    (
-        z_col_sum,
-        x_col_sum,
-        bc_col_sum,
-        dt_col_sum,
-        out_col_sum,
-        norm_total,
-        gated_total,
-        convx_total,
-        convbc_total,
-        head_total,
-    ) = lax.psum(
-        (
+
+    def in_half(values):
+        return join_halves(values, jnp.zeros_like(values), half, values.ndim - 1)
+
+    def packed_sum(pieces, axis_bits):
+        sizes = [piece.size for piece in pieces]
+        flat = jnp.concatenate([piece.reshape(-1) for piece in pieces])
+        fill = -flat.size % 128
+        flat = jnp.pad(flat, (0, fill)).reshape(-1, 128)
+        for axis, bits in axis_bits:
+            flat = add_over(flat, axis, bits)
+        flat = flat.reshape(-1)
+        result, at = [], 0
+        for piece, size in zip(pieces, sizes):
+            result.append(flat[at : at + size].reshape(piece.shape))
+            at += size
+        return result
+
+    norm_total, convbc_total = packed_sum(
+        [from_relative(gain_slot, data_at), convbc_part],
+        [("tensor", (1, 2)), ("dp", dp_bits())],
+    )
+    gated_total, convx_total, head_total = packed_sum(
+        [in_half(gated_slot), in_half(convx_slot), in_half(head_slot)], [("dp", dp_bits())]
+    )
+    z_col_sum, x_col_sum, bc_col_sum, dt_col_sum, out_col_sum = packed_sum(
+        [
             jnp.sum(z_square, axis=0),
             jnp.sum(x_square, axis=0),
             jnp.sum(bc_square, axis=0),
             jnp.sum(dt_square, axis=0),
             jnp.sum(out_square, axis=0),
-            gain_slot,
-            gated_slot,
-            convx_slot,
-            convbc_slot,
-            head_slot,
-        ),
-        "dp",
+        ],
+        [("dp", dp_bits())],
     )
     z_rows_new = mix_state(z_rows, z_row_sum / INNER)
     x_rows_new = mix_state(x_rows, x_row_sum / INNER)
@@ -285,32 +506,33 @@
     bc_unit = bc_share * lax.rsqrt(bc_rows_new[:, None] * bc_cols_new[None, :])
     dt_unit = dt_share * lax.rsqrt(dt_rows_new[:, None] * dt_cols_new[None, :])
     out_unit = out_share * lax.rsqrt(out_rows_new[:, None] * out_cols_new[None, :])
+    tensor_count = lax.axis_size("tensor")
+    unit_sums = jnp.stack(
+        [
+            jnp.sum(z_unit * z_unit),
+            jnp.sum(x_unit * x_unit),
+            jnp.sum(bc_unit * bc_unit) / tensor_count,
+            jnp.sum(dt_unit * dt_unit),
+            jnp.sum(out_unit * out_unit),
+            jnp.sum(gated_unit * gated_unit) / data_count,
+            jnp.sum(convx_unit * convx_unit) / data_count,
+            jnp.sum(head_unit * head_unit) / data_count,
+        ]
+    )
+    unit_sums = jnp.broadcast_to(unit_sums[:, None], (8, 128))
+    unit_sums = add_over(add_over(unit_sums, "tensor", (1, 2)), "dp", dp_bits())
     (
         z_total,
         x_total,
         bc_total_sq,
         dt_total,
         out_total,
-        norm_sq_total,
         gated_sq_total,
         convx_sq_total,
-        convbc_sq_total,
         head_sq_total,
-    ) = lax.psum(
-        (
-            jnp.sum(z_unit * z_unit),
-            jnp.sum(x_unit * x_unit),
-            jnp.sum(bc_unit * bc_unit) / tensor_count,
-            jnp.sum(dt_unit * dt_unit),
-            jnp.sum(out_unit * out_unit),
-            jnp.sum(norm_unit * norm_unit) / full_copies,
-            jnp.sum(gated_unit * gated_unit) / data_count,
-            jnp.sum(convx_unit * convx_unit) / data_count,
-            jnp.sum(convbc_unit * convbc_unit) / full_copies,
-            jnp.sum(head_unit * head_unit) / data_count,
-        ),
-        ("dp", "tensor"),
-    )
+    ) = unit_sums[:, 0]
+    norm_sq_total = jnp.sum(norm_unit * norm_unit)
+    convbc_sq_total = jnp.sum(convbc_unit * convbc_unit)
     in_rate = D ** (-0.5)
     out_rate = INNER ** (-0.5)
     z_upd = -in_rate * normalized(z_unit, z_total, D * INNER)

time: 1290 us -> 838 us (0.65)
  waiting for transfers between devices: 799 us -> 261 us
  blocking collectives: 136 us -> 0 us
  other arithmetic: 97 us -> 187 us
  local copies, waits for them, and re-layouts: 75 us -> 160 us
  starting transfers between devices: 0.86 us -> 75.9 us
    reduce_scatter x5 -> x0, waiting for transfers between devices: 520 us -> none  [the longest x1 149 us: shards(): lax.psum_scatter(out_part, 'dp', scatter_dimension=0, tiled=True)]
    ppermute x0 -> x72, waiting for transfers between devices: none -> 261 us  [swap(): lax.ppermute(value, axis, [(place, place ^ bit) for place in range(size)])]
    psum x2 -> x0, waiting for transfers between devices: 140 us -> none  [the longest x1 77.8 us: shards(): lax.psum((rows_times(scaled_low, low_out), squares), 'tensor')]
    all_gather x4 -> x0, waiting for transfers between devices: 139 us -> none  [the longest x1 68.4 us: shards(): lax.all_gather(x_weight.astype(jnp.bfloat16), 'dp', axis=0, tiled=True)]
    psum x4 -> x0, blocking collectives: 104 us -> none  [the longest x1 37.3 us: shards(): lax.psum((jnp.sum(z_unit * z_unit), jnp.sum(x_unit * x_unit), jnp.sum(bc_...]
    ppermute x0 -> x72, starting transfers between devices: none -> 75.9 us  [swap(): lax.ppermute(value, axis, [(place, place ^ bit) for place in range(size)])]
    all_gather x1 -> x0, blocking collectives: 32.5 us -> none  [shards(): lax.all_gather(dt_weight.astype(jnp.bfloat16), 'dp', axis=0, tiled=True)]
    unnamed x206 -> x434, local copies, waits for them, and re-layouts: 13.4 us -> 36.9 us
  transfers between devices with their start and end apart: 11 -> 72, of which waited for: 11 -> 29; matrix products, arithmetic and copies ran while one was open for 12% -> 52% of each run, Pallas kernels for 0% -> 0%
where the time goes in v1:
time: 838 us; the launch traced here: 827 us
  waiting for transfers between devices  261 us (31%)
  other arithmetic  187 us (22%)
  local copies, waits for them, and re-layouts  160 us (19%)
  matrix products  127 us (15%)
  starting transfers between devices  75.9 us (9%)
  between operations  13.9 us (2%)
    ppermute x72, waiting for transfers between devices, swap(): lax.ppermute(value, axis, [(place, place ^ bit) for place in range(size)])  261 us
    ppermute x72, starting transfers between devices, swap(): lax.ppermute(value, axis, [(place, place ^ bit) for place in range(size)])  75.9 us
    dot_general x6, matrix products, advance(): inside = jnp.einsum('hts,hps->hpt', mixing, block_x, precision=highest)  39.5 us
    unnamed x434, local copies, waits for them, and re-layouts  36.9 us
    another operation x17, other arithmetic  25.3 us
    dot_general x5, matrix products, rows_times(): lax.dot_general(left, right, (((1,), (1,)), ((), ())), preferred_element_...  22 us
    select_n x12, other arithmetic, join_halves(): jnp.where(half == 0, jnp.concatenate([mine, other], axis=axis), jnp.conca...  19.1 us
  transfers between devices with their start and end apart: 72, of which 29 were waited for; matrix products, arithmetic and copies ran while one was open for 52% of the time, Pallas kernels for 0%

profile of v1, /device:TPU:0, one launch (start us, length us, event | category | flops | bytes accessed | tf_op | source)
XLA Modules:
  0.0 826.7 jit_solution(3428740334670708345)
XLA Ops:
  21.1 32.0 %collective-permute-done.5 = s32[5,128]{1,0:T(8,128)S(1)} collective-permute-done((s32[5,128]{1,0:T(8,128)S(1)}, s32[5,128]{1,0:T(8,128)S(1)}, u32[]{:S(2)}, u32[]{:S(2)}) %collective-permute-start.5) | collective-permute-done | bytes 2592 | tf_op jit(solution)/shard_map/ppermute | solution.py:125
  55.9 8.4 %collective-permute-done.6 = bf16[1,160,128]{2,1,0:T(8,128)(2,1)S(1)} collective-permute-done((bf16[1,160,128]{2,1,0:T(8,128)(2,1)S(1)}, bf16[1,160,128]{2,1,0:T(8,128)(2,1)S(1)}, u32[]{:S(2)}, u32[]{:S(2)}) %collective-permute-start.6) | collective-permute-done | bytes 40992 | tf_op jit(solution)/shard_map/ppermute | solution.py:125
  87.2 36.5 %collective-permute-done.18 = bf16[512,512]{1,0:T(8,128)(2,1)} collective-permute-done((bf16[512,512]{1,0:T(8,128)(2,1)}, bf16[512,512]{1,0:T(8,128)(2,1)}, u32[]{:S(2)}, u32[]{:S(2)}) %collective-permute-start.18) | collective-permute-done | bytes 524320 | tf_op jit(solution)/shard_map/ppermute | solution.py:125
  128.2 6.7 collective-permute-done.3
  137.6 6.2 collective-permute-done.12
  166.6 17.0 %collective-permute-done.4 = bf16[1024,512]{1,0:T(8,128)(2,1)S(1)} collective-permute-done((bf16[1024,512]{1,0:T(8,128)(2,1)S(1)}, bf16[1024,512]{1,0:T(8,128)(2,1)S(1)}, u32[]{:S(2)}, u32[]{:S(2)}) %collective-permute-start.4) | collective-permute-done | bytes 1048608 | tf_op jit(solution)/shard_map/ppermute | solution.py:125
  208.8 30.1 %while.46 = (s32[]{:T(128)}, f32[2,8,64,128]{3,2,1,0:T(8,128)S(1)}, s32[2]{0:T(128)S(1)}, f32[2,2,8,64,256]{4,3,2,1,0:T(8,128)}, f32[2,2,8,64,128]{4,3,2,1,0:T(8...) while((s32[]{:T(128)}, f32[2,8,64,128]{3,2,1,0:T(8,128)S(1)}, ...), condition=%wide.region_4.5_spmd.clone, body=%wide.region_1.4_spmd.clone.sunk | while | flops 1819498496 | bytes 37907116 | solution.py:76
  213.4 6.4 fusion.310
  228.5 6.4 fusion.310
  246.9 4.9 reshape.1448
  261.8 6.5 multiply_reduce_fusion.12
  268.3 6.1 convert_multiply_fusion
  297.6 6.5 copy.423
  304.5 7.0 convolution_bitcast_fusion.4
  311.6 7.7 multiply_reduce_fusion.6
  327.4 123.4 %while.47 = (s32[]{:T(128)}, f32[8]{0:T(128)}, f32[2,8,64,128]{3,2,1,0:T(8,128)}, f32[2,2,8,64,256]{4,3,2,1,0:T(8,128)}, f32[2,2,8,256]{3,2,1,0:T(8,128)}, /*ind...) while((s32[]{:T(128)}, f32[8]{0:T(128)}, ...), condition=%wide.region_20.21_spmd.clone, body=%wide.region_7.20_spmd.clone.sunk | while | flops 4253329408 | bytes 67376968 | solution.py:76
  351.9 8.6 %fusion.333 = (f32[2,8,256]{2,1,0:T(8,128)}, f32[2,8,256]{2,1,0:T(8,128)}, f32[2,8,256]{2,1,0:T(8,128)}, f32[2,256,256]{2,1,0:T(8,128)}) fusion(f32[2,8,256]{2,1,0:T(8,128)} %get-tuple-element.1542, f32[2,8,256]{2,1,0:T(8,128)S(1)} %dynamic-slice_bitcast_fusion.13, f32[2,256,256]{2,1,0:T(8,128)} %fusion.332, ...), kind=kOutput, calls=%fused_computation.70.clone.1 | convolution fusion | flops 820891648 | bytes 3358720 | tf_op jit(solution)/shard_map/transpose(jvp(vmap()))/while/body/eval_jaxpr/checkpoint/hts,hps->hpt/dot_general | solution.py:59
  370.7 5.0 reduce-window.74
  379.3 4.8 fusion.337
  413.5 8.6 %fusion.333 = (f32[2,8,256]{2,1,0:T(8,128)}, f32[2,8,256]{2,1,0:T(8,128)}, f32[2,8,256]{2,1,0:T(8,128)}, f32[2,256,256]{2,1,0:T(8,128)}) fusion(f32[2,8,256]{2,1,0:T(8,128)} %get-tuple-element.1542, f32[2,8,256]{2,1,0:T(8,128)S(1)} %dynamic-slice_bitcast_fusion.13, f32[2,256,256]{2,1,0:T(8,128)} %fusion.332, ...), kind=kOutput, calls=%fused_computation.70.clone.1 | convolution fusion | flops 820891648 | bytes 3358720 | tf_op jit(solution)/shard_map/transpose(jvp(vmap()))/while/body/eval_jaxpr/checkpoint/hts,hps->hpt/dot_general | solution.py:59
  432.3 5.0 reduce-window.74
  441.5 4.8 fusion.337
  455.4 4.9 reshape.1449
  503.5 7.3 fusion.147
  518.1 17.2 %collective-permute-done.66 = f32[41,128]{1,0:T(8,128)S(1)} collective-permute-done((f32[41,128]{1,0:T(8,128)S(1)}, f32[41,128]{1,0:T(8,128)S(1)}, u32[]{:S(2)}, u32[]{:S(2)}) %collective-permute-start.66) | collective-permute-done | bytes 21024 | tf_op jit(solution)/shard_map/ppermute | solution.py:125
  558.9 6.5 collective-permute-done.51
  572.1 46.0 %collective-permute-done.52 = f32[2,144,128]{2,1,0:T(8,128)S(1)} collective-permute-done((f32[2,144,128]{2,1,0:T(8,128)S(1)}, f32[2,144,128]{2,1,0:T(8,128)S(1)}, u32[]{:S(2)}, u32[]{:S(2)}) %collective-permute-start.52) | collective-permute-done | bytes 147488 | tf_op jit(solution)/shard_map/ppermute | solution.py:125
  622.2 8.2 collective-permute-done.53
  684.7 6.6 add_add_fusion
  725.5 19.8 %collective-permute-done.21 = bf16[2,128,2048]{2,1,0:T(8,128)(2,1)S(1)} collective-permute-done((bf16[2,128,2048]{2,1,0:T(8,128)(2,1)S(1)}, bf16[2,128,2048]{2,1,0:T(8,128)(2,1)S(1)}, u32[]{:S(2)}, u32[]{:S(2)}) %collective-permute-start.21) | collective-permute-done | bytes 1048608 | tf_op jit(solution)/shard_map/ppermute | solution.py:125
  746.5 19.3 %collective-permute-done.31 = bf16[2,128,2048]{2,1,0:T(8,128)(2,1)S(1)} collective-permute-done((bf16[2,128,2048]{2,1,0:T(8,128)(2,1)S(1)}, bf16[2,128,2048]{2,1,0:T(8,128)(2,1)S(1)}, u32[]{:S(2)}, u32[]{:S(2)}) %collective-permute-start.31) | collective-permute-done | bytes 1048608 | tf_op jit(solution)/shard_map/ppermute | solution.py:125
  767.7 10.5 %collective-permute-done.32 = bf16[128,2048]{1,0:T(8,128)(2,1)S(1)} collective-permute-done((bf16[128,2048]{1,0:T(8,128)(2,1)S(1)}, bf16[128,2048]{1,0:T(8,128)(2,1)S(1)}, u32[]{:S(2)}, u32[]{:S(2)}) %collective-permute-start.32) | collective-permute-done | bytes 524320 | tf_op jit(solution)/shard_map/ppermute | solution.py:125
  (1106 shorter events, 470.0 us)
Async XLA Ops:
  3.2 76.2 %collective-permute-start = (bf16[256,2048]{1,0:T(8,128)(2,1)}, bf16[256,2048]{1,0:T(8,128)(2,1)}, u32[]{:S(2)}, u32[]{:S(2)}) collective-permute-start(bf16[256,2048]{1,0:T(8,128)(2,1)} %dynamic-slice_bitcast_fusion.7), channel_id=1, source_target_pairs={{0,8},{4,12},{8,0},{12,4},{16,24},{20,28},{24,16},{28,20},{1,9},{5... | collective-permute-start | bytes 3145736 | tf_op jit(solution)/shard_map/ppermute | solution.py:125
  7.3 79.7 %collective-permute-start.25 = (bf16[256,2048]{1,0:T(8,128)(2,1)}, bf16[256,2048]{1,0:T(8,128)(2,1)}, u32[]{:S(2)}, u32[]{:S(2)}) collective-permute-start(bf16[256,2048]{1,0:T(8,128)(2,1)} %dynamic-slice_bitcast_fusion.6), channel_id=1, source_target_pairs={{0,8},{4,12},{8,0},{12,4},{16,24},{20,28},{24,16},{28,20},{1,9},{5... | collective-permute-start | bytes 3145736 | tf_op jit(solution)/shard_map/ppermute | solution.py:125
  8.0 45.1 %collective-permute-start.5 = (s32[5,128]{1,0:T(8,128)S(1)}, s32[5,128]{1,0:T(8,128)S(1)}, u32[]{:S(2)}, u32[]{:S(2)}) collective-permute-start(s32[5,128]{1,0:T(8,128)S(1)} %pad_bitcast_fusion.1), channel_id=1, source_target_pairs={{0,8},{4,12},{8,0},{12,4},{16,24},{20,28},{24,16},{28,20},{1,9},{5... | collective-permute-start | bytes 7688 | tf_op jit(solution)/shard_map/ppermute | solution.py:125
  10.9 61.2 %collective-permute-start.17 = (bf16[256,512]{1,0:T(8,128)(2,1)}, bf16[256,512]{1,0:T(8,128)(2,1)S(1)}, u32[]{:S(2)}, u32[]{:S(2)}) collective-permute-start(bf16[256,512]{1,0:T(8,128)(2,1)} %get-tuple-element.1286), channel_id=1, source_target_pairs={{0,8},{4,12},{8,0},{12,4},{16,24},{20,28},{24,16},{28,20},{1,9},{5... | collective-permute-start | bytes 786440 | tf_op jit(solution)/shard_map/ppermute | solution.py:125
  13.2 64.9 %collective-permute-start.2 = (bf16[256,512]{1,0:T(8,128)(2,1)}, bf16[256,512]{1,0:T(8,128)(2,1)S(1)}, u32[]{:S(2)}, u32[]{:S(2)}) collective-permute-start(bf16[256,512]{1,0:T(8,128)(2,1)} %get-tuple-element.1282), channel_id=1, source_target_pairs={{0,8},{4,12},{8,0},{12,4},{16,24},{20,28},{24,16},{28,20},{1,9},{5... | collective-permute-start | bytes 786440 | tf_op jit(solution)/shard_map/ppermute | solution.py:125
  75.2 48.5 %collective-permute-start.18 = (bf16[512,512]{1,0:T(8,128)(2,1)}, bf16[512,512]{1,0:T(8,128)(2,1)}, u32[]{:S(2)}, u32[]{:S(2)}) collective-permute-start(bf16[512,512]{1,0:T(8,128)(2,1)} %pad_maximum_fusion.7), channel_id=1, source_target_pairs={{0,16},{4,20},{8,24},{12,28},{16,0},{20,4},{24,8},{28,12},{1,17},{... | collective-permute-start | bytes 1572872 | tf_op jit(solution)/shard_map/ppermute | solution.py:125
  79.4 69.9 %collective-permute-start.1 = (bf16[256,2048]{1,0:T(8,128)(2,1)}, bf16[256,2048]{1,0:T(8,128)(2,1)}, u32[]{:S(2)}, u32[]{:S(2)}) collective-permute-start(bf16[256,2048]{1,0:T(8,128)(2,1)} %collective-permute-done), channel_id=1, source_target_pairs={{0,1},{1,0},{2,3},{3,2},{4,5},{5,4},{6,7},{7,6},{8,9},{9,8},{10,11... | collective-permute-start | bytes 3145736 | tf_op jit(solution)/shard_map/ppermute | solution.py:125
  81.9 53.0 %collective-permute-start.3 = (bf16[512,512]{1,0:T(8,128)(2,1)}, bf16[512,512]{1,0:T(8,128)(2,1)}, u32[]{:S(2)}, u32[]{:S(2)}) collective-permute-start(bf16[512,512]{1,0:T(8,128)(2,1)} %pad_maximum_fusion.5), channel_id=1, source_target_pairs={{0,16},{4,20},{8,24},{12,28},{16,0},{20,4},{24,8},{28,12},{1,17},{... | collective-permute-start | bytes 1572872 | tf_op jit(solution)/shard_map/ppermute | solution.py:125
  85.1 58.6 %collective-permute-start.12 = (bf16[512,512]{1,0:T(8,128)(2,1)}, bf16[512,512]{1,0:T(8,128)(2,1)S(1)}, u32[]{:S(2)}, u32[]{:S(2)}) collective-permute-start(bf16[512,512]{1,0:T(8,128)(2,1)} %pad_maximum_fusion.6), channel_id=1, source_target_pairs={{0,16},{4,20},{8,24},{12,28},{16,0},{20,4},{24,8},{28,12},{1,17},{... | collective-permute-start | bytes 1572872 | tf_op jit(solution)/shard_map/ppermute | solution.py:125
  87.0 65.4 %collective-permute-start.26 = (bf16[256,2048]{1,0:T(8,128)(2,1)}, bf16[256,2048]{1,0:T(8,128)(2,1)}, u32[]{:S(2)}, u32[]{:S(2)}) collective-permute-start(bf16[256,2048]{1,0:T(8,128)(2,1)} %collective-permute-done.25), channel_id=1, source_target_pairs={{0,1},{1,0},{2,3},{3,2},{4,5},{5,4},{6,7},{7,6},{8,9},{9,8},{10,11... | collective-permute-start | bytes 3145736 | tf_op jit(solution)/shard_map/ppermute | solution.py:125
  123.7 22.0 %collective-permute-start.10 = (bf16[8,128,256]{2,1,0:T(8,128)(2,1)S(1)}, bf16[8,128,256]{2,1,0:T(8,128)(2,1)}, u32[]{:S(2)}, u32[]{:S(2)}) collective-permute-start(bf16[8,128,256]{2,1,0:T(8,128)(2,1)S(1)} %maximum_select_fusion.10), channel_id=1, source_target_pairs={{0,2},{1,3},{2,0},{3,1},{4,6},{5,7},{6,4},{7,5},{8,10},{9,11},{10,... | collective-permute-start | bytes 1572872 | tf_op jit(solution)/shard_map/ppermute | solution.py:125
  134.9 133.3 %collective-permute-start.19 = (bf16[1024,512]{1,0:T(8,128)(2,1)}, bf16[1024,512]{1,0:T(8,128)(2,1)}, u32[]{:S(2)}, u32[]{:S(2)}) collective-permute-start(bf16[1024,512]{1,0:T(8,128)(2,1)} %pad_maximum_fusion.4), channel_id=1, source_target_pairs={{0,4},{4,0},{8,12},{12,8},{16,20},{20,16},{24,28},{28,24},{1,5},{5... | collective-permute-start | bytes 3145736 | tf_op jit(solution)/shard_map/ppermute | solution.py:125
  143.8 39.9 %collective-permute-start.4 = (bf16[1024,512]{1,0:T(8,128)(2,1)S(1)}, bf16[1024,512]{1,0:T(8,128)(2,1)S(1)}, u32[]{:S(2)}, u32[]{:S(2)}) collective-permute-start(bf16[1024,512]{1,0:T(8,128)(2,1)S(1)} %pad_maximum_fusion.2), channel_id=1, source_target_pairs={{0,4},{4,0},{8,12},{12,8},{16,20},{20,16},{24,28},{28,24},{1,5},{5... | collective-permute-start | bytes 3145736 | tf_op jit(solution)/shard_map/ppermute | solution.py:125
  145.7 113.7 %collective-permute-start.13 = (bf16[1024,512]{1,0:T(8,128)(2,1)}, bf16[1024,512]{1,0:T(8,128)(2,1)}, u32[]{:S(2)}, u32[]{:S(2)}) collective-permute-start(bf16[1024,512]{1,0:T(8,128)(2,1)} %pad_maximum_fusion.3), channel_id=1, source_target_pairs={{0,4},{4,0},{8,12},{12,8},{16,20},{20,16},{24,28},{28,24},{1,5},{5... | collective-permute-start | bytes 3145736 | tf_op jit(solution)/shard_map/ppermute | solution.py:125
  282.2 433.3 %collective-permute-start.20 = (bf16[2,256,2048]{2,1,0:T(8,128)(2,1)}, bf16[2,256,2048]{2,1,0:T(8,128)(2,1)}, u32[]{:S(2)}, u32[]{:S(2)}) collective-permute-start(bf16[2,256,2048]{2,1,0:T(8,128)(2,1)} %dynamic-slice_convert_fusion.1), channel_id=1, source_target_pairs={{0,1},{1,0},{2,3},{3,2},{4,5},{5,4},{6,7},{7,6},{8,9},{9,8},{10,11... | collective-permute-start | bytes 6291464 | tf_op jit(solution)/shard_map/ppermute | solution.py:125
  481.7 29.6 %collective-permute-start.33 = (f32[2,256,256]{2,1,0:T(8,128)}, f32[2,256,256]{2,1,0:T(8,128)}, u32[]{:S(2)}, u32[]{:S(2)}) collective-permute-start(f32[2,256,256]{2,1,0:T(8,128)} %constant_dynamic-slice_fusion.6), channel_id=1, source_target_pairs={{0,1},{1,0},{2,3},{3,2},{4,5},{5,4},{6,7},{7,6},{8,9},{9,8},{10,11... | collective-permute-start | bytes 1572872 | tf_op jit(solution)/shard_map/ppermute | solution.py:125
  487.7 60.3 %collective-permute-start.43 = (bf16[1024,512]{0,1:T(8,128)(2,1)}, bf16[1024,512]{0,1:T(8,128)(2,1)S(1)}, u32[]{:S(2)}, u32[]{:S(2)}) collective-permute-start(bf16[1024,512]{0,1:T(8,128)(2,1)} %slice.746), channel_id=1, source_target_pairs={{0,4},{4,0},{8,12},{12,8},{16,20},{20,16},{24,28},{28,24},{1,5},{5... | collective-permute-start | bytes 3145736 | tf_op jit(solution)/shard_map/ppermute | solution.py:125
  500.4 55.1 %collective-permute-start.46 = (bf16[1024,512]{0,1:T(8,128)(2,1)}, bf16[1024,512]{0,1:T(8,128)(2,1)}, u32[]{:S(2)}, u32[]{:S(2)}) collective-permute-start(bf16[1024,512]{0,1:T(8,128)(2,1)} %slice.745), channel_id=1, source_target_pairs={{0,4},{4,0},{8,12},{12,8},{16,20},{20,16},{24,28},{28,24},{1,5},{5... | collective-permute-start | bytes 3145736 | tf_op jit(solution)/shard_map/ppermute | solution.py:125
  510.8 24.5 %collective-permute-start.66 = (f32[41,128]{1,0:T(8,128)S(1)}, f32[41,128]{1,0:T(8,128)S(1)}, u32[]{:S(2)}, u32[]{:S(2)}) collective-permute-start(f32[41,128]{1,0:T(8,128)S(1)} %fusion.258), channel_id=1, source_target_pairs={{0,4},{4,0},{8,12},{12,8},{16,20},{20,16},{24,28},{28,24},{1,5},{5... | collective-permute-start | bytes 62984 | tf_op jit(solution)/shard_map/ppermute | solution.py:125
  512.5 25.6 %collective-permute-start.34 = (f32[2,128,256]{2,1,0:T(8,128)S(1)}, f32[2,128,256]{2,1,0:T(8,128)S(1)}, u32[]{:S(2)}, u32[]{:S(2)}) collective-permute-start(f32[2,128,256]{2,1,0:T(8,128)S(1)} %constant_dynamic-slice_fusion.5), channel_id=1, source_target_pairs={{0,2},{1,3},{2,0},{3,1},{4,6},{5,7},{6,4},{7,5},{8,10},{9,11},{10,... | collective-permute-start | bytes 786440 | tf_op jit(solution)/shard_map/ppermute | solution.py:125
  535.3 33.6 %collective-permute-start.54 = (bf16[1024,512]{0,1:T(8,128)(2,1)}, bf16[1024,512]{0,1:T(8,128)(2,1)}, u32[]{:S(2)}, u32[]{:S(2)}) collective-permute-start(bf16[1024,512]{0,1:T(8,128)(2,1)} %slice.744), channel_id=1, source_target_pairs={{0,4},{4,0},{8,12},{12,8},{16,20},{20,16},{24,28},{28,24},{1,5},{5... | collective-permute-start | bytes 3145736 | tf_op jit(solution)/shard_map/ppermute | solution.py:125
  550.9 67.3 %collective-permute-start.44 = (bf16[512,512]{0,1:T(8,128)(2,1)}, bf16[512,512]{0,1:T(8,128)(2,1)}, u32[]{:S(2)}, u32[]{:S(2)}) collective-permute-start(bf16[512,512]{0,1:T(8,128)(2,1)} %slice.749), channel_id=1, source_target_pairs={{0,16},{4,20},{8,24},{12,28},{16,0},{20,4},{24,8},{28,12},{1,17},{... | collective-permute-start | bytes 1572872 | tf_op jit(solution)/shard_map/ppermute | solution.py:125
  558.9 72.3 %collective-permute-start.47 = (bf16[512,512]{0,1:T(8,128)(2,1)}, bf16[512,512]{0,1:T(8,128)(2,1)}, u32[]{:S(2)}, u32[]{:S(2)}) collective-permute-start(bf16[512,512]{0,1:T(8,128)(2,1)} %slice.748), channel_id=1, source_target_pairs={{0,16},{4,20},{8,24},{12,28},{16,0},{20,4},{24,8},{28,12},{1,17},{... | collective-permute-start | bytes 1572872 | tf_op jit(solution)/shard_map/ppermute | solution.py:125
  565.5 52.6 %collective-permute-start.52 = (f32[2,144,128]{2,1,0:T(8,128)S(1)}, f32[2,144,128]{2,1,0:T(8,128)S(1)}, u32[]{:S(2)}, u32[]{:S(2)}) collective-permute-start(f32[2,144,128]{2,1,0:T(8,128)S(1)} %slice.576), channel_id=1, source_target_pairs={{0,16},{4,20},{8,24},{12,28},{16,0},{20,4},{24,8},{28,12},{1,17},{... | collective-permute-start | bytes 442376 | tf_op jit(solution)/shard_map/ppermute | solution.py:125
  572.1 62.6 %collective-permute-start.55 = (bf16[512,512]{0,1:T(8,128)(2,1)}, bf16[512,512]{0,1:T(8,128)(2,1)}, u32[]{:S(2)}, u32[]{:S(2)}) collective-permute-start(bf16[512,512]{0,1:T(8,128)(2,1)} %slice.747), channel_id=1, source_target_pairs={{0,16},{4,20},{8,24},{12,28},{16,0},{20,4},{24,8},{28,12},{1,17},{... | collective-permute-start | bytes 1572872 | tf_op jit(solution)/shard_map/ppermute | solution.py:125
  620.2 21.9 %collective-permute-start.45 = (bf16[256,512]{0,1:T(8,128)(2,1)}, bf16[256,512]{0,1:T(8,128)(2,1)}, u32[]{:S(2)}, u32[]{:S(2)}) collective-permute-start(bf16[256,512]{0,1:T(8,128)(2,1)} %slice.752), channel_id=1, source_target_pairs={{0,8},{4,12},{8,0},{12,4},{16,24},{20,28},{24,16},{28,20},{1,9},{5... | collective-permute-start | bytes 786440 | tf_op jit(solution)/shard_map/ppermute | solution.py:125
  696.3 24.3 %collective-permute-start.30 = (bf16[2,256,2048]{2,1,0:T(8,128)(2,1)}, bf16[2,256,2048]{2,1,0:T(8,128)(2,1)}, u32[]{:S(2)}, u32[]{:S(2)}) collective-permute-start(bf16[2,256,2048]{2,1,0:T(8,128)(2,1)} %dynamic-slice_convert_fusion), channel_id=1, source_target_pairs={{0,1},{1,0},{2,3},{3,2},{4,5},{5,4},{6,7},{7,6},{8,9},{9,8},{10,11... | collective-permute-start | bytes 6291464 | tf_op jit(solution)/shard_map/ppermute | solution.py:125
  719.2 26.1 %collective-permute-start.21 = (bf16[2,128,2048]{2,1,0:T(8,128)(2,1)S(1)}, bf16[2,128,2048]{2,1,0:T(8,128)(2,1)S(1)}, u32[]{:S(2)}, u32[]{:S(2)}) collective-permute-start(bf16[2,128,2048]{2,1,0:T(8,128)(2,1)S(1)} %dynamic-slice_convert_fusion.3), channel_id=1, source_target_pairs={{0,2},{1,3},{2,0},{3,1},{4,6},{5,7},{6,4},{7,5},{8,10},{9,11},{10,... | collective-permute-start | bytes 3145736 | tf_op jit(solution)/shard_map/ppermute | solution.py:125
  723.3 42.5 %collective-permute-start.31 = (bf16[2,128,2048]{2,1,0:T(8,128)(2,1)S(1)}, bf16[2,128,2048]{2,1,0:T(8,128)(2,1)S(1)}, u32[]{:S(2)}, u32[]{:S(2)}) collective-permute-start(bf16[2,128,2048]{2,1,0:T(8,128)(2,1)S(1)} %dynamic-slice_convert_fusion.2), channel_id=1, source_target_pairs={{0,2},{1,3},{2,0},{3,1},{4,6},{5,7},{6,4},{7,5},{8,10},{9,11},{10,... | collective-permute-start | bytes 3145736 | tf_op jit(solution)/shard_map/ppermute | solution.py:125
  745.6 21.7 %collective-permute-start.22 = (bf16[128,2048]{1,0:T(8,128)(2,1)S(1)}, bf16[128,2048]{1,0:T(8,128)(2,1)S(1)}, u32[]{:S(2)}, u32[]{:S(2)}) collective-permute-start(bf16[128,2048]{1,0:T(8,128)(2,1)S(1)} %fusion.145), channel_id=1, source_target_pairs={{0,8},{4,12},{8,0},{12,4},{16,24},{20,28},{24,16},{28,20},{1,9},{5... | collective-permute-start | bytes 1572872 | tf_op jit(solution)/shard_map/ppermute | solution.py:125
  786.2 25.8 %collective-permute-start.23 = (bf16[128,2048]{1,0:T(8,128)(2,1)}, bf16[128,2048]{1,0:T(8,128)(2,1)}, u32[]{:S(2)}, u32[]{:S(2)}) collective-permute-start(bf16[128,2048]{1,0:T(8,128)(2,1)} %constant_dynamic-update-slice_fusion.9), channel_id=1, source_target_pairs={{0,2},{1,3},{2,0},{3,1},{4,6},{5,7},{6,4},{7,5},{8,10},{9,11},{10,... | collective-permute-start | bytes 1572872 | tf_op jit(solution)/shard_map/ppermute | solution.py:125
  800.2 13.8 %collective-permute-start.36 = (bf16[128,2048]{1,0:T(8,128)(2,1)}, bf16[128,2048]{1,0:T(8,128)(2,1)}, u32[]{:S(2)}, u32[]{:S(2)}) collective-permute-start(bf16[128,2048]{1,0:T(8,128)(2,1)} %constant_dynamic-update-slice_fusion.17), channel_id=1, source_target_pairs={{0,2},{1,3},{2,0},{3,1},{4,6},{5,7},{6,4},{7,5},{8,10},{9,11},{10,... | collective-permute-start | bytes 1572872 | tf_op jit(solution)/shard_map/ppermute | solution.py:125
  (292 other events, 2973.2 us)

commit v2 on v1

v2 whole, which is shorter than its diff:
```python
import jax
import jax.numpy as jnp
from jax import lax
from jax.experimental import pallas as pl
from jax.experimental.pallas import tpu as pltpu
from jax.sharding import PartitionSpec as P

D = 2048
HEADS = 64
STATE = 128
INNER = 4096
KCONV = 4


norm_eps = 1e-05
decay_rate = 0.5
tiny_eps = 1e-30
unit_eps = 1e-06
vector_rate = 0.05


LANES = 128
PART = 256
WIDTH = 64


def cost_of(micros):
    return pl.CostEstimate(flops=micros * 1_000_000_000, bytes_accessed=1 << 20, transcendentals=0)


def two_parts(values):
    high = values.astype(jnp.bfloat16)
    return high, (values - high.astype(jnp.float32)).astype(jnp.bfloat16)


def plain(left, right):
    return lax.dot_general(
        left, right, (((1,), (0,)), ((), ())), preferred_element_type=jnp.float32
    )


def turned(left, right):
    return lax.dot_general(
        left, right, (((1,), (1,)), ((), ())), preferred_element_type=jnp.float32
    )


def fine(product, left, right):
    left_high, left_low = two_parts(left)
    right_high, right_low = two_parts(right)
    return (
        product(left_high, right_high)
        + product(left_high, right_low)
        + product(left_low, right_high)
    )


def running_sum(values, backward):
    rows = lax.broadcasted_iota(jnp.int32, (PART, PART), 0)
    columns = lax.broadcasted_iota(jnp.int32, (PART, PART), 1)
    within = (rows <= columns) if backward else (rows >= columns)
    ones = within.astype(jnp.float32).astype(jnp.bfloat16)

    def inside(block):
        high, rest = block.astype(jnp.bfloat16), block
        total = plain(ones, high)
        rest = block - high.astype(jnp.float32)
        for _ in range(2):
            part = rest.astype(jnp.bfloat16)
            total = total + plain(ones, part)
            rest = rest - part.astype(jnp.float32)
        return total

    blocks = [inside(values[:PART]), inside(values[PART:])]
    if backward:
        blocks[0] = blocks[0] + blocks[1][0:1]
    else:
        blocks[1] = blocks[1] + blocks[0][PART - 1 : PART]
    return jnp.concatenate(blocks, axis=0)


def sigmoid(values):
    return 1.0 / (1.0 + jnp.exp(-values))


def conv_rows(values, taps, same):
    result = taps[0:1] * values
    for offset in range(1, 4):
        shifted = pltpu.roll(values, offset, 0)
        result = result + taps[offset : offset + 1] * (shifted * same[offset - 1])
    return result


def conv_rows_back(grad, values, taps, same):
    length = values.shape[0]
    result = taps[0:1] * grad
    tap_rows = [jnp.sum(grad * values, axis=0, keepdims=True)]
    for offset in range(1, 4):
        kept = grad * same[offset - 1]
        result = result + pltpu.roll(taps[offset : offset + 1] * kept, length - offset, 0)
        tap_rows.append(
            jnp.sum(kept * pltpu.roll(values, offset, 0), axis=0, keepdims=True)
        )
    return result, tap_rows


def softplus(values):
    return jnp.maximum(values, 0.0) + jnp.log1p(jnp.exp(-jnp.abs(values)))


def marks_of(marks_ref):
    marks = marks_ref[0]
    same = [marks[:, place : place + 1] for place in (1, 2, 3)]
    return marks[:, 0:1], same, marks[:, 4:5]


def prepare(transposed, marks_ref, row_ref, bc_ref, dt_ref, taps_bc_ref, head_ref,
            bc_pre_ref, bc_ref_out, dt_out, cum_wide, dt_wide, cum_rows, score, bias):
    doc, same, _ = marks_of(marks_ref)
    bc_pre = conv_rows(bc_ref[0], taps_bc_ref[...], same)
    bc = bc_pre * sigmoid(bc_pre)
    bc_pre_ref[...] = bc_pre
    bc_ref_out[...] = bc
    b_mat, c_mat = bc[:, :LANES], bc[:, LANES:]
    first, second = slice(0, PART), slice(PART, 2 * PART)
    for place, (out_rows, in_rows) in enumerate(((first, first), (second, second), (second, first))):
        if transposed:
            score[place] = fine(turned, b_mat[in_rows], c_mat[out_rows])
        else:
            score[place] = fine(turned, c_mat[out_rows], b_mat[in_rows])
    rows = lax.broadcasted_iota(jnp.int32, (PART, PART), 0)
    columns = lax.broadcasted_iota(jnp.int32, (PART, PART), 1)
    causal = (rows <= columns) if transposed else (rows >= columns)
    doc_row = row_ref[0][0:1]
    for place, part in enumerate((first, second)):
        seen = causal & (doc[part] == doc_row[:, part])
        bias[place] = jnp.where(seen, 0.0, -1e30)
    step = softplus(dt_ref[0] + head_ref[0:1])
    decay = step * -jnp.exp(head_ref[1:2])
    total = running_sum(decay, False)
    dt_out[...] = step
    flipped = total.T
    lane = lax.broadcasted_iota(jnp.int32, (2 * PART, LANES), 1)
    for pair in range(cum_wide.shape[0]):
        one, two = 2 * pair, 2 * pair + 1
        cum_wide[pair] = jnp.where(lane < WIDTH, total[:, one : one + 1], total[:, two : two + 1])
        dt_wide[pair] = jnp.where(lane < WIDTH, step[:, one : one + 1], step[:, two : two + 1])
        cum_rows[one] = flipped[one : one + 1]
        cum_rows[two] = flipped[two : two + 1]


def edge_weights(wide, in_last):
    edge = wide[PART - 1 : PART]
    after = jnp.exp(wide[PART:] - edge) * in_last[PART:]
    before = jnp.exp(edge - wide[:PART]) * in_last[:PART]
    return after, before


def forward_body(marks_ref, row_ref, bc_ref, dt_ref, taps_bc_ref, head_ref, x_ref, z_ref, vec_ref,
                 scaled_ref, scan_ref, squares_ref,
                 bc_pre, bc_act, dt_act, cum_wide, dt_wide, cum_rows, score, bias):
    pair = pl.program_id(1)

    @pl.when(pair == 0)
    def _():
        prepare(False, marks_ref, row_ref, bc_ref, dt_ref, taps_bc_ref, head_ref,
                bc_pre, bc_act, dt_act, cum_wide, dt_wide, cum_rows, score, bias)
        squares_ref[...] = jnp.zeros_like(squares_ref)

    _, same, in_last = marks_of(marks_ref)
    vec = vec_ref[...]
    pre = conv_rows(x_ref[0], vec[0:4], same)
    values = pre * sigmoid(pre)
    wide = cum_wide[pair]
    stepped = dt_wide[pair] * values
    high, low_part = two_parts(stepped)
    both = jnp.concatenate([high, low_part], axis=1)
    lane = lax.broadcasted_iota(jnp.int32, (PART, LANES), 1)
    blocks = []
    for place in range(2):
        part = slice(place * PART, (place + 1) * PART)
        answers = []
        for k in range(2):
            row = cum_rows[2 * pair + k][:, part]
            kernel = jnp.exp(wide[part, k * WIDTH : k * WIDTH + 1] - row + bias[place])
            mixing_high, mixing_low = two_parts(score[place] * kernel)
            answer = plain(mixing_high, both[part])
            answers.append(
                answer[:, :LANES] + answer[:, LANES:] + plain(mixing_low, high[part])
            )
        blocks.append(jnp.where(lane < WIDTH, answers[0], answers[1]))
    after, before = edge_weights(wide, in_last)
    blocks[1] = blocks[1] + after * fine(plain, score[2], before * stepped[:PART])
    scanned = jnp.concatenate(blocks, axis=0)
    scan_ref[0] = scanned
    gate = z_ref[0]
    gated = (scanned + vec[5:6] * values) * (gate * sigmoid(gate))
    squares_ref[0] = squares_ref[0] + gated * gated
    scaled_ref[0] = (gated * vec[4:5]).astype(scaled_ref.dtype)


def backward_body(marks_ref, row_ref, bc_ref, dt_ref, taps_bc_ref, head_ref, x_ref, z_ref, vec_ref,
                  scan_ref, grad_ref, sq_grad_ref,
                  z_out, x_out, bc_out, dt_out, vec_out, taps_bc_out, head_out,
                  bc_pre, bc_act, dt_act, cum_wide, dt_wide, cum_rows, score, bias,
                  score_grad, from_rows, from_columns, from_in):
    pair = pl.program_id(1)

    @pl.when(pair == 0)
    def _():
        prepare(True, marks_ref, row_ref, bc_ref, dt_ref, taps_bc_ref, head_ref,
                bc_pre, bc_act, dt_act, cum_wide, dt_wide, cum_rows, score, bias)
        score_grad[...] = jnp.zeros_like(score_grad)
        from_rows[...] = jnp.zeros_like(from_rows)
        from_columns[...] = jnp.zeros_like(from_columns)
        from_in[...] = jnp.zeros_like(from_in)

    _, same, in_last = marks_of(marks_ref)
    vec = vec_ref[...]
    taps, gain, skip = vec[0:4], vec[4:5], vec[5:6]
    x_raw = x_ref[0]
    pre = conv_rows(x_raw, taps, same)
    pre_sig = sigmoid(pre)
    values = pre * pre_sig
    wide = cum_wide[pair]
    step = dt_wide[pair]
    stepped = step * values
    gate = z_ref[0]
    gate_sig = sigmoid(gate)
    gate_act = gate * gate_sig
    scanned = scan_ref[0]
    mixed = scanned + skip * values
    gated = mixed * gate_act
    scaled_grad = grad_ref[0]
    gated_grad = scaled_grad * gain + 2.0 * sq_grad_ref[0][:, 0:1] * gated
    z_out[0] = (gated_grad * mixed * (gate_sig * (1.0 + gate * (1.0 - gate_sig)))).astype(z_out.dtype)
    grad = gated_grad * gate_act
    rows = [
        None, None, None, None,
        jnp.sum(scaled_grad * gated, axis=0, keepdims=True),
        jnp.sum(grad * values, axis=0, keepdims=True),
    ]
    high, low_part = two_parts(grad)
    both = jnp.concatenate([high, low_part], axis=1)
    lane = lax.broadcasted_iota(jnp.int32, (PART, LANES), 1)

    def add_exponents(head, out_part, in_part, terms):
        from_rows[head, :, out_part] += jnp.sum(terms, axis=0, keepdims=True)
        gone = jnp.sum(terms, axis=1, keepdims=True)
        from_columns[in_part] += jnp.where(lane == head, gone, 0.0)

    blocks = []
    for place in range(2):
        part = slice(place * PART, (place + 1) * PART)
        answers = []
        total = score_grad[place]
        for k in range(2):
            row = cum_rows[2 * pair + k][:, part]
            kernel = jnp.exp(row - wide[part, k * WIDTH : k * WIDTH + 1] + bias[place])
            mixing = score[place] * kernel
            mixing_high, mixing_low = two_parts(mixing)
            answer = plain(mixing_high, both[part])
            answers.append(
                answer[:, :LANES] + answer[:, LANES:] + plain(mixing_low, high[part])
            )
            own = (lane < WIDTH) if k == 0 else (lane >= WIDTH)
            own_high, own_low = two_parts(jnp.where(own, stepped[part], 0.0))
            pulled = turned(
                jnp.concatenate([own_high, own_high], axis=1), both[part]
            ) + turned(own_low, high[part])
            total = total + pulled * kernel
            add_exponents(2 * pair + k, part, part, pulled * mixing)
        score_grad[place] = total
        blocks.append(jnp.where(lane < WIDTH, answers[0], answers[1]))
    after, before = edge_weights(wide, in_last)
    late = after * grad[PART:]
    early = before * stepped[:PART]
    blocks[0] = blocks[0] + before * fine(plain, score[2], late)
    for k in range(2):
        own = (lane < WIDTH) if k == 0 else (lane >= WIDTH)
        pulled = fine(turned, jnp.where(own, early, 0.0), late)
        score_grad[2] = score_grad[2] + pulled
        add_exponents(2 * pair + k, slice(PART, 2 * PART), slice(0, PART), pulled * score[2])
    pulled_in = jnp.concatenate(blocks, axis=0)
    places = lax.broadcasted_iota(jnp.int32, (LANES, LANES), 0) // WIDTH + 2 * pair
    columns = lax.broadcasted_iota(jnp.int32, (LANES, LANES), 1)
    chosen = (places == columns).astype(jnp.float32).astype(jnp.bfloat16)
    chosen = jnp.concatenate([chosen, chosen], axis=0)
    from_in[...] += plain(jnp.concatenate(two_parts(values * pulled_in), axis=1), chosen)
    pre_grad = (skip * grad + step * pulled_in) * (pre_sig * (1.0 + pre * (1.0 - pre_sig)))
    x_grad, rows[:4] = conv_rows_back(pre_grad, x_raw, taps, same)
    x_out[0] = x_grad.astype(x_out.dtype)
    vec_out[0] = jnp.concatenate(rows + [jnp.zeros((2, LANES), jnp.float32)], axis=0)

    @pl.when(pair == pl.num_programs(1) - 1)
    def _():
        steps = dt_act[...]
        rate = -jnp.exp(head_ref[1:2])
        direct = from_in[...]
        heads = from_rows.shape[0]
        arrived = jnp.concatenate(
            [from_rows[head] for head in range(heads)]
            + [jnp.zeros((LANES - heads, 2 * PART), jnp.float32)],
            axis=0,
        ).T
        decay_grad = running_sum(arrived - from_columns[...], True)
        step_grad = (direct + rate * decay_grad) * sigmoid(dt_ref[0] + head_ref[0:1])
        dt_out[0] = step_grad
        head_out[0] = jnp.concatenate(
            [
                jnp.sum(step_grad, axis=0, keepdims=True),
                rate * jnp.sum(decay_grad * steps, axis=0, keepdims=True),
                jnp.zeros((6, LANES), jnp.float32),
            ],
            axis=0,
        )
        b_mat, c_mat = bc_act[:, :LANES], bc_act[:, LANES:]
        first, second, cross = score_grad[0], score_grad[1], score_grad[2]
        b_grad = jnp.concatenate(
            [
                fine(plain, first, c_mat[:PART]) + fine(plain, cross, c_mat[PART:]),
                fine(plain, second, c_mat[PART:]),
            ],
            axis=0,
        )
        c_grad = jnp.concatenate(
            [
                fine(plain, first.T, b_mat[:PART]),
                fine(plain, second.T, b_mat[PART:]) + fine(plain, cross.T, b_mat[:PART]),
            ],
            axis=0,
        )
        shape = bc_pre[...]
        slope = sigmoid(shape)
        slope = slope * (1.0 + shape * (1.0 - slope))
        bc_grad, tap_rows = conv_rows_back(
            jnp.concatenate([b_grad, c_grad], axis=1) * slope, bc_ref[0], taps_bc_ref[...], same
        )
        bc_out[0] = bc_grad
        taps_bc_out[0] = jnp.concatenate(
            tap_rows + [jnp.zeros((4, 2 * LANES), jnp.float32)], axis=0
        )


def slot_block(first, *shape):
    return pl.BlockSpec((1,) + shape, lambda slot, pair: (slot + first, 0, 0))


def whole_block(*shape):
    return pl.BlockSpec(shape, lambda slot, pair: (0,) * len(shape))


def pair_block(first, length):
    return pl.BlockSpec((1, length, LANES), lambda slot, pair: (slot + first, 0, pair))


def common_specs(first, length):
    return [
        slot_block(first, length, 8),
        slot_block(first, 8, length),
        slot_block(first, length, 2 * LANES),
        slot_block(first, length, LANES),
        whole_block(4, 2 * LANES),
        whole_block(8, LANES),
        pair_block(first, length),
        pair_block(first, length),
        pl.BlockSpec((8, LANES), lambda slot, pair: (0, pair)),
    ]


def common_scratch(length, pairs):
    return [
        pltpu.VMEM((length, 2 * LANES), jnp.float32),
        pltpu.VMEM((length, 2 * LANES), jnp.float32),
        pltpu.VMEM((length, LANES), jnp.float32),
        pltpu.VMEM((pairs, length, LANES), jnp.float32),
        pltpu.VMEM((pairs, length, LANES), jnp.float32),
        pltpu.VMEM((2 * pairs, 1, length), jnp.float32),
        pltpu.VMEM((3, PART, PART), jnp.float32),
        pltpu.VMEM((2, PART, PART), jnp.float32),
    ]


def mixer_forward(common, interpret=False):
    slots, length, width = common[6].shape
    pairs = width // LANES
    return pl.pallas_call(
        forward_body,
        grid=(slots, pairs),
        in_specs=common_specs(0, length),
        out_specs=[pair_block(0, length), pair_block(0, length), slot_block(0, length, LANES)],
        out_shape=[
            jax.ShapeDtypeStruct((slots, length, width), jnp.bfloat16),
            jax.ShapeDtypeStruct((slots, length, width), jnp.float32),
            jax.ShapeDtypeStruct((slots, length, LANES), jnp.float32),
        ],
        scratch_shapes=common_scratch(length, pairs),
        cost_estimate=cost_of(16),
        name="mixer_forward",
        interpret=interpret,
    )(*common)


def mixer_backward(common, scanned, scaled_grad, sq_grad, slot, earlier=(), interpret=False):
    slots, length, width = common[6].shape
    pairs = width // LANES
    given = len(common) + 3

    def body(*refs):
        backward_body(*refs[:given], *refs[given + len(earlier) :])

    return pl.pallas_call(
        body,
        grid=(1, pairs),
        in_specs=common_specs(slot, length)
        + [pair_block(slot, length), pair_block(slot, length), slot_block(slot, length, 8)]
        + [pl.BlockSpec(memory_space=pl.ANY) for _ in earlier],
        out_specs=[
            pair_block(slot, length),
            pair_block(slot, length),
            slot_block(slot, length, 2 * LANES),
            slot_block(slot, length, LANES),
            pl.BlockSpec((1, 8, LANES), lambda _, pair: (slot, 0, pair)),
            slot_block(slot, 8, 2 * LANES),
            slot_block(slot, 8, LANES),
        ],
        out_shape=[
            jax.ShapeDtypeStruct((slots, length, width), jnp.bfloat16),
            jax.ShapeDtypeStruct((slots, length, width), jnp.bfloat16),
            jax.ShapeDtypeStruct((slots, length, 2 * LANES), jnp.float32),
            jax.ShapeDtypeStruct((slots, length, LANES), jnp.float32),
            jax.ShapeDtypeStruct((slots, 8, width), jnp.float32),
            jax.ShapeDtypeStruct((slots, 8, 2 * LANES), jnp.float32),
            jax.ShapeDtypeStruct((slots, 8, LANES), jnp.float32),
        ],
        input_output_aliases={given + place: place for place in range(len(earlier))},
        scratch_shapes=common_scratch(length, pairs)
        + [
            pltpu.VMEM((3, PART, PART), jnp.float32),
            pltpu.VMEM((2 * pairs, 1, length), jnp.float32),
            pltpu.VMEM((length, LANES), jnp.float32),
            pltpu.VMEM((length, LANES), jnp.float32),
        ],
        cost_estimate=cost_of(16),
        name="mixer_backward",
        interpret=interpret,
    )(*common, scanned, scaled_grad, sq_grad, *earlier)


def input_body(place_ref, z_ref, x_ref, dt_ref, z_rows_ref, x_rows_ref, dt_rows_ref, *rest):
    del place_ref

    def flat(ref):
        return ref[...].reshape(-1, ref.shape[-1])

    total = (
        turned(flat(z_ref), z_rows_ref[...])
        + turned(flat(x_ref), x_rows_ref[...])
        + plain(flat(dt_ref), dt_rows_ref[...])
    ).reshape(rest[-1].shape)
    for added in rest[:-1]:
        total = total + added[...]
    rest[-1][...] = total


def input_terms(place, z_low, x_low, dt_low, low_z, low_x, low_dt, *added):
    tokens = z_low.shape[0] // 4
    width = low_z.shape[1]
    features = low_z.shape[0]
    block = features // 4

    def by_half(values):
        return values.reshape(2, 2, tokens, -1)

    def half_block(values):
        return pl.BlockSpec((2, 1, tokens, values.shape[1]), lambda at, where: (0, where[0], 0, 0))

    weight = pl.BlockSpec((block, width), lambda at, where: (at, 0))
    out = pl.BlockSpec((2, tokens, block), lambda at, where: (0, 0, at))
    return pl.pallas_call(
        input_body,
        grid_spec=pltpu.PrefetchScalarGridSpec(
            num_scalar_prefetch=1,
            grid=(4,),
            in_specs=[
                half_block(z_low),
                half_block(x_low),
                half_block(dt_low),
                weight,
                weight,
                pl.BlockSpec((low_dt.shape[0], block), lambda at, where: (0, at)),
            ]
            + [out] * len(added),
            out_specs=out,
        ),
        out_shape=jax.ShapeDtypeStruct((2, tokens, features), jnp.float32),
        cost_estimate=cost_of(6),
        name="input_terms",
    )(
        place.astype(jnp.int32).reshape(1),
        by_half(z_low),
        by_half(x_low),
        by_half(dt_low),
        low_z,
        low_x,
        low_dt,
        *added,
    )


def document_marks(segments):
    slots, length = segments.shape
    docs = segments.astype(jnp.float32)
    columns = [docs]
    for offset in (1, 2, 3):
        same = (segments[:, offset:] == segments[:, :-offset]).astype(jnp.float32)
        columns.append(jnp.pad(same, ((0, 0), (offset, 0))))
    columns.append((segments == segments[:, PART - 1 : PART]).astype(jnp.float32))
    zero = jnp.zeros_like(docs)
    marks = jnp.stack(columns + [zero] * 3, axis=-1)
    return marks, jnp.broadcast_to(docs[:, None, :], (slots, 8, length))


def norm_input(values, gain):
    mean_square = jnp.mean(values * values, axis=1, keepdims=True)
    return values * lax.rsqrt(mean_square + norm_eps) * gain


def rows_times(left, right):
    return lax.dot_general(
        left, right, (((1,), (1,)), ((), ())), preferred_element_type=jnp.float32
    )


def tokens_out(left, right):
    return lax.dot_general(
        left, right, (((0,), (0,)), ((), ())), preferred_element_type=jnp.float32
    )


def mix_state(old_state, fresh_term):
    return decay_rate * old_state + (1.0 - decay_rate) * fresh_term


def normalized(unit, square_total, entries):
    return unit * lax.rsqrt(square_total / entries + unit_eps)


def swap(value, axis, bit):
    size = lax.axis_size(axis)
    return lax.ppermute(value, axis, [(place, place ^ bit) for place in range(size)])


def add_over(value, axis, bits):
    for bit in bits:
        value = value + swap(value, axis, bit)
    return value


PAIR = 2


def dp_bits():
    count = lax.axis_size("dp")
    rest = [1 << place for place in reversed(range(count.bit_length() - 1)) if 1 << place != PAIR]
    return [PAIR] + rest


def block_masks():
    bits = dp_bits()
    return [
        sum(bit for place, bit in enumerate(bits) if (number >> place) & 1)
        for number in range(lax.axis_size("dp"))
    ]


def place_of(offset):
    return sum(
        ((offset // bit) % 2) << place for place, bit in enumerate(dp_bits())
    )


def to_relative(values, mine):
    blocks = lax.axis_size("dp")
    width = values.shape[-1] // blocks
    return jnp.concatenate(
        [
            lax.dynamic_slice_in_dim(values, (mine ^ mask) * width, width, values.ndim - 1)
            for mask in block_masks()
        ],
        axis=-1,
    )


def from_relative(values, mine):
    blocks = lax.axis_size("dp")
    width = values.shape[-1] // blocks
    return jnp.concatenate(
        [
            lax.dynamic_slice_in_dim(values, place_of(mine ^ block) * width, width, values.ndim - 1)
            for block in range(blocks)
        ],
        axis=-1,
    )


def halves(values, half, axis):
    width = values.shape[axis] // 2
    mine = lax.dynamic_slice_in_dim(values, half * width, width, axis)
    other = lax.dynamic_slice_in_dim(values, (1 - half) * width, width, axis)
    return mine, other


def join_halves(mine, other, half, axis):
    return jnp.where(
        half == 0,
        jnp.concatenate([mine, other], axis=axis),
        jnp.concatenate([other, mine], axis=axis),
    )


def after(value, *others):
    return lax.optimization_barrier((value,) + others)[0] if others else value


def step(*values):
    return lax.optimization_barrier(values)


def gather_middle(held):
    middle = dp_bits()[1:-1]
    for bit in middle[:-1]:
        held = jnp.concatenate([held, swap(held, "dp", bit)], axis=0)
    return held, swap(held, "dp", middle[-1])


def gradient_rows(left, right, place, kind, *added):
    part = left.shape[1] // 4
    total = tokens_out(left[:, place * part : (place + 1) * part], right)
    for value in added:
        total = total + value.astype(jnp.float32)
    return total.astype(kind)


def low_bits(value):
    return value.astype(jnp.bfloat16)


def middle_sum(held, got):
    held = held + got
    for bit in reversed(dp_bits()[1:-2]):
        count = held.shape[0] // 2
        sent = swap(low_bits(held[count:]), "dp", bit)
        held = held[:count] + sent.astype(jnp.float32)
    count = held.shape[0] // 2
    return held[:count], low_bits(held[count:])


def kept_and_sent(held, tensor_at, bit, kind):
    mine, other = halves(held, (tensor_at // bit) % 2, 1)
    return mine, other.astype(kind)


def share_tokens(terms, tensor_at):
    held = terms
    for bit in (1, 2):
        mine, other = kept_and_sent(held, tensor_at, bit, jnp.float32)
        held = mine + swap(other, "tensor", bit)
    return held[0] + swap(held[1], "dp", PAIR)


def flip_pairs(values):
    blocks = lax.axis_size("dp")
    width = values.shape[-1] // blocks
    pieces = [values[..., (place ^ 1) * width : ((place ^ 1) + 1) * width] for place in range(blocks)]
    return jnp.concatenate(pieces, axis=-1)


def whole_tokens(values, tensor_at):
    for bit in (2, 1):
        values = join_halves(values, swap(values, "tensor", bit), (tensor_at // bit) % 2, 0)
    return values


def shards(
    block_input,
    out_grad,
    seg_ids,
    slot_live,
    norm_gain,
    z_weight,
    x_weight,
    bc_weight,
    dt_weight,
    conv_x,
    conv_bc,
    head_params,
    gated_gain,
    out_weight,
    norm_gain_sq,
    z_rows,
    z_cols,
    x_rows,
    x_cols,
    bc_rows,
    bc_cols,
    dt_rows,
    dt_cols,
    conv_x_sq,
    conv_bc_sq,
    head_sq,
    gated_gain_sq,
    out_rows,
    out_cols,
):
    data_count = lax.axis_size("dp")
    data_at = lax.axis_index("dp")
    tensor_at = lax.axis_index("tensor")
    half = (data_at // PAIR) % 2
    core = tensor_at % 2
    row_count = z_weight.shape[0]
    quarter = row_count // 4
    slot_tokens = block_input.shape[1]
    f32, bf16 = jnp.float32, jnp.bfloat16

    share = slot_tokens // 4
    share_at = (core * 2 + tensor_at // 2) * share
    last_bit = dp_bits()[-1]

    def share_of(values):
        return lax.dynamic_slice_in_dim(values, share_at, share, 0)

    def halves_of(weight):
        return halves(weight.astype(bf16), half, 1)

    def rows_of(*pieces):
        return jnp.concatenate(pieces, axis=0)

    whole_numbers = jnp.concatenate(
        [seg_ids[0], jnp.broadcast_to(slot_live, (8 * 128 - slot_tokens,))]
    ).astype(bf16).reshape(-1, 128)
    dt_rows_low = dt_weight.astype(bf16).T
    bc_mine = lax.dynamic_slice_in_dim(bc_weight.astype(bf16), tensor_at * quarter, quarter, 0)
    small = rows_of(bc_mine.reshape(-1, 128), dt_rows_low.reshape(-1, 128))
    small_count = small.shape[0]
    x_mine, x_other = halves_of(x_weight)
    small_far = swap(rows_of(small, whole_numbers), "dp", PAIR)
    x_far = swap(x_other, "dp", PAIR)
    small_far, x_far, x_mine, small, z_weight, out_weight, block_input, out_grad = step(
        small_far, x_far, x_mine, small, z_weight, out_weight, block_input, out_grad
    )

    far_numbers = small_far[small_count:].astype(jnp.int32)
    segments = jnp.stack([seg_ids[0], far_numbers.reshape(-1)[:slot_tokens]])
    live = jnp.stack([slot_live[0], far_numbers[-1, 0]]).astype(f32)
    small = jnp.stack([small, small_far[:small_count]])
    for bit in dp_bits()[1:-1]:
        small = rows_of(small, swap(small, "dp", bit))
    x_held, x_got = gather_middle(rows_of(x_mine, x_far))
    x_first = swap(x_held, "dp", last_bit)
    z_mine, z_other = halves_of(z_weight)
    out_mine, out_other = halves_of(out_weight)
    in_share, grad_share = share_of(block_input[0]), share_of(out_grad[0])
    marks, doc_rows = document_marks(segments)
    taps_x, _ = halves(conv_x, half, 1)
    per_head, _ = halves(head_params, half, 1)
    gain_inner, _ = halves(gated_gain, half, 0)
    head_count = per_head.shape[1]
    head_rows = jnp.pad(per_head, ((0, 5), (0, 128 - head_count)))
    vectors = jnp.concatenate(
        [taps_x, gain_inner[None], jnp.repeat(per_head[2], WIDTH)[None], jnp.zeros((2, taps_x.shape[1]))]
    )
    marks, doc_rows, head_rows, vectors, z_mine, out_mine = step(
        marks, doc_rows, head_rows, vectors, z_mine, out_mine
    )
    gain_rel = to_relative(norm_gain, data_at)
    own_rel = to_relative(block_input[0], data_at).astype(f32)
    x_got, x_first, small, z_other, in_share, grad_share, out_other, own_rel, marks, vectors = step(
        x_got, x_first, small, z_other, in_share, grad_share, out_other, own_rel, marks, vectors
    )

    x_second = swap(x_got, "dp", last_bit)
    small = rows_of(small, swap(small, "dp", last_bit))
    z_far = swap(z_other, "dp", PAIR)
    in_far = swap(in_share, "dp", PAIR)
    bc_piece_rows = quarter * bc_weight.shape[1] // 128
    bc_held = small[:, :bc_piece_rows].reshape(data_count, quarter, -1)
    x_second, small, z_far, in_far, z_mine, grad_share, out_other, bc_held = step(
        x_second, small, z_far, in_far, z_mine, grad_share, out_other, bc_held
    )

    z_held, z_got = gather_middle(rows_of(z_mine, z_far))
    z_first = swap(z_held, "dp", last_bit)
    in_far = join_halves(in_far, swap(in_far, "tensor", 2), tensor_at // 2, 0)
    bc_held = join_halves(bc_held, swap(bc_held, "tensor", 1), core, 1)
    low_x = rows_of(x_held, x_got, x_first, x_second)
    z_got, z_first, in_far, bc_held, grad_share, out_other, low_x = step(
        z_got, z_first, in_far, bc_held, grad_share, out_other, low_x
    )

    z_second = swap(z_got, "dp", last_bit)
    out_far = swap(out_other, "dp", PAIR)
    grad_far = swap(grad_share, "dp", PAIR)
    in_far = join_halves(in_far, swap(in_far, "tensor", 1), core, 0)
    bc_held = join_halves(bc_held, swap(bc_held, "tensor", 2), tensor_at // 2, 1)
    low_bc = bc_held.reshape(data_count * row_count, -1)
    in_rel = jnp.stack([own_rel, to_relative(in_far, data_at).astype(f32)])
    mean_square = jnp.mean(in_rel * in_rel, axis=-1, keepdims=True)
    normed_low = (in_rel * lax.rsqrt(mean_square + norm_eps) * gain_rel).astype(bf16)
    z_second, out_far, grad_far, normed_low = step(z_second, out_far, grad_far, normed_low)
    low_z = rows_of(z_held, z_got, z_first, z_second)
    out_held, out_got = gather_middle(rows_of(out_mine, out_far))
    out_first = swap(out_held, "dp", last_bit)
    grad_far = join_halves(grad_far, swap(grad_far, "tensor", 2), tensor_at // 2, 0)
    low_out = rows_of(out_held, out_got, out_first, swap(out_got, "dp", last_bit))
    grad_far = join_halves(grad_far, swap(grad_far, "tensor", 1), core, 0)
    both_grad = jnp.stack([out_grad[0], grad_far])

    low_dt = (
        small[:, bc_piece_rows:].reshape(data_count, dt_weight.shape[1], row_count).transpose(1, 0, 2)
    ).reshape(dt_weight.shape[1], -1)
    low_dt, _ = halves(low_dt, half, 0)
    low_dt = jnp.pad(low_dt, ((0, 128 - head_count), (0, 0)))
    normed_flat = normed_low.reshape(-1, normed_low.shape[-1])
    tokens = normed_flat.shape[0]

    def per_slot(values):
        return values.reshape(2, slot_tokens, -1)

    bc_raw = per_slot(jnp.dot(normed_flat, low_bc, preferred_element_type=f32))
    dt_raw = per_slot(rows_times(normed_flat, low_dt))
    x_raw = per_slot(jnp.dot(normed_flat, low_x, preferred_element_type=f32))
    gate_z = per_slot(jnp.dot(normed_flat, low_z, preferred_element_type=f32))
    common = (marks, doc_rows, bc_raw, dt_raw, conv_bc, head_rows, x_raw, gate_z, vectors)
    scaled_both, scanned, square_parts = mixer_forward(common)
    scaled_low = scaled_both.reshape(tokens, -1)

    projected = per_slot(rows_times(scaled_low, low_out))
    cot_rel = to_relative(both_grad, data_at) * live.astype(bf16)[:, None, None]
    totals = jnp.stack([jnp.sum(square_parts, axis=-1), jnp.sum(cot_rel.astype(f32) * projected, axis=-1)], axis=1)
    totals = totals + swap(totals, "tensor", 1)
    _, leaving = kept_and_sent(projected, tensor_at, 1, bf16)
    arriving = swap(after(leaving, totals), "tensor", 1)
    totals = totals + swap(totals, "tensor", 2)
    totals = totals + swap(totals, "dp", PAIR)[::-1]
    total_squares, rms_grad = totals[:, 0], totals[:, 1]
    inv_rms = lax.rsqrt(total_squares / INNER + norm_eps)
    squares_grad = rms_grad * -0.5 * inv_rms * inv_rms * inv_rms / INNER
    proj_grad = (cot_rel.astype(f32) * inv_rms[:, :, None]).astype(bf16).reshape(tokens, -1)
    scaled_grad = per_slot(jnp.dot(proj_grad, low_out, preferred_element_type=f32))

    part = low_out.shape[0] // 4
    middle_bit = dp_bits()[-2]

    def across(value, bit):
        return swap(value, "dp", bit).astype(f32)

    out_sent = [gradient_rows(proj_grad, scaled_low, place, bf16) for place in (3, 2)]
    out_passed, out_kept = [swap(value, "dp", last_bit) for value in out_sent]
    gradients = (
        after(scaled_grad, *out_sent, arriving),
        jnp.broadcast_to(squares_grad[:, :, None], (2, slot_tokens, 8)),
    )
    backward = mixer_backward(common, scanned, *gradients, 0)
    proj_later, out_passed, projected, *backward = step(proj_grad, out_passed, projected, *backward)
    shared, _ = kept_and_sent(projected, tensor_at, 1, bf16)
    shared, leaving = kept_and_sent(shared + arriving.astype(f32), tensor_at, 2, bf16)
    out_middle = gradient_rows(proj_later, scaled_low, 1, bf16, out_passed)
    out_middle, leaving, *backward = step(out_middle, leaving, *backward)
    out_got = across(out_middle, middle_bit)
    arriving = swap(leaving, "tensor", 2)
    inv_mine = lax.dynamic_slice_in_dim(inv_rms[0], share_at, share, 0)
    in_mine = to_relative(share_of(block_input[0]), data_at).astype(f32)
    cot_mine = to_relative(share_of(out_grad[0]), data_at).astype(f32) * live[0]
    z_both, x_both, bc_grad_part, dt_both, vector_terms, taps_bc_terms, head_terms = mixer_backward(
        common, scanned, *gradients, 1, backward
    )
    x_both, z_both, bc_grad_part, out_got, out_kept, arriving = step(
        x_both, z_both, bc_grad_part, out_got, out_kept, arriving
    )
    vector_terms = jnp.sum(vector_terms, axis=0)
    convx_slot, gated_slot = vector_terms[:4], vector_terms[4]
    convbc_part = jnp.sum(taps_bc_terms, axis=0)[:4]
    head_slot = jnp.concatenate(
        [
            jnp.sum(head_terms, axis=0)[:2, :head_count],
            jnp.sum(vector_terms[5].reshape(head_count, -1), axis=1)[None],
        ]
    )
    bc_kept, bc_leaving = kept_and_sent(bc_grad_part, tensor_at, 1, f32)
    bc_arriving = swap(bc_leaving, "tensor", 1)
    z_low = z_both.reshape(tokens, -1)
    x_low = x_both.reshape(tokens, -1)
    dt_low = dt_both.astype(bf16).reshape(tokens, -1)
    matrices = (low_z, low_x, low_dt)
    x_sent = gradient_rows(normed_flat, x_low, 3, bf16)
    x_low, z_low, x_sent, bc_arriving = step(x_low, z_low, x_sent, bc_arriving)

    x_passed = swap(x_sent, "dp", last_bit)
    bc_kept, bc_leaving = kept_and_sent(bc_kept + bc_arriving, tensor_at, 2, f32)
    bc_arriving = swap(bc_leaving, "tensor", 2)
    x_low, z_low, bc_leaving = step(x_low, z_low, bc_leaving)
    z_sent = gradient_rows(normed_flat, z_low, 3, bf16)
    both_sent = jnp.concatenate(
        [gradient_rows(normed_flat, values, 2, bf16) for values in (x_low, z_low)], axis=0
    )
    input_leaving = input_terms(1 - core, z_low, x_low, dt_low, *matrices)
    x_low, z_low, x_passed, z_sent, both_sent, input_leaving, bc_arriving = step(
        x_low, z_low, x_passed, z_sent, both_sent, input_leaving, bc_arriving
    )

    x_middle = gradient_rows(normed_flat, x_low, 1, bf16, x_passed)
    x_got = across(x_middle, middle_bit)
    z_passed = swap(z_sent, "dp", last_bit)
    input_arriving = swap(input_leaving, "tensor", 1)
    bc_kept = bc_kept + bc_arriving
    bc_far = swap(bc_kept[1], "dp", PAIR)
    x_low, z_low, x_middle, bc_kept, arriving = step(x_low, z_low, x_middle, bc_kept, arriving)
    input_kept = input_terms(core, z_low, x_low, dt_low, *matrices)
    shared = shared + arriving.astype(f32)
    out_mine, out_leaving = middle_sum(gradient_rows(proj_later, scaled_low, 0, f32, out_kept), out_got)
    x_low, z_low, input_kept, z_passed, input_arriving, bc_far, shared, out_mine, out_leaving = step(
        x_low, z_low, input_kept, z_passed, input_arriving, bc_far, shared, out_mine, out_leaving
    )

    z_middle = gradient_rows(normed_flat, z_low, 1, bf16, z_passed)
    z_got = across(z_middle, middle_bit)
    both_kept = swap(both_sent, "dp", last_bit)
    bc_low_mine = (bc_kept[0] + bc_far).astype(bf16)
    bc_far = swap(bc_low_mine, "tensor", 2)
    x_low, z_low, z_middle, bc_low_mine = step(x_low, z_low, z_middle, bc_low_mine)
    input_kept, input_leaving = kept_and_sent(input_kept + input_arriving, tensor_at, 2, bf16)
    bc_far, input_kept, input_leaving = step(bc_far, input_kept, input_leaving)

    input_arriving = swap(input_leaving, "tensor", 2)
    bc_low = join_halves(bc_low_mine, bc_far, tensor_at // 2, 0)
    bc_far = swap(bc_low, "tensor", 1)
    dt_part = tokens_out(dt_low, normed_flat)[:head_count]
    bc_far, dt_part = step(bc_far, dt_part)

    bc_low = join_halves(bc_low, bc_far, core, 0)
    bc_columns = bc_low.shape[1] // 4
    bc_part = tokens_out(
        lax.dynamic_slice_in_dim(bc_low, tensor_at * bc_columns, bc_columns, 1), normed_low[0]
    )
    held = jnp.concatenate([bc_part, dt_part], axis=0)
    held = jnp.stack(
        [held[:, block * row_count : (block + 1) * row_count] for block in range(data_count)]
    )
    both_kept, held, x_got = step(both_kept, held, x_got)

    count = held.shape[0] // 2
    held = held[:count] + swap(held[count:], "dp", last_bit)
    out_far = across(out_leaving, PAIR)
    projected_far = across(low_bits(shared[1]), PAIR)
    x_terms = gradient_rows(normed_flat, x_low, 0, f32, both_kept[:part])
    z_terms = gradient_rows(normed_flat, z_low, 0, f32, both_kept[part:])
    x_mine, x_leaving = middle_sum(x_terms, x_got)
    input_arriving, held, z_terms, x_leaving, z_got, projected_far, out_far = step(
        input_arriving, held, z_terms, x_leaving, z_got, projected_far, out_far
    )

    input_mine = input_kept + input_arriving.astype(f32)
    input_far = swap(low_bits(input_mine[1]), "dp", PAIR)
    for bit in reversed(dp_bits()[1:-1]):
        count = held.shape[0] // 2
        held = held[:count] + swap(held[count:], "dp", bit)
    z_mine, z_leaving = middle_sum(z_terms, z_got)
    both_far = across(jnp.concatenate([x_leaving, z_leaving], axis=0), PAIR)
    projected_mine = shared[0] + flip_pairs(projected_far)
    output = from_relative((in_mine + inv_mine[:, None] * projected_mine).astype(bf16), data_at)
    output_far = swap(output, "tensor", 2)
    out_share = join_halves(out_mine, out_far, half, 1)
    input_far, held, out_share = step(input_far, held, out_share)

    small_far = swap(held[1], "dp", PAIR)
    normed_grad = (
        input_mine[0] + flip_pairs(input_far.astype(f32)) + rows_times(bc_low_mine, low_bc)
    )

    _, norm_pull = jax.vjp(norm_input, in_mine, gain_rel)
    block_grad, gain_slot = norm_pull(normed_grad)
    input_grad = from_relative((cot_mine + block_grad).astype(bf16), data_at)
    both_far, small_far, gain_slot, output_far = step(both_far, small_far, gain_slot, output_far)
    output = join_halves(output, output_far, tensor_at // 2, 0)
    output = join_halves(output, swap(output, "tensor", 1), core, 0)
    x_share = join_halves(x_mine, both_far[: x_mine.shape[0]], half, 1)
    z_share = join_halves(z_mine, both_far[x_mine.shape[0] :], half, 1)

    bc_share = held[0, :bc_columns] + small_far[:bc_columns]
    dt_share = join_halves(held[0, bc_columns:], small_far[bc_columns:], half, 0).T
    bc_share = join_halves(bc_share, swap(bc_share, "tensor", 1), core, 0)
    bc_share = join_halves(bc_share, swap(bc_share, "tensor", 2), tensor_at // 2, 0).T

    def in_half(values):
        return join_halves(values, jnp.zeros_like(values), half, values.ndim - 1)

    def packed_sum(pieces, axis_bits):
        sizes = [piece.size for piece in pieces]
        flat = jnp.concatenate([piece.reshape(-1) for piece in pieces])
        fill = -flat.size % 128
        flat = jnp.pad(flat, (0, fill)).reshape(-1, 128)
        for axis, bits in axis_bits:
            flat = add_over(flat, axis, bits)
        flat = flat.reshape(-1)
        result, at = [], 0
        for piece, size in zip(pieces, sizes):
            result.append(flat[at : at + size].reshape(piece.shape))
            at += size
        return result

    norm_sum, convbc_sum = packed_sum(
        [from_relative(gain_slot, data_at), convbc_part], [("tensor", (1, 2))]
    )
    z_share, bc_share, norm_sum, convbc_sum = step(z_share, bc_share, norm_sum, convbc_sum)
    z_square = z_share * z_share + tiny_eps
    x_square = x_share * x_share + tiny_eps
    bc_square = bc_share * bc_share + tiny_eps
    dt_square = dt_share * dt_share + tiny_eps
    out_square = out_share * out_share + tiny_eps
    row_sums = jnp.stack(
        [
            jnp.sum(z_square, axis=1),
            jnp.sum(x_square, axis=1),
            jnp.sum(dt_square, axis=1),
            jnp.sum(out_square, axis=1),
        ]
    )
    z_row_sum, x_row_sum, dt_row_sum, out_row_sum = add_over(row_sums, "tensor", (1, 2))
    bc_row_sum = jnp.sum(bc_square, axis=1)

    (
        norm_total,
        convbc_total,
        gated_total,
        convx_total,
        head_total,
        z_col_sum,
        x_col_sum,
        bc_col_sum,
        dt_col_sum,
        out_col_sum,
    ) = packed_sum(
        [
            norm_sum,
            convbc_sum,
            in_half(gated_slot),
            in_half(convx_slot),
            in_half(head_slot),
            jnp.sum(z_square, axis=0),
            jnp.sum(x_square, axis=0),
            jnp.sum(bc_square, axis=0),
            jnp.sum(dt_square, axis=0),
            jnp.sum(out_square, axis=0),
        ],
        [("dp", dp_bits())],
    )
    z_rows_new = mix_state(z_rows, z_row_sum / INNER)
    x_rows_new = mix_state(x_rows, x_row_sum / INNER)
    bc_rows_new = mix_state(bc_rows, bc_row_sum / (2 * STATE))
    dt_rows_new = mix_state(dt_rows, dt_row_sum / HEADS)
    out_rows_new = mix_state(out_rows, out_row_sum / INNER)
    z_cols_new = mix_state(z_cols, z_col_sum / D)
    x_cols_new = mix_state(x_cols, x_col_sum / D)
    bc_cols_new = mix_state(bc_cols, bc_col_sum / D)
    dt_cols_new = mix_state(dt_cols, dt_col_sum / D)
    out_cols_new = mix_state(out_cols, out_col_sum / D)
    norm_second = mix_state(norm_gain_sq, norm_total * norm_total + tiny_eps)
    gated_second = mix_state(gated_gain_sq, gated_total * gated_total + tiny_eps)
    convx_second = mix_state(conv_x_sq, convx_total * convx_total + tiny_eps)
    convbc_second = mix_state(conv_bc_sq, convbc_total * convbc_total + tiny_eps)
    head_second = mix_state(head_sq, head_total * head_total + tiny_eps)
    norm_unit = norm_total * lax.rsqrt(norm_second)
    gated_unit = gated_total * lax.rsqrt(gated_second)
    convx_unit = convx_total * lax.rsqrt(convx_second)
    convbc_unit = convbc_total * lax.rsqrt(convbc_second)
    head_unit = head_total * lax.rsqrt(head_second)
    z_unit = z_share * lax.rsqrt(z_rows_new[:, None] * z_cols_new[None, :])
    x_unit = x_share * lax.rsqrt(x_rows_new[:, None] * x_cols_new[None, :])
    bc_unit = bc_share * lax.rsqrt(bc_rows_new[:, None] * bc_cols_new[None, :])
    dt_unit = dt_share * lax.rsqrt(dt_rows_new[:, None] * dt_cols_new[None, :])
    out_unit = out_share * lax.rsqrt(out_rows_new[:, None] * out_cols_new[None, :])
    tensor_count = lax.axis_size("tensor")
    unit_sums = jnp.stack(
        [
            jnp.sum(z_unit * z_unit),
            jnp.sum(x_unit * x_unit),
            jnp.sum(bc_unit * bc_unit) / tensor_count,
            jnp.sum(dt_unit * dt_unit),
            jnp.sum(out_unit * out_unit),
            jnp.sum(gated_unit * gated_unit) / data_count,
            jnp.sum(convx_unit * convx_unit) / data_count,
            jnp.sum(head_unit * head_unit) / data_count,
        ]
    )
    unit_sums = jnp.broadcast_to(unit_sums[:, None], (8, 128))
    unit_sums = add_over(unit_sums, "tensor", (1, 2))
    unit_sums, input_grad, output = step(unit_sums, input_grad, output)
    input_far = swap(input_grad, "tensor", 2)
    unit_sums = add_over(unit_sums, "dp", dp_bits())
    input_far, unit_sums = step(input_far, unit_sums)
    input_grad = join_halves(input_grad, input_far, tensor_at // 2, 0)
    input_grad = join_halves(input_grad, swap(input_grad, "tensor", 1), core, 0)
    (
        z_total,
        x_total,
        bc_total_sq,
        dt_total,
        out_total,
        gated_sq_total,
        convx_sq_total,
        head_sq_total,
    ) = unit_sums[:, 0]
    norm_sq_total = jnp.sum(norm_unit * norm_unit)
    convbc_sq_total = jnp.sum(convbc_unit * convbc_unit)
    in_rate = D ** (-0.5)
    out_rate = INNER ** (-0.5)
    z_upd = -in_rate * normalized(z_unit, z_total, D * INNER)
    x_upd = -in_rate * normalized(x_unit, x_total, D * INNER)
    bc_upd = -in_rate * normalized(bc_unit, bc_total_sq, D * 2 * STATE)
    dt_upd = -in_rate * normalized(dt_unit, dt_total, D * HEADS)
    out_upd = -out_rate * normalized(out_unit, out_total, D * INNER)
    norm_upd = -vector_rate * normalized(norm_unit, norm_sq_total, D)
    gated_upd = -vector_rate * normalized(gated_unit, gated_sq_total, INNER)
    convx_upd = -vector_rate * normalized(convx_unit, convx_sq_total, KCONV * INNER)
    convbc_upd = -vector_rate * normalized(convbc_unit, convbc_sq_total, KCONV * 2 * STATE)
    head_upd = -vector_rate * normalized(head_unit, head_sq_total, 3 * HEADS)
    return (
        output[None],
        input_grad[None],
        norm_total,
        norm_upd,
        norm_second,
        z_share,
        z_upd,
        z_rows_new,
        z_cols_new,
        x_share,
        x_upd,
        x_rows_new,
        x_cols_new,
        bc_share,
        bc_upd,
        bc_rows_new,
        bc_cols_new,
        dt_share,
        dt_upd,
        dt_rows_new,
        dt_cols_new,
        convx_total,
        convx_upd,
        convx_second,
        convbc_total,
        convbc_upd,
        convbc_second,
        head_total,
        head_upd,
        head_second,
        gated_total,
        gated_upd,
        gated_second,
        out_share,
        out_upd,
        out_rows_new,
        out_cols_new,
    )


def solution(mesh):
    in_specs = (
        P("dp", None, None),
        P("dp", None, None),
        P("dp", None),
        P("dp"),
        P(),
        P("dp", "tensor"),
        P("dp", "tensor"),
        P("dp", None),
        P("dp", "tensor"),
        P(None, "tensor"),
        P(),
        P(None, "tensor"),
        P("tensor"),
        P("dp", "tensor"),
        P(),
        P("dp"),
        P("tensor"),
        P("dp"),
        P("tensor"),
        P("dp"),
        P(),
        P("dp"),
        P("tensor"),
        P(None, "tensor"),
        P(),
        P(None, "tensor"),
        P("tensor"),
        P("dp"),
        P("tensor"),
    )
    out_specs = (
        P("dp", None, None),
        P("dp", None, None),
        P(),
        P(),
        P(),
        P("dp", "tensor"),
        P("dp", "tensor"),
        P("dp"),
        P("tensor"),
        P("dp", "tensor"),
        P("dp", "tensor"),
        P("dp"),
        P("tensor"),
        P("dp", None),
        P("dp", None),
        P("dp"),
        P(),
        P("dp", "tensor"),
        P("dp", "tensor"),
        P("dp"),
        P("tensor"),
        P(None, "tensor"),
        P(None, "tensor"),
        P(None, "tensor"),
        P(),
        P(),
        P(),
        P(None, "tensor"),
        P(None, "tensor"),
        P(None, "tensor"),
        P("tensor"),
        P("tensor"),
        P("tensor"),
        P("dp", "tensor"),
        P("dp", "tensor"),
        P("dp"),
        P("tensor"),
    )
    return jax.shard_map(shards, mesh=mesh, in_specs=in_specs, out_specs=out_specs, check_vma=False)
```

time: 838 us -> 516 us (0.62)
  waiting for transfers between devices: 261 us -> 147 us
  other arithmetic: 187 us -> 99.3 us
  matrix products: 127 us -> 44.4 us
  local copies, waits for them, and re-layouts: 160 us -> 78.7 us
  Pallas kernels: 0 us -> 61.7 us
  starting transfers between devices: 75.9 us -> 61.9 us
    ppermute x72 -> x68, waiting for transfers between devices: 261 us -> 147 us  [swap(): lax.ppermute(value, axis, [(place, place ^ bit) for place in range(size)])]
    dot_general x29 -> x0, matrix products: 72.4 us -> none  [the longest x6 39.5 us: advance(): inside = jnp.einsum('hts,hps->hpt', mixing, block_x, precision=highest)]
    pallas_call x0 -> x5, Pallas kernels: none -> 61.7 us  [the longest x2 31.1 us: mixer_backward(): pl.pallas_call(body, grid=(1, pairs), in_specs=common_specs(slot, length)...]
    reshape x17 -> x2, local copies, waits for them, and re-layouts: 26 us -> 0.03 us  [shards(): small = rows_of(bc_mine.reshape(-1, 128), dt_rows_low.reshape(-1, 128))]
    another operation x19 -> x7, other arithmetic: 26.4 us -> 1.01 us
    slice x28 -> x19, local copies, waits for them, and re-layouts: 19.5 us -> 1.11 us  [the longest x1 0.84 us: shards(): small[:, bc_piece_rows:].reshape(data_count, dt_weight.shape[1], row_count)]
    mul x25 -> x0, other arithmetic: 17.6 us -> none  [the longest x6 5.13 us: causal_conv(): taps[offset] * shift_down(values, offset)]
    dot_general x5 -> x3, matrix products: 22 us -> 5.28 us  [rows_times(): lax.dot_general(left, right, (((1,), (1,)), ((), ())), preferred_element_...]
  transfers between devices with their start and end apart: 72 -> 68, of which waited for: 29 -> 28; matrix products, arithmetic and copies ran while one was open for 52% -> 36% of each run, Pallas kernels for 0% -> 12%
where the time goes in v2:
time: 516 us; the launch traced here: 507 us
  waiting for transfers between devices  147 us (28%)
  other arithmetic  99.3 us (19%)
  local copies, waits for them, and re-layouts  78.7 us (15%)
  starting transfers between devices  61.9 us (12%)
  Pallas kernels  61.7 us (12%)
  matrix products  44.4 us (9%)
  between operations  13.9 us (3%)
    ppermute x68, waiting for transfers between devices, swap(): lax.ppermute(value, axis, [(place, place ^ bit) for place in range(size)])  147 us
    ppermute x68, starting transfers between devices, swap(): lax.ppermute(value, axis, [(place, place ^ bit) for place in range(size)])  61.9 us
    unnamed x263, local copies, waits for them, and re-layouts  49.7 us
    pallas_call x2, Pallas kernels, mixer_backward(): pl.pallas_call(body, grid=(1, pairs), in_specs=common_specs(slot, length)...  31.1 us
    select_n x16, other arithmetic, join_halves(): jnp.where(half == 0, jnp.concatenate([mine, other], axis=axis), jnp.conca...  27 us
    dot_general x14, matrix products, tokens_out(): lax.dot_general(left, right, (((0,), (0,)), ((), ())), preferred_element_...  25.8 us
    pallas_call x1, Pallas kernels, mixer_forward(): pl.pallas_call(forward_body, grid=(slots, pairs), in_specs=common_specs(0...  16.5 us
    pallas_call x2, Pallas kernels, input_terms(): pl.pallas_call(input_body, grid_spec=pltpu.PrefetchScalarGridSpec(num_sca...  14.2 us
  transfers between devices with their start and end apart: 68, of which 28 were waited for; matrix products, arithmetic and copies ran while one was open for 36% of the time, Pallas kernels for 12%

profile of v2, /device:TPU:0, one launch (start us, length us, event | category | flops | bytes accessed | tf_op | source)
XLA Modules:
  0.0 507.2 jit_solution(1967277381134706818)
XLA Ops:
  3.0 3.1 collective-permute-start
  10.1 5.2 %collective-permute-done.1 = bf16[256,512]{1,0:T(8,128)(2,1)S(1)} collective-permute-done((bf16[256,512]{1,0:T(8,128)(2,1)S(1)}, bf16[256,512]{1,0:T(8,128)(2,1)S(1)}, u32[]{:S(2)}, u32[]{:S(2)}) %collective-permute-start.1) | collective-permute-done | bytes 262176 | tf_op jit(solution)/shard_map/ppermute | solution.py:551
  33.5 11.8 %collective-permute-done.4 = bf16[2,160,128]{2,1,0:T(8,128)(2,1)S(1)} collective-permute-done((bf16[2,160,128]{2,1,0:T(8,128)(2,1)S(1)}, bf16[2,160,128]{2,1,0:T(8,128)(2,1)S(1)}, u32[]{:S(2)}, u32[]{:S(2)}) %collective-permute-start.4) | collective-permute-done | bytes 81952 | tf_op jit(solution)/shard_map/ppermute | solution.py:551
  53.5 9.3 %collective-permute-done.6 = bf16[4,160,128]{2,1,0:T(8,128)(2,1)S(1)} collective-permute-done((bf16[4,160,128]{2,1,0:T(8,128)(2,1)S(1)}, bf16[4,160,128]{2,1,0:T(8,128)(2,1)S(1)}, u32[]{:S(2)}, u32[]{:S(2)}) %collective-permute-start.6) | collective-permute-done | bytes 163872 | tf_op jit(solution)/shard_map/ppermute | solution.py:551
  76.3 3.0 collective-permute-done.11
  81.8 14.7 %collective-permute-done.9 = bf16[512,512]{1,0:T(8,128)(2,1)S(1)} collective-permute-done((bf16[512,512]{1,0:T(8,128)(2,1)S(1)}, bf16[512,512]{1,0:T(8,128)(2,1)S(1)}, u32[]{:S(2)}, u32[]{:S(2)}) %collective-permute-start.9) | collective-permute-done | bytes 524320 | tf_op jit(solution)/shard_map/ppermute | solution.py:551
  107.7 4.6 collective-permute-done.17
  113.8 3.4 maximum_select_fusion
  124.4 3.6 fusion.13.x_ref.refs_6_
  129.4 3.7 fusion.11.z_ref.refs_7_
  138.9 6.8 %collective-permute-done.18 = bf16[128,2048]{1,0:T(8,128)(2,1)S(1)} collective-permute-done((bf16[128,2048]{1,0:T(8,128)(2,1)S(1)}, bf16[128,2048]{1,0:T(8,128)(2,1)S(1)}, u32[]{:S(2)}, u32[]{:S(2)}) %collective-permute-start.18) | collective-permute-done | bytes 524320 | tf_op jit(solution)/shard_map/ppermute | solution.py:551
  149.0 16.5 %mixer_forward.1 = (bf16[2,512,512]{2,1,0:T(8,128)(2,1)}, f32[2,512,512]{2,1,0:T(8,128)}, f32[2,512,128]{2,1,0:T(8,128)}) custom-call(f32[2,512,8]{2,1,0:T(8,128)} %copy.138.marks_ref.refs_0_, f32[2,8,512]{2,1,0:T(8,128)} %broadcast_in_dim.22.row_ref.refs_1_, f32[2,512,256]{2,1,0:T(8,128)} %fusion.137.bc_ref.refs_2_, f32[2,512,128]{2,1,0:T(8,128)} %fusion.62.dt_ref.refs_3_, ...), custom_call_target="tpu_custom_call" | custom-call | flops 16000000000 | bytes 1048576 | tf_op jit(solution)/shard_map/mixer_forward/pallas_call | solution.py:387
  171.4 3.1 maximum_select_fusion.1
  191.5 2.9 multiply_convert_fusion
  199.6 3.7 fusion.2.refs_10_
  204.4 15.7 %mixer_backward.2 = (bf16[2,512,512]{2,1,0:T(8,128)(2,1)}, bf16[2,512,512]{2,1,0:T(8,128)(2,1)}, f32[2,512,256]{2,1,0:T(8,128)}, f32[2,512,128]{2,1,0:T(8,128)},...) custom-call(f32[2,512,8]{2,1,0:T(8,128)} %copy.138.marks_ref.refs_0_, ...), custom_call_target="tpu_custom_call" | custom-call | flops 16000000000 | bytes 1048576 | tf_op jit(solution)/shard_map/mixer_backward/pallas_call | solution.py:412
  220.1 3.2 fusion.18
  223.3 3.4 convert_add_fusion
  232.4 15.4 %mixer_backward.3 = (bf16[2,512,512]{2,1,0:T(8,128)(2,1)}, bf16[2,512,512]{2,1,0:T(8,128)(2,1)}, f32[2,512,256]{2,1,0:T(8,128)}, f32[2,512,128]{2,1,0:T(8,128)},...) custom-call(f32[2,512,8]{2,1,0:T(8,128)} %copy.138.marks_ref.refs_0_, ...), custom_call_target="tpu_custom_call", output_to_operand_aliasing={{0}: (12, {}), {1}: (13, {}), {2}: (14, {}), {3}: (15, {}),... | custom-call | flops 16000000000 | bytes 1048576 | tf_op jit(solution)/shard_map/mixer_backward/pallas_call | solution.py:412
  247.8 6.2 %collective-permute-done.28 = bf16[512,512]{1,0:T(8,128)(2,1)} collective-permute-done((bf16[512,512]{1,0:T(8,128)(2,1)}, bf16[512,512]{1,0:T(8,128)(2,1)}, u32[]{:S(2)}, u32[]{:S(2)}) %collective-permute-start.28) | collective-permute-done | bytes 524320 | tf_op jit(solution)/shard_map/ppermute | solution.py:551
  270.1 7.0 %input_terms.2 = f32[2,256,2048]{2,1,0:T(8,128)} custom-call(s32[1]{0:T(128)} %bitcast.60.place_ref, bf16[2,2,256,512]{3,2,1,0:T(8,128)(2,1)} %bitcast.383, bf16[2,2,256,512]{3,2,1,0:T(8,128)(2,1)} %bitcast.390, bf16[2,2,256,128]{3,2,1,0:T(8,128)(2,1)} %bitcast.331, bf16[2048,512]{1,0:T(8,128)(2,1)} %copy-done.53, ...), custom_call_target="tpu_custom_call" | custom-call | flops 6000000000 | bytes 1048576 | tf_op jit(solution)/shard_map/input_terms/pallas_call | solution.py:480
  290.9 3.2 fusion.19
  300.0 7.2 %input_terms.3 = f32[2,256,2048]{2,1,0:T(8,128)} custom-call(s32[1]{0:T(128)} %bitcast.65.place_ref, bf16[2,2,256,512]{3,2,1,0:T(8,128)(2,1)} %bitcast.384, bf16[2,2,256,512]{3,2,1,0:T(8,128)(2,1)} %bitcast.392, bf16[2,2,256,128]{3,2,1,0:T(8,128)(2,1)} %bitcast.332, bf16[2048,512]{1,0:T(8,128)(2,1)} %copy-done.53, ...), custom_call_target="tpu_custom_call" | custom-call | flops 6000000000 | bytes 1048576 | tf_op jit(solution)/shard_map/input_terms/pallas_call | solution.py:480
  309.5 10.8 %collective-permute-done.41 = bf16[512,512]{1,0:T(8,128)(2,1)S(1)} collective-permute-done((bf16[512,512]{1,0:T(8,128)(2,1)}, bf16[512,512]{1,0:T(8,128)(2,1)S(1)}, u32[]{:S(2)}, u32[]{:S(2)}) %collective-permute-start.41) | collective-permute-done | bytes 524320 | tf_op jit(solution)/shard_map/ppermute | solution.py:551
  321.3 3.0 add.792
  338.6 22.5 %collective-permute-done.45 = bf16[256,512]{1,0:T(8,128)(2,1)S(1)} collective-permute-done((bf16[256,512]{1,0:T(8,128)(2,1)S(1)}, bf16[256,512]{1,0:T(8,128)(2,1)S(1)}, u32[]{:S(2)}, u32[]{:S(2)}) %collective-permute-start.45) | collective-permute-done | bytes 262176 | tf_op jit(solution)/shard_map/ppermute | solution.py:551
  366.0 21.2 %collective-permute-done.48 = f32[2,72,256]{2,1,0:T(8,128)S(1)} collective-permute-done((f32[2,72,256]{2,1,0:T(8,128)S(1)}, f32[2,72,256]{2,1,0:T(8,128)S(1)}, u32[]{:S(2)}, u32[]{:S(2)}) %collective-permute-start.48) | collective-permute-done | bytes 147488 | tf_op jit(solution)/shard_map/ppermute | solution.py:551
  400.1 6.7 %collective-permute-done.50 = bf16[128,2048]{1,0:T(8,128)(2,1)S(1)} collective-permute-done((bf16[128,2048]{1,0:T(8,128)(2,1)S(1)}, bf16[128,2048]{1,0:T(8,128)(2,1)S(1)}, u32[]{:S(2)}, u32[]{:S(2)}) %collective-permute-start.50) | collective-permute-done | bytes 524320 | tf_op jit(solution)/shard_map/ppermute | solution.py:551
  415.0 3.8 collective-permute-done.52
  462.7 4.6 maximum_select_fusion.2
  481.4 3.1 maximum_select_fusion.11
  502.2 4.6 maximum_select_fusion.3
  (641 shorter events, 256.1 us)
Async XLA Ops:
  17.0 28.4 %collective-permute-start.2 = (bf16[512,512]{1,0:T(8,128)(2,1)}, bf16[512,512]{1,0:T(8,128)(2,1)}, u32[]{:S(2)}, u32[]{:S(2)}) collective-permute-start(bf16[512,512]{1,0:T(8,128)(2,1)} %get-tuple-element.617), channel_id=1, source_target_pairs={{0,16},{4,20},{8,24},{12,28},{16,0},{20,4},{24,8},{28,12},{1,17},{... | collective-permute-start | bytes 1572872 | tf_op jit(solution)/shard_map/ppermute | solution.py:551
  19.6 25.8 %collective-permute-start.3 = (bf16[512,512]{1,0:T(8,128)(2,1)}, bf16[512,512]{1,0:T(8,128)(2,1)}, u32[]{:S(2)}, u32[]{:S(2)}) collective-permute-start(bf16[512,512]{1,0:T(8,128)(2,1)} %get-tuple-element.617), channel_id=1, source_target_pairs={{0,4},{4,0},{8,12},{12,8},{16,20},{20,16},{24,28},{28,24},{1,5},{5... | collective-permute-start | bytes 1572872 | tf_op jit(solution)/shard_map/ppermute | solution.py:551
  21.5 23.8 %collective-permute-start.4 = (bf16[2,160,128]{2,1,0:T(8,128)(2,1)S(1)}, bf16[2,160,128]{2,1,0:T(8,128)(2,1)S(1)}, u32[]{:S(2)}, u32[]{:S(2)}) collective-permute-start(bf16[2,160,128]{2,1,0:T(8,128)(2,1)S(1)} %pad_maximum_fusion.4), channel_id=1, source_target_pairs={{0,16},{4,20},{8,24},{12,28},{16,0},{20,4},{24,8},{28,12},{1,17},{... | collective-permute-start | bytes 245768 | tf_op jit(solution)/shard_map/ppermute | solution.py:551
  45.4 20.9 %collective-permute-start.5 = (bf16[512,512]{1,0:T(8,128)(2,1)}, bf16[512,512]{1,0:T(8,128)(2,1)}, u32[]{:S(2)}, u32[]{:S(2)}) collective-permute-start(bf16[512,512]{1,0:T(8,128)(2,1)} %collective-permute-done.2), channel_id=1, source_target_pairs={{0,4},{4,0},{8,12},{12,8},{16,20},{20,16},{24,28},{28,24},{1,5},{5... | collective-permute-start | bytes 1572872 | tf_op jit(solution)/shard_map/ppermute | solution.py:551
  46.8 19.5 %collective-permute-start.8 = (bf16[128,2048]{1,0:T(8,128)(2,1)}, bf16[128,2048]{1,0:T(8,128)(2,1)}, u32[]{:S(2)}, u32[]{:S(2)}) collective-permute-start(bf16[128,2048]{1,0:T(8,128)(2,1)} %get-tuple-element.199), channel_id=1, source_target_pairs={{0,8},{4,12},{8,0},{12,4},{16,24},{20,28},{24,16},{28,20},{1,9},{5... | collective-permute-start | bytes 1572872 | tf_op jit(solution)/shard_map/ppermute | solution.py:551
  70.3 26.2 %collective-permute-start.9 = (bf16[512,512]{1,0:T(8,128)(2,1)S(1)}, bf16[512,512]{1,0:T(8,128)(2,1)S(1)}, u32[]{:S(2)}, u32[]{:S(2)}) collective-permute-start(bf16[512,512]{1,0:T(8,128)(2,1)S(1)} %get-tuple-element.613), channel_id=1, source_target_pairs={{0,16},{4,20},{8,24},{12,28},{16,0},{20,4},{24,8},{28,12},{1,17},{... | collective-permute-start | bytes 1572872 | tf_op jit(solution)/shard_map/ppermute | solution.py:551
  70.8 25.7 %collective-permute-start.10 = (bf16[512,512]{1,0:T(8,128)(2,1)S(1)}, bf16[512,512]{1,0:T(8,128)(2,1)S(1)}, u32[]{:S(2)}, u32[]{:S(2)}) collective-permute-start(bf16[512,512]{1,0:T(8,128)(2,1)S(1)} %get-tuple-element.613), channel_id=1, source_target_pairs={{0,4},{4,0},{8,12},{12,8},{16,20},{20,16},{24,28},{28,24},{1,5},{5... | collective-permute-start | bytes 1572872 | tf_op jit(solution)/shard_map/ppermute | solution.py:551
  101.4 20.2 %collective-permute-start.13 = (bf16[512,512]{1,0:T(8,128)(2,1)}, bf16[512,512]{1,0:T(8,128)(2,1)S(1)}, u32[]{:S(2)}, u32[]{:S(2)}) collective-permute-start(bf16[512,512]{1,0:T(8,128)(2,1)} %copy-done.39), channel_id=1, source_target_pairs={{0,4},{4,0},{8,12},{12,8},{16,20},{20,16},{24,28},{28,24},{1,5},{5... | collective-permute-start | bytes 1572872 | tf_op jit(solution)/shard_map/ppermute | solution.py:551
  101.9 19.7 %collective-permute-start.14 = (bf16[256,512]{1,0:T(8,128)(2,1)}, bf16[256,512]{1,0:T(8,128)(2,1)S(1)}, u32[]{:S(2)}, u32[]{:S(2)}) collective-permute-start(bf16[256,512]{1,0:T(8,128)(2,1)} %get-tuple-element.212), channel_id=1, source_target_pairs={{0,8},{4,12},{8,0},{12,4},{16,24},{20,28},{24,16},{28,20},{1,9},{5... | collective-permute-start | bytes 786440 | tf_op jit(solution)/shard_map/ppermute | solution.py:551
  101.9 19.8 %collective-permute-start.15 = (bf16[128,2048]{1,0:T(8,128)(2,1)}, bf16[128,2048]{1,0:T(8,128)(2,1)S(1)}, u32[]{:S(2)}, u32[]{:S(2)}) collective-permute-start(bf16[128,2048]{1,0:T(8,128)(2,1)} %get-tuple-element.213), channel_id=1, source_target_pairs={{0,8},{4,12},{8,0},{12,4},{16,24},{20,28},{24,16},{28,20},{1,9},{5... | collective-permute-start | bytes 1572872 | tf_op jit(solution)/shard_map/ppermute | solution.py:551
  122.6 25.2 %collective-permute-start.20 = (bf16[512,512]{1,0:T(8,128)(2,1)}, bf16[512,512]{1,0:T(8,128)(2,1)S(1)}, u32[]{:S(2)}, u32[]{:S(2)}) collective-permute-start(bf16[512,512]{1,0:T(8,128)(2,1)} %get-tuple-element.608), channel_id=1, source_target_pairs={{0,16},{4,20},{8,24},{12,28},{16,0},{20,4},{24,8},{28,12},{1,17},{... | collective-permute-start | bytes 1572872 | tf_op jit(solution)/shard_map/ppermute | solution.py:551
  123.3 44.3 %collective-permute-start.21 = (bf16[512,512]{1,0:T(8,128)(2,1)}, bf16[512,512]{1,0:T(8,128)(2,1)}, u32[]{:S(2)}, u32[]{:S(2)}) collective-permute-start(bf16[512,512]{1,0:T(8,128)(2,1)} %get-tuple-element.608), channel_id=1, source_target_pairs={{0,4},{4,0},{8,12},{12,8},{16,20},{20,16},{24,28},{28,24},{1,5},{5... | collective-permute-start | bytes 1572872 | tf_op jit(solution)/shard_map/ppermute | solution.py:551
  146.9 24.6 %collective-permute-start.19 = (bf16[256,2048]{1,0:T(8,128)(2,1)}, bf16[256,2048]{1,0:T(8,128)(2,1)}, u32[]{:S(2)}, u32[]{:S(2)}) collective-permute-start(bf16[256,2048]{1,0:T(8,128)(2,1)} %maximum_select_fusion.6), channel_id=1, source_target_pairs={{0,1},{1,0},{2,3},{3,2},{4,5},{5,4},{6,7},{7,6},{8,9},{9,8},{10,11... | collective-permute-start | bytes 3145736 | tf_op jit(solution)/shard_map/ppermute | solution.py:551
  147.8 21.8 %collective-permute-start.22 = (bf16[512,512]{1,0:T(8,128)(2,1)S(1)}, bf16[512,512]{1,0:T(8,128)(2,1)}, u32[]{:S(2)}, u32[]{:S(2)}) collective-permute-start(bf16[512,512]{1,0:T(8,128)(2,1)S(1)} %collective-permute-done.20), channel_id=1, source_target_pairs={{0,4},{4,0},{8,12},{12,8},{16,20},{20,16},{24,28},{28,24},{1,5},{5... | collective-permute-start | bytes 1572872 | tf_op jit(solution)/shard_map/ppermute | solution.py:551
  196.0 24.0 %collective-permute-start.27 = (bf16[512,512]{1,0:T(8,128)(2,1)}, bf16[512,512]{1,0:T(8,128)(2,1)}, u32[]{:S(2)}, u32[]{:S(2)}) collective-permute-start(bf16[512,512]{1,0:T(8,128)(2,1)} %convolution_convert_fusion.5), channel_id=1, source_target_pairs={{0,4},{4,0},{8,12},{12,8},{16,20},{20,16},{24,28},{28,24},{1,5},{5... | collective-permute-start | bytes 1572872 | tf_op jit(solution)/shard_map/ppermute | solution.py:551
  198.4 57.7 %collective-permute-start.29 = (bf16[512,512]{1,0:T(8,128)(2,1)}, bf16[512,512]{1,0:T(8,128)(2,1)S(1)}, u32[]{:S(2)}, u32[]{:S(2)}) collective-permute-start(bf16[512,512]{1,0:T(8,128)(2,1)} %convolution_convert_fusion.4), channel_id=1, source_target_pairs={{0,4},{4,0},{8,12},{12,8},{16,20},{20,16},{24,28},{28,24},{1,5},{5... | collective-permute-start | bytes 1572872 | tf_op jit(solution)/shard_map/ppermute | solution.py:551
  229.9 24.1 %collective-permute-start.28 = (bf16[512,512]{1,0:T(8,128)(2,1)}, bf16[512,512]{1,0:T(8,128)(2,1)}, u32[]{:S(2)}, u32[]{:S(2)}) collective-permute-start(bf16[512,512]{1,0:T(8,128)(2,1)} %fusion.18), channel_id=1, source_target_pairs={{0,16},{4,20},{8,24},{12,28},{16,0},{20,4},{24,8},{28,12},{1,17},{... | collective-permute-start | bytes 1572872 | tf_op jit(solution)/shard_map/ppermute | solution.py:551
  231.4 24.7 %collective-permute-start.30 = (bf16[2,128,2048]{2,1,0:T(8,128)(2,1)}, bf16[2,128,2048]{2,1,0:T(8,128)(2,1)}, u32[]{:S(2)}, u32[]{:S(2)}) collective-permute-start(bf16[2,128,2048]{2,1,0:T(8,128)(2,1)} %dynamic-slice_convert_fusion.2), channel_id=1, source_target_pairs={{0,2},{1,3},{2,0},{3,1},{4,6},{5,7},{6,4},{7,5},{8,10},{9,11},{10,... | collective-permute-start | bytes 3145736 | tf_op jit(solution)/shard_map/ppermute | solution.py:551
  283.1 37.3 %collective-permute-start.35 = (f32[2,256,2048]{2,1,0:T(8,128)}, f32[2,256,2048]{2,1,0:T(8,128)}, u32[]{:S(2)}, u32[]{:S(2)}) collective-permute-start(f32[2,256,2048]{2,1,0:T(8,128)} %input_terms.2), channel_id=1, source_target_pairs={{0,1},{1,0},{2,3},{3,2},{4,5},{5,4},{6,7},{7,6},{8,9},{9,8},{10,11... | collective-permute-start | bytes 12582920 | tf_op jit(solution)/shard_map/ppermute | solution.py:551
  294.2 26.1 %collective-permute-start.41 = (bf16[512,512]{1,0:T(8,128)(2,1)}, bf16[512,512]{1,0:T(8,128)(2,1)S(1)}, u32[]{:S(2)}, u32[]{:S(2)}) collective-permute-start(bf16[512,512]{1,0:T(8,128)(2,1)} %fusion.19), channel_id=1, source_target_pairs={{0,16},{4,20},{8,24},{12,28},{16,0},{20,4},{24,8},{28,12},{1,17},{... | collective-permute-start | bytes 1572872 | tf_op jit(solution)/shard_map/ppermute | solution.py:551
  295.2 25.3 %collective-permute-start.34 = (bf16[512,512]{1,0:T(8,128)(2,1)}, bf16[512,512]{1,0:T(8,128)(2,1)}, u32[]{:S(2)}, u32[]{:S(2)}) collective-permute-start(bf16[512,512]{1,0:T(8,128)(2,1)} %convolution_convert_fusion.2), channel_id=1, source_target_pairs={{0,4},{4,0},{8,12},{12,8},{16,20},{20,16},{24,28},{28,24},{1,5},{5... | collective-permute-start | bytes 1572872 | tf_op jit(solution)/shard_map/ppermute | solution.py:551
  296.6 23.8 %collective-permute-start.36 = (f32[128,256]{1,0:T(8,128)S(1)}, f32[128,256]{1,0:T(8,128)S(1)}, u32[]{:S(2)}, u32[]{:S(2)}) collective-permute-start(f32[128,256]{1,0:T(8,128)S(1)} %slice_bitcast_fusion.1), channel_id=1, source_target_pairs={{0,8},{4,12},{8,0},{12,4},{16,24},{20,28},{24,16},{28,20},{1,9},{5... | collective-permute-start | bytes 393224 | tf_op jit(solution)/shard_map/ppermute | solution.py:551
  298.9 35.5 %collective-permute-start.39 = (bf16[1024,512]{1,0:T(8,128)(2,1)S(1)}, bf16[1024,512]{1,0:T(8,128)(2,1)}, u32[]{:S(2)}, u32[]{:S(2)}) collective-permute-start(bf16[1024,512]{1,0:T(8,128)(2,1)S(1)} %copy-done.33), channel_id=1, source_target_pairs={{0,4},{4,0},{8,12},{12,8},{16,20},{20,16},{24,28},{28,24},{1,5},{5... | collective-permute-start | bytes 3145736 | tf_op jit(solution)/shard_map/ppermute | solution.py:551
  328.3 32.9 %collective-permute-start.43 = (bf16[512,512]{1,0:T(8,128)(2,1)S(1)}, bf16[512,512]{1,0:T(8,128)(2,1)S(1)}, u32[]{:S(2)}, u32[]{:S(2)}) collective-permute-start(bf16[512,512]{1,0:T(8,128)(2,1)S(1)} %fusion.20), channel_id=1, source_target_pairs={{0,16},{4,20},{8,24},{12,28},{16,0},{20,4},{24,8},{28,12},{1,17},{... | collective-permute-start | bytes 1572872 | tf_op jit(solution)/shard_map/ppermute | solution.py:551
  330.3 31.1 %collective-permute-start.44 = (bf16[128,2048]{1,0:T(8,128)(2,1)S(1)}, bf16[128,2048]{1,0:T(8,128)(2,1)S(1)}, u32[]{:S(2)}, u32[]{:S(2)}) collective-permute-start(bf16[128,2048]{1,0:T(8,128)(2,1)S(1)} %fusion.60), channel_id=1, source_target_pairs={{0,8},{4,12},{8,0},{12,4},{16,24},{20,28},{24,16},{28,20},{1,9},{5... | collective-permute-start | bytes 1572872 | tf_op jit(solution)/shard_map/ppermute | solution.py:551
  331.8 29.3 %collective-permute-start.45 = (bf16[256,512]{1,0:T(8,128)(2,1)S(1)}, bf16[256,512]{1,0:T(8,128)(2,1)S(1)}, u32[]{:S(2)}, u32[]{:S(2)}) collective-permute-start(bf16[256,512]{1,0:T(8,128)(2,1)S(1)} %slice.728), channel_id=1, source_target_pairs={{0,8},{4,12},{8,0},{12,4},{16,24},{20,28},{24,16},{28,20},{1,9},{5... | collective-permute-start | bytes 786440 | tf_op jit(solution)/shard_map/ppermute | solution.py:551
  332.4 29.1 %collective-permute-start.38 = (bf16[2,128,2048]{2,1,0:T(8,128)(2,1)S(1)}, bf16[2,128,2048]{2,1,0:T(8,128)(2,1)S(1)}, u32[]{:S(2)}, u32[]{:S(2)}) collective-permute-start(bf16[2,128,2048]{2,1,0:T(8,128)(2,1)S(1)} %dynamic-slice_convert_fusion.1), channel_id=1, source_target_pairs={{0,2},{1,3},{2,0},{3,1},{4,6},{5,7},{6,4},{7,5},{8,10},{9,11},{10,... | collective-permute-start | bytes 3145736 | tf_op jit(solution)/shard_map/ppermute | solution.py:551
  335.8 25.3 %collective-permute-start.42 = (f32[4,72,256]{2,1,0:T(8,128)S(1)}, f32[4,72,256]{2,1,0:T(8,128)S(1)}, u32[]{:S(2)}, u32[]{:S(2)}) collective-permute-start(f32[4,72,256]{2,1,0:T(8,128)S(1)} %slice.363), channel_id=1, source_target_pairs={{0,4},{4,0},{8,12},{12,8},{16,20},{20,16},{24,28},{28,24},{1,5},{5... | collective-permute-start | bytes 884744 | tf_op jit(solution)/shard_map/ppermute | solution.py:551
  361.8 37.3 %collective-permute-start.46 = (bf16[512,512]{1,0:T(8,128)(2,1)S(1)}, bf16[512,512]{1,0:T(8,128)(2,1)S(1)}, u32[]{:S(2)}, u32[]{:S(2)}) collective-permute-start(bf16[512,512]{1,0:T(8,128)(2,1)S(1)} %pad_maximum_fusion.2), channel_id=1, source_target_pairs={{0,8},{4,12},{8,0},{12,4},{16,24},{20,28},{24,16},{28,20},{1,9},{5... | collective-permute-start | bytes 1572872 | tf_op jit(solution)/shard_map/ppermute | solution.py:551
  362.7 26.6 %collective-permute-start.47 = (bf16[128,2048]{1,0:T(8,128)(2,1)S(1)}, bf16[128,2048]{1,0:T(8,128)(2,1)S(1)}, u32[]{:S(2)}, u32[]{:S(2)}) collective-permute-start(bf16[128,2048]{1,0:T(8,128)(2,1)S(1)} %fusion.61), channel_id=1, source_target_pairs={{0,8},{4,12},{8,0},{12,4},{16,24},{20,28},{24,16},{28,20},{1,9},{5... | collective-permute-start | bytes 1572872 | tf_op jit(solution)/shard_map/ppermute | solution.py:551
  364.4 22.8 %collective-permute-start.48 = (f32[2,72,256]{2,1,0:T(8,128)S(1)}, f32[2,72,256]{2,1,0:T(8,128)S(1)}, u32[]{:S(2)}, u32[]{:S(2)}) collective-permute-start(f32[2,72,256]{2,1,0:T(8,128)S(1)} %slice.373), channel_id=1, source_target_pairs={{0,16},{4,20},{8,24},{12,28},{16,0},{20,4},{24,8},{28,12},{1,17},{... | collective-permute-start | bytes 442376 | tf_op jit(solution)/shard_map/ppermute | solution.py:551
  408.8 53.8 %collective-permute-start.62 = (bf16[256,2048]{1,0:T(8,128)(2,1)}, bf16[256,2048]{1,0:T(8,128)(2,1)}, u32[]{:S(2)}, u32[]{:S(2)}) collective-permute-start(bf16[256,2048]{1,0:T(8,128)(2,1)} %maximum_select_fusion.10), channel_id=1, source_target_pairs={{0,1},{1,0},{2,3},{3,2},{4,5},{5,4},{6,7},{7,6},{8,9},{9,8},{10,11... | collective-permute-start | bytes 3145736 | tf_op jit(solution)/shard_map/ppermute | solution.py:551
  (121 other events, 1743.6 us)

commit v3 on v2

--- a/solution.py
+++ b/solution.py
@@ -612,11 +612,8 @@
 
 
 def join_halves(mine, other, half, axis):
-    return jnp.where(
-        half == 0,
-        jnp.concatenate([mine, other], axis=axis),
-        jnp.concatenate([other, mine], axis=axis),
-    )
+    low, high = jnp.where(half == 0, mine, other), jnp.where(half == 0, other, mine)
+    return jnp.concatenate([low, high], axis=axis)
 
 
 def after(value, *others):
@@ -647,7 +644,7 @@
 
 
 def middle_sum(held, got):
-    held = held + got
+    held = held + got.astype(jnp.float32)
     for bit in reversed(dp_bits()[1:-2]):
         count = held.shape[0] // 2
         sent = swap(low_bits(held[count:]), "dp", bit)
@@ -853,7 +850,7 @@
     middle_bit = dp_bits()[-2]
 
     def across(value, bit):
-        return swap(value, "dp", bit).astype(f32)
+        return swap(value, "dp", bit)
 
     out_sent = [gradient_rows(proj_grad, scaled_low, place, bf16) for place in (3, 2)]
     out_passed, out_kept = [swap(value, "dp", last_bit) for value in out_sent]
@@ -875,8 +872,8 @@
     z_both, x_both, bc_grad_part, dt_both, vector_terms, taps_bc_terms, head_terms = mixer_backward(
         common, scanned, *gradients, 1, backward
     )
-    x_both, z_both, bc_grad_part, out_got, out_kept, arriving = step(
-        x_both, z_both, bc_grad_part, out_got, out_kept, arriving
+    x_both, z_both, bc_grad_part, out_kept, arriving = step(
+        x_both, z_both, bc_grad_part, out_kept, arriving
     )
     vector_terms = jnp.sum(vector_terms, axis=0)
     convx_slot, gated_slot = vector_terms[:4], vector_terms[4]
@@ -894,7 +891,7 @@
     dt_low = dt_both.astype(bf16).reshape(tokens, -1)
     matrices = (low_z, low_x, low_dt)
     x_sent = gradient_rows(normed_flat, x_low, 3, bf16)
-    x_low, z_low, x_sent, bc_arriving = step(x_low, z_low, x_sent, bc_arriving)
+    x_low, z_low, x_sent, bc_arriving, out_got = step(x_low, z_low, x_sent, bc_arriving, out_got)
 
     x_passed = swap(x_sent, "dp", last_bit)
     bc_kept, bc_leaving = kept_and_sent(bc_kept + bc_arriving, tensor_at, 2, f32)
@@ -916,11 +913,17 @@
     bc_kept = bc_kept + bc_arriving
     bc_far = swap(bc_kept[1], "dp", PAIR)
     x_low, z_low, x_middle, bc_kept, arriving = step(x_low, z_low, x_middle, bc_kept, arriving)
+    shared = shared + arriving.astype(f32)
+    shared_leaving = low_bits(shared[1])
+    out_mine, out_leaving = middle_sum(gradient_rows(proj_later, scaled_low, 0, f32, out_kept), out_got)
+    x_low, z_low, bc_far, shared_leaving, out_mine, out_leaving = step(
+        x_low, z_low, bc_far, shared_leaving, out_mine, out_leaving
+    )
+    out_far = across(out_leaving, PAIR)
+    projected_far = across(shared_leaving, PAIR)
     input_kept = input_terms(core, z_low, x_low, dt_low, *matrices)
-    shared = shared + arriving.astype(f32)
-    out_mine, out_leaving = middle_sum(gradient_rows(proj_later, scaled_low, 0, f32, out_kept), out_got)
-    x_low, z_low, input_kept, z_passed, input_arriving, bc_far, shared, out_mine, out_leaving = step(
-        x_low, z_low, input_kept, z_passed, input_arriving, bc_far, shared, out_mine, out_leaving
+    x_low, z_low, input_kept, z_passed, input_arriving, out_far, projected_far, both_sent = step(
+        x_low, z_low, input_kept, z_passed, input_arriving, out_far, projected_far, both_sent
     )
 
     z_middle = gradient_rows(normed_flat, z_low, 1, bf16, z_passed)
@@ -947,33 +950,30 @@
     held = jnp.stack(
         [held[:, block * row_count : (block + 1) * row_count] for block in range(data_count)]
     )
-    both_kept, held, x_got = step(both_kept, held, x_got)
-
     count = held.shape[0] // 2
     held = held[:count] + swap(held[count:], "dp", last_bit)
-    out_far = across(out_leaving, PAIR)
-    projected_far = across(low_bits(shared[1]), PAIR)
+    projected_mine = shared[0] + flip_pairs(projected_far.astype(f32))
+    output = from_relative((in_mine + inv_mine[:, None] * projected_mine).astype(bf16), data_at)
+    output_far = swap(output, "tensor", 2)
+    out_share = join_halves(out_mine, out_far.astype(f32), half, 1)
+    x_got, held, output, out_share = step(x_got, held, output, out_share)
+    for bit in reversed(dp_bits()[1:-1]):
+        count = held.shape[0] // 2
+        held = held[:count] + swap(held[count:], "dp", bit)
     x_terms = gradient_rows(normed_flat, x_low, 0, f32, both_kept[:part])
     z_terms = gradient_rows(normed_flat, z_low, 0, f32, both_kept[part:])
     x_mine, x_leaving = middle_sum(x_terms, x_got)
-    input_arriving, held, z_terms, x_leaving, z_got, projected_far, out_far = step(
-        input_arriving, held, z_terms, x_leaving, z_got, projected_far, out_far
-    )
-
+    input_arriving, held, z_terms, x_leaving, z_got, output_far = step(
+        input_arriving, held, z_terms, x_leaving, z_got, output_far
+    )
+
+    small_far = swap(held[1], "dp", PAIR)
     input_mine = input_kept + input_arriving.astype(f32)
     input_far = swap(low_bits(input_mine[1]), "dp", PAIR)
-    for bit in reversed(dp_bits()[1:-1]):
-        count = held.shape[0] // 2
-        held = held[:count] + swap(held[count:], "dp", bit)
     z_mine, z_leaving = middle_sum(z_terms, z_got)
     both_far = across(jnp.concatenate([x_leaving, z_leaving], axis=0), PAIR)
-    projected_mine = shared[0] + flip_pairs(projected_far)
-    output = from_relative((in_mine + inv_mine[:, None] * projected_mine).astype(bf16), data_at)
-    output_far = swap(output, "tensor", 2)
-    out_share = join_halves(out_mine, out_far, half, 1)
-    input_far, held, out_share = step(input_far, held, out_share)
-
-    small_far = swap(held[1], "dp", PAIR)
+    input_far, small_far = step(input_far, small_far)
+    output = join_halves(output, output_far, tensor_at // 2, 0)
     normed_grad = (
         input_mine[0] + flip_pairs(input_far.astype(f32)) + rows_times(bc_low_mine, low_bc)
     )
@@ -981,11 +981,10 @@
     _, norm_pull = jax.vjp(norm_input, in_mine, gain_rel)
     block_grad, gain_slot = norm_pull(normed_grad)
     input_grad = from_relative((cot_mine + block_grad).astype(bf16), data_at)
-    both_far, small_far, gain_slot, output_far = step(both_far, small_far, gain_slot, output_far)
-    output = join_halves(output, output_far, tensor_at // 2, 0)
+    both_far, gain_slot, small_far, output = step(both_far, gain_slot, small_far, output)
     output = join_halves(output, swap(output, "tensor", 1), core, 0)
-    x_share = join_halves(x_mine, both_far[: x_mine.shape[0]], half, 1)
-    z_share = join_halves(z_mine, both_far[x_mine.shape[0] :], half, 1)
+    x_share = join_halves(x_mine, both_far[: x_mine.shape[0]].astype(f32), half, 1)
+    z_share = join_halves(z_mine, both_far[x_mine.shape[0] :].astype(f32), half, 1)
 
     bc_share = held[0, :bc_columns] + small_far[:bc_columns]
     dt_share = join_halves(held[0, bc_columns:], small_far[bc_columns:], half, 0).T

time: 516 us -> 516 us (level)
  waiting for transfers between devices: 147 us -> 168 us
  other arithmetic: 99.3 us -> 83.7 us
    ppermute x68, waiting for transfers between devices: 147 us -> 168 us  [swap(): lax.ppermute(value, axis, [(place, place ^ bit) for place in range(size)])]
    select_n x16 -> x19, other arithmetic: 27 us -> 12.3 us  [the longest x18 12.3 us: join_halves(): jnp.where(half == 0, mine, other)]
    concatenate x1 -> x12, other arithmetic: 0.01 us -> 6.44 us  [join_halves(): return jnp.concatenate([low, high], axis=axis)]
    unnamed x263 -> x292, local copies, waits for them, and re-layouts: 49.7 us -> 51.8 us
  transfers between devices with their start and end apart: 68 -> 68, of which waited for: 28 -> 31; matrix products, arithmetic and copies ran while one was open for 36% -> 33% of each run, Pallas kernels for 12% -> 12%
where the time goes in v3:
time: 516 us; the launch traced here: 508 us
  waiting for transfers between devices  168 us (33%)
  other arithmetic  83.7 us (16%)
  local copies, waits for them, and re-layouts  78.2 us (15%)
  Pallas kernels  61.7 us (12%)
  starting transfers between devices  58.9 us (11%)
  matrix products  43.8 us (8%)
  between operations  13.7 us (3%)
    ppermute x68, waiting for transfers between devices, swap(): lax.ppermute(value, axis, [(place, place ^ bit) for place in range(size)])  168 us
    ppermute x68, starting transfers between devices, swap(): lax.ppermute(value, axis, [(place, place ^ bit) for place in range(size)])  58.9 us
    unnamed x292, local copies, waits for them, and re-layouts  51.8 us
    pallas_call x2, Pallas kernels, mixer_backward(): pl.pallas_call(body, grid=(1, pairs), in_specs=common_specs(slot, length)...  31 us
    dot_general x14, matrix products, tokens_out(): lax.dot_general(left, right, (((0,), (0,)), ((), ())), preferred_element_...  25.2 us
    pallas_call x1, Pallas kernels, mixer_forward(): pl.pallas_call(forward_body, grid=(slots, pairs), in_specs=common_specs(0...  16.5 us
    pallas_call x2, Pallas kernels, input_terms(): pl.pallas_call(input_body, grid_spec=pltpu.PrefetchScalarGridSpec(num_sca...  14.2 us
    select_n x18, other arithmetic, join_halves(): jnp.where(half == 0, mine, other)  12.3 us
  transfers between devices with their start and end apart: 68, of which 31 were waited for; matrix products, arithmetic and copies ran while one was open for 33% of the time, Pallas kernels for 12%

profile of v3, /device:TPU:0, one launch (start us, length us, event | category | flops | bytes accessed | tf_op | source)
XLA Modules:
  0.0 508.0 jit_solution(12343220892193577592)
XLA Ops:
  3.0 3.1 collective-permute-start
  10.1 5.2 %collective-permute-done.1 = bf16[256,512]{1,0:T(8,128)(2,1)S(1)} collective-permute-done((bf16[256,512]{1,0:T(8,128)(2,1)S(1)}, bf16[256,512]{1,0:T(8,128)(2,1)S(1)}, u32[]{:S(2)}, u32[]{:S(2)}) %collective-permute-start.1) | collective-permute-done | bytes 262176 | tf_op jit(solution)/shard_map/ppermute | solution.py:551
  34.0 4.1 convert_element_type.226
  40.3 5.1 collective-permute-done.4
  53.5 9.4 %collective-permute-done.6 = bf16[4,160,128]{2,1,0:T(8,128)(2,1)S(1)} collective-permute-done((bf16[4,160,128]{2,1,0:T(8,128)(2,1)S(1)}, bf16[4,160,128]{2,1,0:T(8,128)(2,1)S(1)}, u32[]{:S(2)}, u32[]{:S(2)}) %collective-permute-start.6) | collective-permute-done | bytes 163872 | tf_op jit(solution)/shard_map/ppermute | solution.py:551
  73.3 8.3 %collective-permute-done.11 = bf16[128,2048]{1,0:T(8,128)(2,1)S(1)} collective-permute-done((bf16[128,2048]{1,0:T(8,128)(2,1)}, bf16[128,2048]{1,0:T(8,128)(2,1)S(1)}, u32[]{:S(2)}, u32[]{:S(2)}) %collective-permute-start.11) | collective-permute-done | bytes 524320 | tf_op jit(solution)/shard_map/ppermute | solution.py:551
  83.8 12.4 %collective-permute-done.9 = bf16[512,512]{1,0:T(8,128)(2,1)S(1)} collective-permute-done((bf16[512,512]{1,0:T(8,128)(2,1)S(1)}, bf16[512,512]{1,0:T(8,128)(2,1)S(1)}, u32[]{:S(2)}, u32[]{:S(2)}) %collective-permute-start.9) | collective-permute-done | bytes 524320 | tf_op jit(solution)/shard_map/ppermute | solution.py:551
  107.5 3.9 collective-permute-done.17
  124.1 3.7 fusion.13.x_ref.refs_6_
  127.8 3.7 fusion.11.z_ref.refs_7_
  137.3 6.7 %collective-permute-done.18 = bf16[128,2048]{1,0:T(8,128)(2,1)S(1)} collective-permute-done((bf16[128,2048]{1,0:T(8,128)(2,1)S(1)}, bf16[128,2048]{1,0:T(8,128)(2,1)S(1)}, u32[]{:S(2)}, u32[]{:S(2)}) %collective-permute-start.18) | collective-permute-done | bytes 524320 | tf_op jit(solution)/shard_map/ppermute | solution.py:551
  148.8 16.5 %mixer_forward.1 = (bf16[2,512,512]{2,1,0:T(8,128)(2,1)}, f32[2,512,512]{2,1,0:T(8,128)}, f32[2,512,128]{2,1,0:T(8,128)}) custom-call(f32[2,512,8]{2,1,0:T(8,128)} %copy.138.marks_ref.refs_0_, f32[2,8,512]{2,1,0:T(8,128)} %broadcast_in_dim.28.row_ref.refs_1_, f32[2,512,256]{2,1,0:T(8,128)} %fusion.140.bc_ref.refs_2_, f32[2,512,128]{2,1,0:T(8,128)} %fusion.63.dt_ref.refs_3_, ...), custom_call_target="tpu_custom_call" | custom-call | flops 16000000000 | bytes 1048576 | tf_op jit(solution)/shard_map/mixer_forward/pallas_call | solution.py:387
  189.8 2.9 multiply_convert_fusion
  198.0 3.7 fusion.2.refs_10_
  202.7 15.6 %mixer_backward.2 = (bf16[2,512,512]{2,1,0:T(8,128)(2,1)}, bf16[2,512,512]{2,1,0:T(8,128)(2,1)}, f32[2,512,256]{2,1,0:T(8,128)}, f32[2,512,128]{2,1,0:T(8,128)},...) custom-call(f32[2,512,8]{2,1,0:T(8,128)} %copy.138.marks_ref.refs_0_, ...), custom_call_target="tpu_custom_call" | custom-call | flops 16000000000 | bytes 1048576 | tf_op jit(solution)/shard_map/mixer_backward/pallas_call | solution.py:412
  218.3 2.9 fusion.18
  221.3 3.4 convert_add_fusion
  229.1 15.4 %mixer_backward.3 = (bf16[2,512,512]{2,1,0:T(8,128)(2,1)}, bf16[2,512,512]{2,1,0:T(8,128)(2,1)}, f32[2,512,256]{2,1,0:T(8,128)}, f32[2,512,128]{2,1,0:T(8,128)},...) custom-call(f32[2,512,8]{2,1,0:T(8,128)} %copy.138.marks_ref.refs_0_, ...), custom_call_target="tpu_custom_call", output_to_operand_aliasing={{0}: (12, {}), {1}: (13, {}), {2}: (14, {}), {3}: (15, {}),... | custom-call | flops 16000000000 | bytes 1048576 | tf_op jit(solution)/shard_map/mixer_backward/pallas_call | solution.py:412
  244.5 4.9 collective-permute-done.29
  261.6 7.1 %input_terms.2 = f32[2,256,2048]{2,1,0:T(8,128)} custom-call(s32[1]{0:T(128)} %bitcast.59.place_ref, bf16[2,2,256,512]{3,2,1,0:T(8,128)(2,1)} %bitcast.372, bf16[2,2,256,512]{3,2,1,0:T(8,128)(2,1)} %bitcast.378, bf16[2,2,256,128]{3,2,1,0:T(8,128)(2,1)} %bitcast.319, bf16[2048,512]{1,0:T(8,128)(2,1)} %copy-done.60, ...), custom_call_target="tpu_custom_call" | custom-call | flops 6000000000 | bytes 1048576 | tf_op jit(solution)/shard_map/input_terms/pallas_call | solution.py:480
  279.7 3.0 fusion.19
  287.8 11.3 %collective-permute-done.34 = f32[128,256]{1,0:T(8,128)S(1)} collective-permute-done((f32[128,256]{1,0:T(8,128)S(1)}, f32[128,256]{1,0:T(8,128)S(1)}, u32[]{:S(2)}, u32[]{:S(2)}) %collective-permute-start.34) | collective-permute-done | bytes 131104 | tf_op jit(solution)/shard_map/ppermute | solution.py:551
  302.3 7.1 %input_terms.3 = f32[2,256,2048]{2,1,0:T(8,128)} custom-call(s32[1]{0:T(128)} %bitcast.66.place_ref, bf16[2,2,256,512]{3,2,1,0:T(8,128)(2,1)} %bitcast.373, bf16[2,2,256,512]{3,2,1,0:T(8,128)(2,1)} %bitcast.380, bf16[2,2,256,128]{3,2,1,0:T(8,128)(2,1)} %bitcast.320, bf16[2048,512]{1,0:T(8,128)(2,1)} %copy-done.60, ...), custom_call_target="tpu_custom_call" | custom-call | flops 6000000000 | bytes 1048576 | tf_op jit(solution)/shard_map/input_terms/pallas_call | solution.py:480
  310.4 4.8 collective-permute-done.38
  315.6 10.6 %collective-permute-done.39 = bf16[128,2048]{1,0:T(8,128)(2,1)S(1)} collective-permute-done((bf16[128,2048]{1,0:T(8,128)(2,1)}, bf16[128,2048]{1,0:T(8,128)(2,1)S(1)}, u32[]{:S(2)}, u32[]{:S(2)}) %collective-permute-start.39) | collective-permute-done | bytes 524320 | tf_op jit(solution)/shard_map/ppermute | solution.py:551
  326.2 4.3 add.780
  342.0 25.2 %collective-permute-done.43 = f32[4,72,256]{2,1,0:T(8,128)S(1)} collective-permute-done((f32[4,72,256]{2,1,0:T(8,128)S(1)}, f32[4,72,256]{2,1,0:T(8,128)S(1)}, u32[]{:S(2)}, u32[]{:S(2)}) %collective-permute-start.43) | collective-permute-done | bytes 294944 | tf_op jit(solution)/shard_map/ppermute | solution.py:551
  370.8 6.3 %collective-permute-done.44 = f32[2,72,256]{2,1,0:T(8,128)S(1)} collective-permute-done((f32[2,72,256]{2,1,0:T(8,128)S(1)}, f32[2,72,256]{2,1,0:T(8,128)S(1)}, u32[]{:S(2)}, u32[]{:S(2)}) %collective-permute-start.44) | collective-permute-done | bytes 147488 | tf_op jit(solution)/shard_map/ppermute | solution.py:551
  386.7 20.0 %collective-permute-done.50 = f32[72,256]{1,0:T(8,128)S(1)} collective-permute-done((f32[72,256]{1,0:T(8,128)S(1)}, f32[72,256]{1,0:T(8,128)S(1)}, u32[]{:S(2)}, u32[]{:S(2)}) %collective-permute-start.50) | collective-permute-done | bytes 73760 | tf_op jit(solution)/shard_map/ppermute | solution.py:551
  419.5 4.4 collective-permute-done.52
  435.7 3.0 collective-permute-done.58
  473.9 3.0 collective-permute-done.64
  (673 shorter events, 253.1 us)
Async XLA Ops:
  17.0 28.4 %collective-permute-start.2 = (bf16[512,512]{1,0:T(8,128)(2,1)}, bf16[512,512]{1,0:T(8,128)(2,1)}, u32[]{:S(2)}, u32[]{:S(2)}) collective-permute-start(bf16[512,512]{1,0:T(8,128)(2,1)} %get-tuple-element.663), channel_id=1, source_target_pairs={{0,16},{4,20},{8,24},{12,28},{16,0},{20,4},{24,8},{28,12},{1,17},{... | collective-permute-start | bytes 1572872 | tf_op jit(solution)/shard_map/ppermute | solution.py:551
  19.6 25.8 %collective-permute-start.3 = (bf16[512,512]{1,0:T(8,128)(2,1)}, bf16[512,512]{1,0:T(8,128)(2,1)}, u32[]{:S(2)}, u32[]{:S(2)}) collective-permute-start(bf16[512,512]{1,0:T(8,128)(2,1)} %get-tuple-element.663), channel_id=1, source_target_pairs={{0,4},{4,0},{8,12},{12,8},{16,20},{20,16},{24,28},{28,24},{1,5},{5... | collective-permute-start | bytes 1572872 | tf_op jit(solution)/shard_map/ppermute | solution.py:551
  22.1 23.3 %collective-permute-start.4 = (bf16[2,160,128]{2,1,0:T(8,128)(2,1)S(1)}, bf16[2,160,128]{2,1,0:T(8,128)(2,1)S(1)}, u32[]{:S(2)}, u32[]{:S(2)}) collective-permute-start(bf16[2,160,128]{2,1,0:T(8,128)(2,1)S(1)} %pad_maximum_fusion.17), channel_id=1, source_target_pairs={{0,16},{4,20},{8,24},{12,28},{16,0},{20,4},{24,8},{28,12},{1,17},{... | collective-permute-start | bytes 245768 | tf_op jit(solution)/shard_map/ppermute | solution.py:551
  45.4 20.9 %collective-permute-start.5 = (bf16[512,512]{1,0:T(8,128)(2,1)}, bf16[512,512]{1,0:T(8,128)(2,1)}, u32[]{:S(2)}, u32[]{:S(2)}) collective-permute-start(bf16[512,512]{1,0:T(8,128)(2,1)} %collective-permute-done.2), channel_id=1, source_target_pairs={{0,4},{4,0},{8,12},{12,8},{16,20},{20,16},{24,28},{28,24},{1,5},{5... | collective-permute-start | bytes 1572872 | tf_op jit(solution)/shard_map/ppermute | solution.py:551
  46.8 19.5 %collective-permute-start.8 = (bf16[128,2048]{1,0:T(8,128)(2,1)}, bf16[128,2048]{1,0:T(8,128)(2,1)}, u32[]{:S(2)}, u32[]{:S(2)}) collective-permute-start(bf16[128,2048]{1,0:T(8,128)(2,1)} %get-tuple-element.203), channel_id=1, source_target_pairs={{0,8},{4,12},{8,0},{12,4},{16,24},{20,28},{24,16},{28,20},{1,9},{5... | collective-permute-start | bytes 1572872 | tf_op jit(solution)/shard_map/ppermute | solution.py:551
  47.7 18.7 %collective-permute-start.7 = (bf16[256,512]{1,0:T(8,128)(2,1)}, bf16[256,512]{1,0:T(8,128)(2,1)}, u32[]{:S(2)}, u32[]{:S(2)}) collective-permute-start(bf16[256,512]{1,0:T(8,128)(2,1)} %get-tuple-element.202), channel_id=1, source_target_pairs={{0,8},{4,12},{8,0},{12,4},{16,24},{20,28},{24,16},{28,20},{1,9},{5... | collective-permute-start | bytes 786440 | tf_op jit(solution)/shard_map/ppermute | solution.py:551
  70.3 25.9 %collective-permute-start.9 = (bf16[512,512]{1,0:T(8,128)(2,1)S(1)}, bf16[512,512]{1,0:T(8,128)(2,1)S(1)}, u32[]{:S(2)}, u32[]{:S(2)}) collective-permute-start(bf16[512,512]{1,0:T(8,128)(2,1)S(1)} %get-tuple-element.659), channel_id=1, source_target_pairs={{0,16},{4,20},{8,24},{12,28},{16,0},{20,4},{24,8},{28,12},{1,17},{... | collective-permute-start | bytes 1572872 | tf_op jit(solution)/shard_map/ppermute | solution.py:551
  70.8 25.4 %collective-permute-start.10 = (bf16[512,512]{1,0:T(8,128)(2,1)S(1)}, bf16[512,512]{1,0:T(8,128)(2,1)S(1)}, u32[]{:S(2)}, u32[]{:S(2)}) collective-permute-start(bf16[512,512]{1,0:T(8,128)(2,1)S(1)} %get-tuple-element.659), channel_id=1, source_target_pairs={{0,4},{4,0},{8,12},{12,8},{16,20},{20,16},{24,28},{28,24},{1,5},{5... | collective-permute-start | bytes 1572872 | tf_op jit(solution)/shard_map/ppermute | solution.py:551
  101.3 17.9 %collective-permute-start.13 = (bf16[512,512]{1,0:T(8,128)(2,1)}, bf16[512,512]{1,0:T(8,128)(2,1)S(1)}, u32[]{:S(2)}, u32[]{:S(2)}) collective-permute-start(bf16[512,512]{1,0:T(8,128)(2,1)} %copy-done.45), channel_id=1, source_target_pairs={{0,4},{4,0},{8,12},{12,8},{16,20},{20,16},{24,28},{28,24},{1,5},{5... | collective-permute-start | bytes 1572872 | tf_op jit(solution)/shard_map/ppermute | solution.py:551
  101.8 17.4 %collective-permute-start.14 = (bf16[256,512]{1,0:T(8,128)(2,1)}, bf16[256,512]{1,0:T(8,128)(2,1)S(1)}, u32[]{:S(2)}, u32[]{:S(2)}) collective-permute-start(bf16[256,512]{1,0:T(8,128)(2,1)} %get-tuple-element.216), channel_id=1, source_target_pairs={{0,8},{4,12},{8,0},{12,4},{16,24},{20,28},{24,16},{28,20},{1,9},{5... | collective-permute-start | bytes 786440 | tf_op jit(solution)/shard_map/ppermute | solution.py:551
  101.8 19.4 %collective-permute-start.15 = (bf16[128,2048]{1,0:T(8,128)(2,1)}, bf16[128,2048]{1,0:T(8,128)(2,1)S(1)}, u32[]{:S(2)}, u32[]{:S(2)}) collective-permute-start(bf16[128,2048]{1,0:T(8,128)(2,1)} %get-tuple-element.217), channel_id=1, source_target_pairs={{0,8},{4,12},{8,0},{12,4},{16,24},{20,28},{24,16},{28,20},{1,9},{5... | collective-permute-start | bytes 1572872 | tf_op jit(solution)/shard_map/ppermute | solution.py:551
  122.0 25.2 %collective-permute-start.20 = (bf16[512,512]{1,0:T(8,128)(2,1)}, bf16[512,512]{1,0:T(8,128)(2,1)}, u32[]{:S(2)}, u32[]{:S(2)}) collective-permute-start(bf16[512,512]{1,0:T(8,128)(2,1)} %get-tuple-element.654), channel_id=1, source_target_pairs={{0,16},{4,20},{8,24},{12,28},{16,0},{20,4},{24,8},{28,12},{1,17},{... | collective-permute-start | bytes 1572872 | tf_op jit(solution)/shard_map/ppermute | solution.py:551
  122.6 45.9 %collective-permute-start.21 = (bf16[512,512]{1,0:T(8,128)(2,1)}, bf16[512,512]{1,0:T(8,128)(2,1)}, u32[]{:S(2)}, u32[]{:S(2)}) collective-permute-start(bf16[512,512]{1,0:T(8,128)(2,1)} %get-tuple-element.654), channel_id=1, source_target_pairs={{0,4},{4,0},{8,12},{12,8},{16,20},{20,16},{24,28},{28,24},{1,5},{5... | collective-permute-start | bytes 1572872 | tf_op jit(solution)/shard_map/ppermute | solution.py:551
  145.9 26.3 %collective-permute-start.19 = (bf16[256,2048]{1,0:T(8,128)(2,1)}, bf16[256,2048]{1,0:T(8,128)(2,1)}, u32[]{:S(2)}, u32[]{:S(2)}) collective-permute-start(bf16[256,2048]{1,0:T(8,128)(2,1)} %pad_maximum_fusion.4), channel_id=1, source_target_pairs={{0,1},{1,0},{2,3},{3,2},{4,5},{5,4},{6,7},{7,6},{8,9},{9,8},{10,11... | collective-permute-start | bytes 3145736 | tf_op jit(solution)/shard_map/ppermute | solution.py:551
  147.2 23.2 %collective-permute-start.22 = (bf16[512,512]{1,0:T(8,128)(2,1)}, bf16[512,512]{1,0:T(8,128)(2,1)}, u32[]{:S(2)}, u32[]{:S(2)}) collective-permute-start(bf16[512,512]{1,0:T(8,128)(2,1)} %collective-permute-done.20), channel_id=1, source_target_pairs={{0,4},{4,0},{8,12},{12,8},{16,20},{20,16},{24,28},{28,24},{1,5},{5... | collective-permute-start | bytes 1572872 | tf_op jit(solution)/shard_map/ppermute | solution.py:551
  194.4 24.0 %collective-permute-start.27 = (bf16[512,512]{1,0:T(8,128)(2,1)}, bf16[512,512]{1,0:T(8,128)(2,1)}, u32[]{:S(2)}, u32[]{:S(2)}) collective-permute-start(bf16[512,512]{1,0:T(8,128)(2,1)} %convolution_convert_fusion.5), channel_id=1, source_target_pairs={{0,4},{4,0},{8,12},{12,8},{16,20},{20,16},{24,28},{28,24},{1,5},{5... | collective-permute-start | bytes 1572872 | tf_op jit(solution)/shard_map/ppermute | solution.py:551
  196.3 48.2 %collective-permute-start.28 = (bf16[512,512]{1,0:T(8,128)(2,1)}, bf16[512,512]{1,0:T(8,128)(2,1)S(1)}, u32[]{:S(2)}, u32[]{:S(2)}) collective-permute-start(bf16[512,512]{1,0:T(8,128)(2,1)} %convolution_convert_fusion.4), channel_id=1, source_target_pairs={{0,4},{4,0},{8,12},{12,8},{16,20},{20,16},{24,28},{28,24},{1,5},{5... | collective-permute-start | bytes 1572872 | tf_op jit(solution)/shard_map/ppermute | solution.py:551
  226.9 22.5 %collective-permute-start.29 = (bf16[2,128,2048]{2,1,0:T(8,128)(2,1)S(1)}, bf16[2,128,2048]{2,1,0:T(8,128)(2,1)S(1)}, u32[]{:S(2)}, u32[]{:S(2)}) collective-permute-start(bf16[2,128,2048]{2,1,0:T(8,128)(2,1)S(1)} %dynamic-slice_convert_fusion.2), channel_id=1, source_target_pairs={{0,2},{1,3},{2,0},{3,1},{4,6},{5,7},{6,4},{7,5},{8,10},{9,11},{10,... | collective-permute-start | bytes 3145736 | tf_op jit(solution)/shard_map/ppermute | solution.py:551
  228.4 29.0 %collective-permute-start.31 = (bf16[512,512]{1,0:T(8,128)(2,1)}, bf16[512,512]{1,0:T(8,128)(2,1)}, u32[]{:S(2)}, u32[]{:S(2)}) collective-permute-start(bf16[512,512]{1,0:T(8,128)(2,1)} %fusion.18), channel_id=1, source_target_pairs={{0,16},{4,20},{8,24},{12,28},{16,0},{20,4},{24,8},{28,12},{1,17},{... | collective-permute-start | bytes 1572872 | tf_op jit(solution)/shard_map/ppermute | solution.py:551
  273.7 52.5 %collective-permute-start.37 = (f32[2,256,2048]{2,1,0:T(8,128)}, f32[2,256,2048]{2,1,0:T(8,128)}, u32[]{:S(2)}, u32[]{:S(2)}) collective-permute-start(f32[2,256,2048]{2,1,0:T(8,128)} %input_terms.2), channel_id=1, source_target_pairs={{0,1},{1,0},{2,3},{3,2},{4,5},{5,4},{6,7},{7,6},{8,9},{9,8},{10,11... | collective-permute-start | bytes 12582920 | tf_op jit(solution)/shard_map/ppermute | solution.py:551
  282.7 85.1 %collective-permute-start.41 = (bf16[512,512]{1,0:T(8,128)(2,1)}, bf16[512,512]{1,0:T(8,128)(2,1)}, u32[]{:S(2)}, u32[]{:S(2)}) collective-permute-start(bf16[512,512]{1,0:T(8,128)(2,1)} %fusion.19), channel_id=1, source_target_pairs={{0,16},{4,20},{8,24},{12,28},{16,0},{20,4},{24,8},{28,12},{1,17},{... | collective-permute-start | bytes 1572872 | tf_op jit(solution)/shard_map/ppermute | solution.py:551
  286.2 29.4 %collective-permute-start.36 = (bf16[512,512]{1,0:T(8,128)(2,1)}, bf16[512,512]{1,0:T(8,128)(2,1)}, u32[]{:S(2)}, u32[]{:S(2)}) collective-permute-start(bf16[512,512]{1,0:T(8,128)(2,1)} %convolution_convert_fusion.2), channel_id=1, source_target_pairs={{0,4},{4,0},{8,12},{12,8},{16,20},{20,16},{24,28},{28,24},{1,5},{5... | collective-permute-start | bytes 1572872 | tf_op jit(solution)/shard_map/ppermute | solution.py:551
  302.3 24.0 %collective-permute-start.39 = (bf16[128,2048]{1,0:T(8,128)(2,1)}, bf16[128,2048]{1,0:T(8,128)(2,1)S(1)}, u32[]{:S(2)}, u32[]{:S(2)}) collective-permute-start(bf16[128,2048]{1,0:T(8,128)(2,1)} %fusion.61), channel_id=1, source_target_pairs={{0,8},{4,12},{8,0},{12,4},{16,24},{20,28},{24,16},{28,20},{1,9},{5... | collective-permute-start | bytes 1572872 | tf_op jit(solution)/shard_map/ppermute | solution.py:551
  315.2 19.6 %collective-permute-start.35 = (bf16[128,256]{1,0:T(8,128)(2,1)S(1)}, bf16[128,256]{1,0:T(8,128)(2,1)S(1)}, u32[]{:S(2)}, u32[]{:S(2)}) collective-permute-start(bf16[128,256]{1,0:T(8,128)(2,1)S(1)} %fusion.78), channel_id=1, source_target_pairs={{0,2},{1,3},{2,0},{3,1},{4,6},{5,7},{6,4},{7,5},{8,10},{9,11},{10,... | collective-permute-start | bytes 196616 | tf_op jit(solution)/shard_map/ppermute | solution.py:551
  334.7 44.5 %collective-permute-start.46 = (bf16[512,512]{1,0:T(8,128)(2,1)S(1)}, bf16[512,512]{1,0:T(8,128)(2,1)S(1)}, u32[]{:S(2)}, u32[]{:S(2)}) collective-permute-start(bf16[512,512]{1,0:T(8,128)(2,1)S(1)} %fusion.20), channel_id=1, source_target_pairs={{0,16},{4,20},{8,24},{12,28},{16,0},{20,4},{24,8},{28,12},{1,17},{... | collective-permute-start | bytes 1572872 | tf_op jit(solution)/shard_map/ppermute | solution.py:551
  335.9 41.2 %collective-permute-start.45 = (bf16[1024,512]{1,0:T(8,128)(2,1)S(1)}, bf16[1024,512]{1,0:T(8,128)(2,1)S(1)}, u32[]{:S(2)}, u32[]{:S(2)}) collective-permute-start(bf16[1024,512]{1,0:T(8,128)(2,1)S(1)} %copy-done.36), channel_id=1, source_target_pairs={{0,4},{4,0},{8,12},{12,8},{16,20},{20,16},{24,28},{28,24},{1,5},{5... | collective-permute-start | bytes 3145736 | tf_op jit(solution)/shard_map/ppermute | solution.py:551
  337.5 42.8 %collective-permute-start.40 = (bf16[2,128,2048]{2,1,0:T(8,128)(2,1)S(1)}, bf16[2,128,2048]{2,1,0:T(8,128)(2,1)S(1)}, u32[]{:S(2)}, u32[]{:S(2)}) collective-permute-start(bf16[2,128,2048]{2,1,0:T(8,128)(2,1)S(1)} %dynamic-slice_convert_fusion.1), channel_id=1, source_target_pairs={{0,2},{1,3},{2,0},{3,1},{4,6},{5,7},{6,4},{7,5},{8,10},{9,11},{10,... | collective-permute-start | bytes 3145736 | tf_op jit(solution)/shard_map/ppermute | solution.py:551
  340.4 26.9 %collective-permute-start.43 = (f32[4,72,256]{2,1,0:T(8,128)S(1)}, f32[4,72,256]{2,1,0:T(8,128)S(1)}, u32[]{:S(2)}, u32[]{:S(2)}) collective-permute-start(f32[4,72,256]{2,1,0:T(8,128)S(1)} %pad_maximum_fusion.13), channel_id=1, source_target_pairs={{0,4},{4,0},{8,12},{12,8},{16,20},{20,16},{24,28},{28,24},{1,5},{5... | collective-permute-start | bytes 884744 | tf_op jit(solution)/shard_map/ppermute | solution.py:551
  380.5 27.3 %collective-permute-start.48 = (bf16[512,512]{1,0:T(8,128)(2,1)S(1)}, bf16[512,512]{1,0:T(8,128)(2,1)S(1)}, u32[]{:S(2)}, u32[]{:S(2)}) collective-permute-start(bf16[512,512]{1,0:T(8,128)(2,1)S(1)} %pad_maximum_fusion.12), channel_id=1, source_target_pairs={{0,8},{4,12},{8,0},{12,4},{16,24},{20,28},{24,16},{28,20},{1,9},{5... | collective-permute-start | bytes 1572872 | tf_op jit(solution)/shard_map/ppermute | solution.py:551
  383.5 23.3 %collective-permute-start.49 = (bf16[128,2048]{1,0:T(8,128)(2,1)S(1)}, bf16[128,2048]{1,0:T(8,128)(2,1)S(1)}, u32[]{:S(2)}, u32[]{:S(2)}) collective-permute-start(bf16[128,2048]{1,0:T(8,128)(2,1)S(1)} %fusion.62), channel_id=1, source_target_pairs={{0,8},{4,12},{8,0},{12,4},{16,24},{20,28},{24,16},{28,20},{1,9},{5... | collective-permute-start | bytes 1572872 | tf_op jit(solution)/shard_map/ppermute | solution.py:551
  383.6 23.2 %collective-permute-start.50 = (f32[72,256]{1,0:T(8,128)S(1)}, f32[72,256]{1,0:T(8,128)S(1)}, u32[]{:S(2)}, u32[]{:S(2)}) collective-permute-start(f32[72,256]{1,0:T(8,128)S(1)} %slice_bitcast_fusion.3), channel_id=1, source_target_pairs={{0,8},{4,12},{8,0},{12,4},{16,24},{20,28},{24,16},{28,20},{1,9},{5... | collective-permute-start | bytes 221192 | tf_op jit(solution)/shard_map/ppermute | solution.py:551
  414.2 55.0 %collective-permute-start.62 = (bf16[256,2048]{1,0:T(8,128)(2,1)}, bf16[256,2048]{1,0:T(8,128)(2,1)}, u32[]{:S(2)}, u32[]{:S(2)}) collective-permute-start(bf16[256,2048]{1,0:T(8,128)(2,1)} %pad_maximum_fusion.7), channel_id=1, source_target_pairs={{0,1},{1,0},{2,3},{3,2},{4,5},{5,4},{6,7},{7,6},{8,9},{9,8},{10,11... | collective-permute-start | bytes 3145736 | tf_op jit(solution)/shard_map/ppermute | solution.py:551
  (137 other events, 1795.9 us)

commit v4 on v3

--- a/solution.py
+++ b/solution.py
@@ -901,46 +901,52 @@
     both_sent = jnp.concatenate(
         [gradient_rows(normed_flat, values, 2, bf16) for values in (x_low, z_low)], axis=0
     )
-    input_leaving = input_terms(1 - core, z_low, x_low, dt_low, *matrices)
-    x_low, z_low, x_passed, z_sent, both_sent, input_leaving, bc_arriving = step(
-        x_low, z_low, x_passed, z_sent, both_sent, input_leaving, bc_arriving
-    )
-
-    x_middle = gradient_rows(normed_flat, x_low, 1, bf16, x_passed)
-    x_got = across(x_middle, middle_bit)
-    z_passed = swap(z_sent, "dp", last_bit)
-    input_arriving = swap(input_leaving, "tensor", 1)
+    x_low, z_low, z_sent, both_sent, bc_arriving, arriving = step(
+        x_low, z_low, z_sent, both_sent, bc_arriving, arriving
+    )
+
     bc_kept = bc_kept + bc_arriving
     bc_far = swap(bc_kept[1], "dp", PAIR)
-    x_low, z_low, x_middle, bc_kept, arriving = step(x_low, z_low, x_middle, bc_kept, arriving)
     shared = shared + arriving.astype(f32)
     shared_leaving = low_bits(shared[1])
     out_mine, out_leaving = middle_sum(gradient_rows(proj_later, scaled_low, 0, f32, out_kept), out_got)
-    x_low, z_low, bc_far, shared_leaving, out_mine, out_leaving = step(
-        x_low, z_low, bc_far, shared_leaving, out_mine, out_leaving
+    x_low, z_low, shared_leaving, out_mine, out_leaving = step(
+        x_low, z_low, shared_leaving, out_mine, out_leaving
     )
     out_far = across(out_leaving, PAIR)
     projected_far = across(shared_leaving, PAIR)
+    input_leaving = input_terms(1 - core, z_low, x_low, dt_low, *matrices)
+    x_low, z_low, x_passed, input_leaving, bc_far, out_far, projected_far = step(
+        x_low, z_low, x_passed, input_leaving, bc_far, out_far, projected_far
+    )
+
+    z_passed = swap(z_sent, "dp", last_bit)
+    x_middle = gradient_rows(normed_flat, x_low, 1, bf16, x_passed)
+    x_got = across(x_middle, middle_bit)
+    input_arriving = swap(input_leaving, "tensor", 1)
+    bc_low_mine = (bc_kept[0] + bc_far).astype(bf16)
+    bc_far = swap(bc_low_mine, "tensor", 2)
+    x_low, z_low, x_middle, bc_far = step(x_low, z_low, x_middle, bc_far)
+    projected_mine = shared[0] + flip_pairs(projected_far.astype(f32))
+    output = from_relative((in_mine + inv_mine[:, None] * projected_mine).astype(bf16), data_at)
+    output_far = swap(output, "tensor", 2)
     input_kept = input_terms(core, z_low, x_low, dt_low, *matrices)
-    x_low, z_low, input_kept, z_passed, input_arriving, out_far, projected_far, both_sent = step(
-        x_low, z_low, input_kept, z_passed, input_arriving, out_far, projected_far, both_sent
+    out_share = join_halves(out_mine, out_far.astype(f32), half, 1)
+    x_low, z_low, input_kept, z_passed, input_arriving, output_far, out_share = step(
+        x_low, z_low, input_kept, z_passed, input_arriving, output_far, out_share
     )
 
     z_middle = gradient_rows(normed_flat, z_low, 1, bf16, z_passed)
     z_got = across(z_middle, middle_bit)
     both_kept = swap(both_sent, "dp", last_bit)
-    bc_low_mine = (bc_kept[0] + bc_far).astype(bf16)
-    bc_far = swap(bc_low_mine, "tensor", 2)
-    x_low, z_low, z_middle, bc_low_mine = step(x_low, z_low, z_middle, bc_low_mine)
-    input_kept, input_leaving = kept_and_sent(input_kept + input_arriving, tensor_at, 2, bf16)
-    bc_far, input_kept, input_leaving = step(bc_far, input_kept, input_leaving)
-
-    input_arriving = swap(input_leaving, "tensor", 2)
     bc_low = join_halves(bc_low_mine, bc_far, tensor_at // 2, 0)
     bc_far = swap(bc_low, "tensor", 1)
+    x_low, z_low, z_middle, bc_low = step(x_low, z_low, z_middle, bc_low)
+    input_kept, input_leaving = kept_and_sent(input_kept + input_arriving, tensor_at, 2, bf16)
     dt_part = tokens_out(dt_low, normed_flat)[:head_count]
-    bc_far, dt_part = step(bc_far, dt_part)
-
+    bc_far, dt_part, input_kept, input_leaving = step(bc_far, dt_part, input_kept, input_leaving)
+
+    input_arriving = swap(input_leaving, "tensor", 2)
     bc_low = join_halves(bc_low, bc_far, core, 0)
     bc_columns = bc_low.shape[1] // 4
     bc_part = tokens_out(
@@ -952,28 +958,25 @@
     )
     count = held.shape[0] // 2
     held = held[:count] + swap(held[count:], "dp", last_bit)
-    projected_mine = shared[0] + flip_pairs(projected_far.astype(f32))
-    output = from_relative((in_mine + inv_mine[:, None] * projected_mine).astype(bf16), data_at)
-    output_far = swap(output, "tensor", 2)
-    out_share = join_halves(out_mine, out_far.astype(f32), half, 1)
-    x_got, held, output, out_share = step(x_got, held, output, out_share)
+    output = join_halves(output, output_far, tensor_at // 2, 0)
+    output_far = swap(output, "tensor", 1)
+    held, both_kept, x_got, output_far = step(held, both_kept, x_got, output_far)
     for bit in reversed(dp_bits()[1:-1]):
         count = held.shape[0] // 2
         held = held[:count] + swap(held[count:], "dp", bit)
     x_terms = gradient_rows(normed_flat, x_low, 0, f32, both_kept[:part])
     z_terms = gradient_rows(normed_flat, z_low, 0, f32, both_kept[part:])
     x_mine, x_leaving = middle_sum(x_terms, x_got)
-    input_arriving, held, z_terms, x_leaving, z_got, output_far = step(
-        input_arriving, held, z_terms, x_leaving, z_got, output_far
-    )
-
+    output = join_halves(output, output_far, core, 0)
+    input_mine = input_kept + input_arriving.astype(f32)
+    input_leaving = low_bits(input_mine[1])
+    held, z_terms, x_leaving, input_leaving = step(held, z_terms, x_leaving, input_leaving)
+
+    input_far = swap(input_leaving, "dp", PAIR)
     small_far = swap(held[1], "dp", PAIR)
-    input_mine = input_kept + input_arriving.astype(f32)
-    input_far = swap(low_bits(input_mine[1]), "dp", PAIR)
     z_mine, z_leaving = middle_sum(z_terms, z_got)
+    z_leaving, small_far, input_far = step(z_leaving, small_far, input_far)
     both_far = across(jnp.concatenate([x_leaving, z_leaving], axis=0), PAIR)
-    input_far, small_far = step(input_far, small_far)
-    output = join_halves(output, output_far, tensor_at // 2, 0)
     normed_grad = (
         input_mine[0] + flip_pairs(input_far.astype(f32)) + rows_times(bc_low_mine, low_bc)
     )
@@ -981,8 +984,7 @@
     _, norm_pull = jax.vjp(norm_input, in_mine, gain_rel)
     block_grad, gain_slot = norm_pull(normed_grad)
     input_grad = from_relative((cot_mine + block_grad).astype(bf16), data_at)
-    both_far, gain_slot, small_far, output = step(both_far, gain_slot, small_far, output)
-    output = join_halves(output, swap(output, "tensor", 1), core, 0)
+    both_far, gain_slot, output = step(both_far, gain_slot, output)
     x_share = join_halves(x_mine, both_far[: x_mine.shape[0]].astype(f32), half, 1)
     z_share = join_halves(z_mine, both_far[x_mine.shape[0] :].astype(f32), half, 1)
 

time: 516 us -> 484 us (0.938)
  waiting for transfers between devices: 168 us -> 134 us
  starting transfers between devices: 58.9 us -> 66.8 us
  local copies, waits for them, and re-layouts: 78.2 us -> 71.9 us
    ppermute x68, waiting for transfers between devices: 168 us -> 134 us  [swap(): lax.ppermute(value, axis, [(place, place ^ bit) for place in range(size)])]
    ppermute x68, starting transfers between devices: 58.9 us -> 66.8 us  [swap(): lax.ppermute(value, axis, [(place, place ^ bit) for place in range(size)])]
    unnamed x292 -> x302, local copies, waits for them, and re-layouts: 51.8 us -> 45.8 us
  transfers between devices with their start and end apart: 68 -> 68, of which waited for: 31 -> 29; matrix products, arithmetic and copies ran while one was open for 33% -> 31% of each run, Pallas kernels for 12% -> 13%
where the time goes in v4:
time: 484 us; the launch traced here: 476 us
  waiting for transfers between devices  134 us (28%)
  other arithmetic  84.5 us (17%)
  local copies, waits for them, and re-layouts  71.9 us (15%)
  starting transfers between devices  66.8 us (14%)
  Pallas kernels  61.6 us (13%)
  matrix products  43.6 us (9%)
  between operations  13.9 us (3%)
    ppermute x68, waiting for transfers between devices, swap(): lax.ppermute(value, axis, [(place, place ^ bit) for place in range(size)])  134 us
    ppermute x68, starting transfers between devices, swap(): lax.ppermute(value, axis, [(place, place ^ bit) for place in range(size)])  66.8 us
    unnamed x302, local copies, waits for them, and re-layouts  45.8 us
    pallas_call x2, Pallas kernels, mixer_backward(): pl.pallas_call(body, grid=(1, pairs), in_specs=common_specs(slot, length)...  31 us
    dot_general x14, matrix products, tokens_out(): lax.dot_general(left, right, (((0,), (0,)), ((), ())), preferred_element_...  25.1 us
    pallas_call x1, Pallas kernels, mixer_forward(): pl.pallas_call(forward_body, grid=(slots, pairs), in_specs=common_specs(0...  16.4 us
    pallas_call x2, Pallas kernels, input_terms(): pl.pallas_call(input_body, grid_spec=pltpu.PrefetchScalarGridSpec(num_sca...  14.2 us
    select_n x18, other arithmetic, join_halves(): jnp.where(half == 0, mine, other)  12.3 us
  transfers between devices with their start and end apart: 68, of which 29 were waited for; matrix products, arithmetic and copies ran while one was open for 31% of the time, Pallas kernels for 13%

profile of v4, /device:TPU:0, one launch (start us, length us, event | category | flops | bytes accessed | tf_op | source)
XLA Modules:
  0.0 476.0 jit_solution(12952006211557777763)
XLA Ops:
  3.0 3.1 collective-permute-start
  10.1 5.2 %collective-permute-done.1 = bf16[256,512]{1,0:T(8,128)(2,1)S(1)} collective-permute-done((bf16[256,512]{1,0:T(8,128)(2,1)S(1)}, bf16[256,512]{1,0:T(8,128)(2,1)S(1)}, u32[]{:S(2)}, u32[]{:S(2)}) %collective-permute-start.1) | collective-permute-done | bytes 262176 | tf_op jit(solution)/shard_map/ppermute | solution.py:551
  39.0 6.4 %collective-permute-done.4 = bf16[2,160,128]{2,1,0:T(8,128)(2,1)S(1)} collective-permute-done((bf16[2,160,128]{2,1,0:T(8,128)(2,1)S(1)}, bf16[2,160,128]{2,1,0:T(8,128)(2,1)S(1)}, u32[]{:S(2)}, u32[]{:S(2)}) %collective-permute-start.4) | collective-permute-done | bytes 81952 | tf_op jit(solution)/shard_map/ppermute | solution.py:551
  54.4 8.4 %collective-permute-done.6 = bf16[4,160,128]{2,1,0:T(8,128)(2,1)S(1)} collective-permute-done((bf16[4,160,128]{2,1,0:T(8,128)(2,1)S(1)}, bf16[4,160,128]{2,1,0:T(8,128)(2,1)S(1)}, u32[]{:S(2)}, u32[]{:S(2)}) %collective-permute-start.6) | collective-permute-done | bytes 163872 | tf_op jit(solution)/shard_map/ppermute | solution.py:551
  73.3 8.3 %collective-permute-done.11 = bf16[128,2048]{1,0:T(8,128)(2,1)S(1)} collective-permute-done((bf16[128,2048]{1,0:T(8,128)(2,1)}, bf16[128,2048]{1,0:T(8,128)(2,1)S(1)}, u32[]{:S(2)}, u32[]{:S(2)}) %collective-permute-start.11) | collective-permute-done | bytes 524320 | tf_op jit(solution)/shard_map/ppermute | solution.py:551
  83.8 12.4 %collective-permute-done.9 = bf16[512,512]{1,0:T(8,128)(2,1)S(1)} collective-permute-done((bf16[512,512]{1,0:T(8,128)(2,1)S(1)}, bf16[512,512]{1,0:T(8,128)(2,1)S(1)}, u32[]{:S(2)}, u32[]{:S(2)}) %collective-permute-start.9) | collective-permute-done | bytes 524320 | tf_op jit(solution)/shard_map/ppermute | solution.py:551
  107.0 4.7 collective-permute-done.17
  124.7 3.6 fusion.13.x_ref.refs_6_
  128.4 3.7 fusion.11.z_ref.refs_7_
  137.9 6.7 %collective-permute-done.18 = bf16[128,2048]{1,0:T(8,128)(2,1)S(1)} collective-permute-done((bf16[128,2048]{1,0:T(8,128)(2,1)S(1)}, bf16[128,2048]{1,0:T(8,128)(2,1)S(1)}, u32[]{:S(2)}, u32[]{:S(2)}) %collective-permute-start.18) | collective-permute-done | bytes 524320 | tf_op jit(solution)/shard_map/ppermute | solution.py:551
  149.4 16.4 %mixer_forward.1 = (bf16[2,512,512]{2,1,0:T(8,128)(2,1)}, f32[2,512,512]{2,1,0:T(8,128)}, f32[2,512,128]{2,1,0:T(8,128)}) custom-call(f32[2,512,8]{2,1,0:T(8,128)} %copy.138.marks_ref.refs_0_, f32[2,8,512]{2,1,0:T(8,128)} %broadcast_in_dim.28.row_ref.refs_1_, f32[2,512,256]{2,1,0:T(8,128)} %fusion.143.bc_ref.refs_2_, f32[2,512,128]{2,1,0:T(8,128)} %fusion.64.dt_ref.refs_3_, ...), custom_call_target="tpu_custom_call" | custom-call | flops 16000000000 | bytes 1048576 | tf_op jit(solution)/shard_map/mixer_forward/pallas_call | solution.py:387
  190.3 2.9 multiply_convert_fusion
  198.9 3.7 fusion.2.refs_10_
  203.7 15.6 %mixer_backward.2 = (bf16[2,512,512]{2,1,0:T(8,128)(2,1)}, bf16[2,512,512]{2,1,0:T(8,128)(2,1)}, f32[2,512,256]{2,1,0:T(8,128)}, f32[2,512,128]{2,1,0:T(8,128)},...) custom-call(f32[2,512,8]{2,1,0:T(8,128)} %copy.138.marks_ref.refs_0_, ...), custom_call_target="tpu_custom_call" | custom-call | flops 16000000000 | bytes 1048576 | tf_op jit(solution)/shard_map/mixer_backward/pallas_call | solution.py:412
  219.3 2.8 fusion.18
  222.1 3.4 convert_add_fusion
  230.0 15.4 %mixer_backward.3 = (bf16[2,512,512]{2,1,0:T(8,128)(2,1)}, bf16[2,512,512]{2,1,0:T(8,128)(2,1)}, f32[2,512,256]{2,1,0:T(8,128)}, f32[2,512,128]{2,1,0:T(8,128)},...) custom-call(f32[2,512,8]{2,1,0:T(8,128)} %copy.138.marks_ref.refs_0_, ...), custom_call_target="tpu_custom_call", output_to_operand_aliasing={{0}: (12, {}), {1}: (13, {}), {2}: (14, {}), {3}: (15, {}),... | custom-call | flops 16000000000 | bytes 1048576 | tf_op jit(solution)/shard_map/mixer_backward/pallas_call | solution.py:412
  248.6 3.0 convolution_bitcast_fusion
  254.1 3.1 convolution_convert_fusion.3
  275.7 7.0 %input_terms.2 = f32[2,256,2048]{2,1,0:T(8,128)} custom-call(s32[1]{0:T(128)} %bitcast.60.place_ref, bf16[2,2,256,512]{3,2,1,0:T(8,128)(2,1)} %bitcast.375, bf16[2,2,256,512]{3,2,1,0:T(8,128)(2,1)} %bitcast.382, bf16[2,2,256,128]{3,2,1,0:T(8,128)(2,1)} %bitcast.322, bf16[2048,512]{1,0:T(8,128)(2,1)} %copy-done.63, ...), custom_call_target="tpu_custom_call" | custom-call | flops 6000000000 | bytes 1048576 | tf_op jit(solution)/shard_map/input_terms/pallas_call | solution.py:480
  284.3 8.7 %collective-permute-done.36 = bf16[128,2048]{1,0:T(8,128)(2,1)S(1)} collective-permute-done((bf16[128,2048]{1,0:T(8,128)(2,1)}, bf16[128,2048]{1,0:T(8,128)(2,1)S(1)}, u32[]{:S(2)}, u32[]{:S(2)}) %collective-permute-start.36) | collective-permute-done | bytes 524320 | tf_op jit(solution)/shard_map/ppermute | solution.py:551
  298.5 2.9 fusion.19
  303.8 7.2 %input_terms.3 = f32[2,256,2048]{2,1,0:T(8,128)} custom-call(s32[1]{0:T(128)} %bitcast.66.place_ref, bf16[2,2,256,512]{3,2,1,0:T(8,128)(2,1)} %bitcast.376, bf16[2,2,256,512]{3,2,1,0:T(8,128)(2,1)} %bitcast.383, bf16[2,2,256,128]{3,2,1,0:T(8,128)(2,1)} %bitcast.323, bf16[2048,512]{1,0:T(8,128)(2,1)} %copy-done.63, ...), custom_call_target="tpu_custom_call" | custom-call | flops 6000000000 | bytes 1048576 | tf_op jit(solution)/shard_map/input_terms/pallas_call | solution.py:480
  311.1 4.2 add.830
  324.7 6.7 %collective-permute-done.42 = f32[4,72,256]{2,1,0:T(8,128)S(1)} collective-permute-done((f32[4,72,256]{2,1,0:T(8,128)S(1)}, f32[4,72,256]{2,1,0:T(8,128)S(1)}, u32[]{:S(2)}, u32[]{:S(2)}) %collective-permute-start.42) | collective-permute-done | bytes 294944 | tf_op jit(solution)/shard_map/ppermute | solution.py:551
  334.5 12.1 %collective-permute-done.47 = bf16[2,128,2048]{2,1,0:T(8,128)(2,1)S(1)} collective-permute-done((bf16[2,128,2048]{2,1,0:T(8,128)(2,1)S(1)}, bf16[2,128,2048]{2,1,0:T(8,128)(2,1)S(1)}, u32[]{:S(2)}, u32[]{:S(2)}) %collective-permute-start.47) | collective-permute-done | bytes 1048608 | tf_op jit(solution)/shard_map/ppermute | solution.py:551
  350.7 11.9 %collective-permute-done.46 = f32[2,72,256]{2,1,0:T(8,128)S(1)} collective-permute-done((f32[2,72,256]{2,1,0:T(8,128)S(1)}, f32[2,72,256]{2,1,0:T(8,128)S(1)}, u32[]{:S(2)}, u32[]{:S(2)}) %collective-permute-start.46) | collective-permute-done | bytes 147488 | tf_op jit(solution)/shard_map/ppermute | solution.py:551
  366.4 10.6 %collective-permute-done.49 = f32[72,256]{1,0:T(8,128)S(1)} collective-permute-done((f32[72,256]{1,0:T(8,128)S(1)}, f32[72,256]{1,0:T(8,128)S(1)}, u32[]{:S(2)}, u32[]{:S(2)}) %collective-permute-start.49) | collective-permute-done | bytes 73760 | tf_op jit(solution)/shard_map/ppermute | solution.py:551
  383.3 3.0 collective-permute-done.53
  386.3 2.8 collective-permute-done.51
  391.3 3.6 collective-permute-start.55
  411.4 2.8 collective-permute-done.60
  (684 shorter events, 249.8 us)
Async XLA Ops:
  17.0 28.4 %collective-permute-start.2 = (bf16[512,512]{1,0:T(8,128)(2,1)}, bf16[512,512]{1,0:T(8,128)(2,1)}, u32[]{:S(2)}, u32[]{:S(2)}) collective-permute-start(bf16[512,512]{1,0:T(8,128)(2,1)} %get-tuple-element.664), channel_id=1, source_target_pairs={{0,16},{4,20},{8,24},{12,28},{16,0},{20,4},{24,8},{28,12},{1,17},{... | collective-permute-start | bytes 1572872 | tf_op jit(solution)/shard_map/ppermute | solution.py:551
  19.6 25.8 %collective-permute-start.3 = (bf16[512,512]{1,0:T(8,128)(2,1)}, bf16[512,512]{1,0:T(8,128)(2,1)}, u32[]{:S(2)}, u32[]{:S(2)}) collective-permute-start(bf16[512,512]{1,0:T(8,128)(2,1)} %get-tuple-element.664), channel_id=1, source_target_pairs={{0,4},{4,0},{8,12},{12,8},{16,20},{20,16},{24,28},{28,24},{1,5},{5... | collective-permute-start | bytes 1572872 | tf_op jit(solution)/shard_map/ppermute | solution.py:551
  22.1 23.3 %collective-permute-start.4 = (bf16[2,160,128]{2,1,0:T(8,128)(2,1)S(1)}, bf16[2,160,128]{2,1,0:T(8,128)(2,1)S(1)}, u32[]{:S(2)}, u32[]{:S(2)}) collective-permute-start(bf16[2,160,128]{2,1,0:T(8,128)(2,1)S(1)} %pad_maximum_fusion.17), channel_id=1, source_target_pairs={{0,16},{4,20},{8,24},{12,28},{16,0},{20,4},{24,8},{28,12},{1,17},{... | collective-permute-start | bytes 245768 | tf_op jit(solution)/shard_map/ppermute | solution.py:551
  45.4 20.9 %collective-permute-start.5 = (bf16[512,512]{1,0:T(8,128)(2,1)}, bf16[512,512]{1,0:T(8,128)(2,1)}, u32[]{:S(2)}, u32[]{:S(2)}) collective-permute-start(bf16[512,512]{1,0:T(8,128)(2,1)} %collective-permute-done.2), channel_id=1, source_target_pairs={{0,4},{4,0},{8,12},{12,8},{16,20},{20,16},{24,28},{28,24},{1,5},{5... | collective-permute-start | bytes 1572872 | tf_op jit(solution)/shard_map/ppermute | solution.py:551
  46.8 19.5 %collective-permute-start.8 = (bf16[128,2048]{1,0:T(8,128)(2,1)}, bf16[128,2048]{1,0:T(8,128)(2,1)}, u32[]{:S(2)}, u32[]{:S(2)}) collective-permute-start(bf16[128,2048]{1,0:T(8,128)(2,1)} %get-tuple-element.203), channel_id=1, source_target_pairs={{0,8},{4,12},{8,0},{12,4},{16,24},{20,28},{24,16},{28,20},{1,9},{5... | collective-permute-start | bytes 1572872 | tf_op jit(solution)/shard_map/ppermute | solution.py:551
  48.6 17.7 %collective-permute-start.7 = (bf16[256,512]{1,0:T(8,128)(2,1)}, bf16[256,512]{1,0:T(8,128)(2,1)}, u32[]{:S(2)}, u32[]{:S(2)}) collective-permute-start(bf16[256,512]{1,0:T(8,128)(2,1)} %get-tuple-element.202), channel_id=1, source_target_pairs={{0,8},{4,12},{8,0},{12,4},{16,24},{20,28},{24,16},{28,20},{1,9},{5... | collective-permute-start | bytes 786440 | tf_op jit(solution)/shard_map/ppermute | solution.py:551
  70.3 25.9 %collective-permute-start.9 = (bf16[512,512]{1,0:T(8,128)(2,1)S(1)}, bf16[512,512]{1,0:T(8,128)(2,1)S(1)}, u32[]{:S(2)}, u32[]{:S(2)}) collective-permute-start(bf16[512,512]{1,0:T(8,128)(2,1)S(1)} %get-tuple-element.660), channel_id=1, source_target_pairs={{0,16},{4,20},{8,24},{12,28},{16,0},{20,4},{24,8},{28,12},{1,17},{... | collective-permute-start | bytes 1572872 | tf_op jit(solution)/shard_map/ppermute | solution.py:551
  70.8 25.4 %collective-permute-start.10 = (bf16[512,512]{1,0:T(8,128)(2,1)S(1)}, bf16[512,512]{1,0:T(8,128)(2,1)S(1)}, u32[]{:S(2)}, u32[]{:S(2)}) collective-permute-start(bf16[512,512]{1,0:T(8,128)(2,1)S(1)} %get-tuple-element.660), channel_id=1, source_target_pairs={{0,4},{4,0},{8,12},{12,8},{16,20},{20,16},{24,28},{28,24},{1,5},{5... | collective-permute-start | bytes 1572872 | tf_op jit(solution)/shard_map/ppermute | solution.py:551
  96.2 16.8 %collective-permute-start.16 = (bf16[256,2048]{1,0:T(8,128)(2,1)}, bf16[256,2048]{1,0:T(8,128)(2,1)}, u32[]{:S(2)}, u32[]{:S(2)}) collective-permute-start(bf16[256,2048]{1,0:T(8,128)(2,1)} %pad_maximum_fusion.2), channel_id=1, source_target_pairs={{0,1},{1,0},{2,3},{3,2},{4,5},{5,4},{6,7},{7,6},{8,9},{9,8},{10,11... | collective-permute-start | bytes 3145736 | tf_op jit(solution)/shard_map/ppermute | solution.py:551
  101.9 17.6 %collective-permute-start.13 = (bf16[512,512]{1,0:T(8,128)(2,1)}, bf16[512,512]{1,0:T(8,128)(2,1)S(1)}, u32[]{:S(2)}, u32[]{:S(2)}) collective-permute-start(bf16[512,512]{1,0:T(8,128)(2,1)} %copy-done.47), channel_id=1, source_target_pairs={{0,4},{4,0},{8,12},{12,8},{16,20},{20,16},{24,28},{28,24},{1,5},{5... | collective-permute-start | bytes 1572872 | tf_op jit(solution)/shard_map/ppermute | solution.py:551
  102.3 17.2 %collective-permute-start.14 = (bf16[256,512]{1,0:T(8,128)(2,1)}, bf16[256,512]{1,0:T(8,128)(2,1)S(1)}, u32[]{:S(2)}, u32[]{:S(2)}) collective-permute-start(bf16[256,512]{1,0:T(8,128)(2,1)} %get-tuple-element.216), channel_id=1, source_target_pairs={{0,8},{4,12},{8,0},{12,4},{16,24},{20,28},{24,16},{28,20},{1,9},{5... | collective-permute-start | bytes 786440 | tf_op jit(solution)/shard_map/ppermute | solution.py:551
  102.3 19.4 %collective-permute-start.15 = (bf16[128,2048]{1,0:T(8,128)(2,1)}, bf16[128,2048]{1,0:T(8,128)(2,1)S(1)}, u32[]{:S(2)}, u32[]{:S(2)}) collective-permute-start(bf16[128,2048]{1,0:T(8,128)(2,1)} %get-tuple-element.217), channel_id=1, source_target_pairs={{0,8},{4,12},{8,0},{12,4},{16,24},{20,28},{24,16},{28,20},{1,9},{5... | collective-permute-start | bytes 1572872 | tf_op jit(solution)/shard_map/ppermute | solution.py:551
  122.6 25.2 %collective-permute-start.20 = (bf16[512,512]{1,0:T(8,128)(2,1)}, bf16[512,512]{1,0:T(8,128)(2,1)}, u32[]{:S(2)}, u32[]{:S(2)}) collective-permute-start(bf16[512,512]{1,0:T(8,128)(2,1)} %get-tuple-element.655), channel_id=1, source_target_pairs={{0,16},{4,20},{8,24},{12,28},{16,0},{20,4},{24,8},{28,12},{1,17},{... | collective-permute-start | bytes 1572872 | tf_op jit(solution)/shard_map/ppermute | solution.py:551
  123.2 45.8 %collective-permute-start.21 = (bf16[512,512]{1,0:T(8,128)(2,1)}, bf16[512,512]{1,0:T(8,128)(2,1)}, u32[]{:S(2)}, u32[]{:S(2)}) collective-permute-start(bf16[512,512]{1,0:T(8,128)(2,1)} %get-tuple-element.655), channel_id=1, source_target_pairs={{0,4},{4,0},{8,12},{12,8},{16,20},{20,16},{24,28},{28,24},{1,5},{5... | collective-permute-start | bytes 1572872 | tf_op jit(solution)/shard_map/ppermute | solution.py:551
  146.5 26.3 %collective-permute-start.19 = (bf16[256,2048]{1,0:T(8,128)(2,1)}, bf16[256,2048]{1,0:T(8,128)(2,1)}, u32[]{:S(2)}, u32[]{:S(2)}) collective-permute-start(bf16[256,2048]{1,0:T(8,128)(2,1)} %pad_maximum_fusion.4), channel_id=1, source_target_pairs={{0,1},{1,0},{2,3},{3,2},{4,5},{5,4},{6,7},{7,6},{8,9},{9,8},{10,11... | collective-permute-start | bytes 3145736 | tf_op jit(solution)/shard_map/ppermute | solution.py:551
  147.8 23.1 %collective-permute-start.22 = (bf16[512,512]{1,0:T(8,128)(2,1)}, bf16[512,512]{1,0:T(8,128)(2,1)}, u32[]{:S(2)}, u32[]{:S(2)}) collective-permute-start(bf16[512,512]{1,0:T(8,128)(2,1)} %collective-permute-done.20), channel_id=1, source_target_pairs={{0,4},{4,0},{8,12},{12,8},{16,20},{20,16},{24,28},{28,24},{1,5},{5... | collective-permute-start | bytes 1572872 | tf_op jit(solution)/shard_map/ppermute | solution.py:551
  186.6 16.1 %collective-permute-start.26 = (bf16[2,256,2048]{2,1,0:T(8,128)(2,1)S(1)}, bf16[2,256,2048]{2,1,0:T(8,128)(2,1)}, u32[]{:S(2)}, u32[]{:S(2)}) collective-permute-start(bf16[2,256,2048]{2,1,0:T(8,128)(2,1)S(1)} %dynamic-slice_convert_fusion), channel_id=1, source_target_pairs={{0,1},{1,0},{2,3},{3,2},{4,5},{5,4},{6,7},{7,6},{8,9},{9,8},{10,11... | collective-permute-start | bytes 6291464 | tf_op jit(solution)/shard_map/ppermute | solution.py:551
  194.9 24.5 %collective-permute-start.27 = (bf16[512,512]{1,0:T(8,128)(2,1)}, bf16[512,512]{1,0:T(8,128)(2,1)S(1)}, u32[]{:S(2)}, u32[]{:S(2)}) collective-permute-start(bf16[512,512]{1,0:T(8,128)(2,1)} %convolution_convert_fusion.5), channel_id=1, source_target_pairs={{0,4},{4,0},{8,12},{12,8},{16,20},{20,16},{24,28},{28,24},{1,5},{5... | collective-permute-start | bytes 1572872 | tf_op jit(solution)/shard_map/ppermute | solution.py:551
  196.8 54.8 %collective-permute-start.28 = (bf16[512,512]{1,0:T(8,128)(2,1)}, bf16[512,512]{1,0:T(8,128)(2,1)}, u32[]{:S(2)}, u32[]{:S(2)}) collective-permute-start(bf16[512,512]{1,0:T(8,128)(2,1)} %convolution_convert_fusion.4), channel_id=1, source_target_pairs={{0,4},{4,0},{8,12},{12,8},{16,20},{20,16},{24,28},{28,24},{1,5},{5... | collective-permute-start | bytes 1572872 | tf_op jit(solution)/shard_map/ppermute | solution.py:551
  227.7 23.9 %collective-permute-start.29 = (bf16[2,128,2048]{2,1,0:T(8,128)(2,1)S(1)}, bf16[2,128,2048]{2,1,0:T(8,128)(2,1)}, u32[]{:S(2)}, u32[]{:S(2)}) collective-permute-start(bf16[2,128,2048]{2,1,0:T(8,128)(2,1)S(1)} %dynamic-slice_convert_fusion.2), channel_id=1, source_target_pairs={{0,2},{1,3},{2,0},{3,1},{4,6},{5,7},{6,4},{7,5},{8,10},{9,11},{10,... | collective-permute-start | bytes 3145736 | tf_op jit(solution)/shard_map/ppermute | solution.py:551
  229.2 28.0 %collective-permute-start.31 = (bf16[512,512]{1,0:T(8,128)(2,1)}, bf16[512,512]{1,0:T(8,128)(2,1)}, u32[]{:S(2)}, u32[]{:S(2)}) collective-permute-start(bf16[512,512]{1,0:T(8,128)(2,1)} %fusion.18), channel_id=1, source_target_pairs={{0,16},{4,20},{8,24},{12,28},{16,0},{20,4},{24,8},{28,12},{1,17},{... | collective-permute-start | bytes 1572872 | tf_op jit(solution)/shard_map/ppermute | solution.py:551
  263.0 21.3 %collective-permute-start.33 = (bf16[512,512]{1,0:T(8,128)(2,1)}, bf16[512,512]{1,0:T(8,128)(2,1)}, u32[]{:S(2)}, u32[]{:S(2)}) collective-permute-start(bf16[512,512]{1,0:T(8,128)(2,1)} %convolution_convert_fusion.3), channel_id=1, source_target_pairs={{0,4},{4,0},{8,12},{12,8},{16,20},{20,16},{24,28},{28,24},{1,5},{5... | collective-permute-start | bytes 1572872 | tf_op jit(solution)/shard_map/ppermute | solution.py:551
  273.6 19.4 %collective-permute-start.36 = (bf16[128,2048]{1,0:T(8,128)(2,1)}, bf16[128,2048]{1,0:T(8,128)(2,1)S(1)}, u32[]{:S(2)}, u32[]{:S(2)}) collective-permute-start(bf16[128,2048]{1,0:T(8,128)(2,1)} %fusion.62), channel_id=1, source_target_pairs={{0,8},{4,12},{8,0},{12,4},{16,24},{20,28},{24,16},{28,20},{1,9},{5... | collective-permute-start | bytes 1572872 | tf_op jit(solution)/shard_map/ppermute | solution.py:551
  275.2 35.8 %collective-permute-start.38 = (bf16[512,512]{1,0:T(8,128)(2,1)}, bf16[512,512]{1,0:T(8,128)(2,1)}, u32[]{:S(2)}, u32[]{:S(2)}) collective-permute-start(bf16[512,512]{1,0:T(8,128)(2,1)} %convolution_convert_fusion.2), channel_id=1, source_target_pairs={{0,4},{4,0},{8,12},{12,8},{16,20},{20,16},{24,28},{28,24},{1,5},{5... | collective-permute-start | bytes 1572872 | tf_op jit(solution)/shard_map/ppermute | solution.py:551
  282.7 50.6 %collective-permute-start.43 = (bf16[1024,512]{1,0:T(8,128)(2,1)}, bf16[1024,512]{1,0:T(8,128)(2,1)}, u32[]{:S(2)}, u32[]{:S(2)}) collective-permute-start(bf16[1024,512]{1,0:T(8,128)(2,1)} %pad_maximum_fusion.5), channel_id=1, source_target_pairs={{0,4},{4,0},{8,12},{12,8},{16,20},{20,16},{24,28},{28,24},{1,5},{5... | collective-permute-start | bytes 3145736 | tf_op jit(solution)/shard_map/ppermute | solution.py:551
  294.4 16.7 %collective-permute-start.39 = (f32[2,256,2048]{2,1,0:T(8,128)}, f32[2,256,2048]{2,1,0:T(8,128)}, u32[]{:S(2)}, u32[]{:S(2)}) collective-permute-start(f32[2,256,2048]{2,1,0:T(8,128)} %input_terms.2), channel_id=1, source_target_pairs={{0,1},{1,0},{2,3},{3,2},{4,5},{5,4},{6,7},{7,6},{8,9},{9,8},{10,11... | collective-permute-start | bytes 12582920 | tf_op jit(solution)/shard_map/ppermute | solution.py:551
  295.1 15.9 %collective-permute-start.40 = (bf16[128,2048]{1,0:T(8,128)(2,1)S(1)}, bf16[128,2048]{1,0:T(8,128)(2,1)}, u32[]{:S(2)}, u32[]{:S(2)}) collective-permute-start(bf16[128,2048]{1,0:T(8,128)(2,1)S(1)} %constant_dynamic-update-slice_fusion.56), channel_id=1, source_target_pairs={{0,2},{1,3},{2,0},{3,1},{4,6},{5,7},{6,4},{7,5},{8,10},{9,11},{10,... | collective-permute-start | bytes 1572872 | tf_op jit(solution)/shard_map/ppermute | solution.py:551
  301.5 31.8 %collective-permute-start.44 = (bf16[512,512]{1,0:T(8,128)(2,1)}, bf16[512,512]{1,0:T(8,128)(2,1)}, u32[]{:S(2)}, u32[]{:S(2)}) collective-permute-start(bf16[512,512]{1,0:T(8,128)(2,1)} %fusion.19), channel_id=1, source_target_pairs={{0,16},{4,20},{8,24},{12,28},{16,0},{20,4},{24,8},{28,12},{1,17},{... | collective-permute-start | bytes 1572872 | tf_op jit(solution)/shard_map/ppermute | solution.py:551
  321.4 25.1 %collective-permute-start.47 = (bf16[2,128,2048]{2,1,0:T(8,128)(2,1)S(1)}, bf16[2,128,2048]{2,1,0:T(8,128)(2,1)S(1)}, u32[]{:S(2)}, u32[]{:S(2)}) collective-permute-start(bf16[2,128,2048]{2,1,0:T(8,128)(2,1)S(1)} %dynamic-slice_convert_fusion.1), channel_id=1, source_target_pairs={{0,2},{1,3},{2,0},{3,1},{4,6},{5,7},{6,4},{7,5},{8,10},{9,11},{10,... | collective-permute-start | bytes 3145736 | tf_op jit(solution)/shard_map/ppermute | solution.py:551
  331.4 34.8 %collective-permute-start.48 = (bf16[512,512]{1,0:T(8,128)(2,1)S(1)}, bf16[512,512]{1,0:T(8,128)(2,1)S(1)}, u32[]{:S(2)}, u32[]{:S(2)}) collective-permute-start(bf16[512,512]{1,0:T(8,128)(2,1)S(1)} %fusion.20), channel_id=1, source_target_pairs={{0,16},{4,20},{8,24},{12,28},{16,0},{20,4},{24,8},{28,12},{1,17},{... | collective-permute-start | bytes 1572872 | tf_op jit(solution)/shard_map/ppermute | solution.py:551
  333.4 29.3 %collective-permute-start.46 = (f32[2,72,256]{2,1,0:T(8,128)S(1)}, f32[2,72,256]{2,1,0:T(8,128)S(1)}, u32[]{:S(2)}, u32[]{:S(2)}) collective-permute-start(f32[2,72,256]{2,1,0:T(8,128)S(1)} %slice.372), channel_id=1, source_target_pairs={{0,16},{4,20},{8,24},{12,28},{16,0},{20,4},{24,8},{28,12},{1,17},{... | collective-permute-start | bytes 442376 | tf_op jit(solution)/shard_map/ppermute | solution.py:551
  457.4 15.0 %collective-permute-start.67 = (bf16[256,2048]{1,0:T(8,128)(2,1)}, bf16[256,2048]{1,0:T(8,128)(2,1)}, u32[]{:S(2)}, u32[]{:S(2)}) collective-permute-start(bf16[256,2048]{1,0:T(8,128)(2,1)} %pad_maximum_fusion.10), channel_id=1, source_target_pairs={{0,1},{1,0},{2,3},{3,2},{4,5},{5,4},{6,7},{7,6},{8,9},{9,8},{10,11... | collective-permute-start | bytes 3145736 | tf_op jit(solution)/shard_map/ppermute | solution.py:551
  (143 other events, 1808.3 us)

commit v5 on v4

--- a/solution.py
+++ b/solution.py
@@ -959,20 +959,20 @@
     count = held.shape[0] // 2
     held = held[:count] + swap(held[count:], "dp", last_bit)
     output = join_halves(output, output_far, tensor_at // 2, 0)
+    held, both_kept, x_got, output = step(held, both_kept, x_got, output)
     output_far = swap(output, "tensor", 1)
-    held, both_kept, x_got, output_far = step(held, both_kept, x_got, output_far)
     for bit in reversed(dp_bits()[1:-1]):
         count = held.shape[0] // 2
         held = held[:count] + swap(held[count:], "dp", bit)
     x_terms = gradient_rows(normed_flat, x_low, 0, f32, both_kept[:part])
     z_terms = gradient_rows(normed_flat, z_low, 0, f32, both_kept[part:])
     x_mine, x_leaving = middle_sum(x_terms, x_got)
-    output = join_halves(output, output_far, core, 0)
     input_mine = input_kept + input_arriving.astype(f32)
     input_leaving = low_bits(input_mine[1])
-    held, z_terms, x_leaving, input_leaving = step(held, z_terms, x_leaving, input_leaving)
+    z_terms, x_leaving, input_leaving = step(z_terms, x_leaving, input_leaving)
 
     input_far = swap(input_leaving, "dp", PAIR)
+    output = join_halves(output, output_far, core, 0)
     small_far = swap(held[1], "dp", PAIR)
     z_mine, z_leaving = middle_sum(z_terms, z_got)
     z_leaving, small_far, input_far = step(z_leaving, small_far, input_far)
@@ -997,17 +997,20 @@
         return join_halves(values, jnp.zeros_like(values), half, values.ndim - 1)
 
     def packed_sum(pieces, axis_bits):
-        sizes = [piece.size for piece in pieces]
-        flat = jnp.concatenate([piece.reshape(-1) for piece in pieces])
-        fill = -flat.size % 128
-        flat = jnp.pad(flat, (0, fill)).reshape(-1, 128)
+        rows = []
+        for piece in pieces:
+            flat = piece.reshape(-1)
+            rows.append(jnp.pad(flat, (0, -flat.size % 128)).reshape(-1, 128))
+        total = jnp.concatenate(rows, axis=0)
         for axis, bits in axis_bits:
-            flat = add_over(flat, axis, bits)
-        flat = flat.reshape(-1)
+            total = add_over(total, axis, bits)
         result, at = [], 0
-        for piece, size in zip(pieces, sizes):
-            result.append(flat[at : at + size].reshape(piece.shape))
-            at += size
+        for piece, row in zip(pieces, rows):
+            part = total[at : at + row.shape[0]]
+            if piece.size % 128:
+                part = part[0, : piece.size]
+            result.append(part.reshape(piece.shape))
+            at += row.shape[0]
         return result
 
     norm_sum, convbc_sum = packed_sum(
@@ -1035,24 +1038,24 @@
         convbc_total,
         gated_total,
         convx_total,
-        head_total,
         z_col_sum,
         x_col_sum,
+        out_col_sum,
         bc_col_sum,
         dt_col_sum,
-        out_col_sum,
+        head_total,
     ) = packed_sum(
         [
             norm_sum,
             convbc_sum,
             in_half(gated_slot),
             in_half(convx_slot),
-            in_half(head_slot),
             jnp.sum(z_square, axis=0),
             jnp.sum(x_square, axis=0),
+            jnp.sum(out_square, axis=0),
             jnp.sum(bc_square, axis=0),
             jnp.sum(dt_square, axis=0),
-            jnp.sum(out_square, axis=0),
+            in_half(head_slot),
         ],
         [("dp", dp_bits())],
     )
@@ -1082,8 +1085,8 @@
     dt_unit = dt_share * lax.rsqrt(dt_rows_new[:, None] * dt_cols_new[None, :])
     out_unit = out_share * lax.rsqrt(out_rows_new[:, None] * out_cols_new[None, :])
     tensor_count = lax.axis_size("tensor")
-    unit_sums = jnp.stack(
-        [
+    scalars = (
+        (
             jnp.sum(z_unit * z_unit),
             jnp.sum(x_unit * x_unit),
             jnp.sum(bc_unit * bc_unit) / tensor_count,
@@ -1092,9 +1095,12 @@
             jnp.sum(gated_unit * gated_unit) / data_count,
             jnp.sum(convx_unit * convx_unit) / data_count,
             jnp.sum(head_unit * head_unit) / data_count,
-        ]
-    )
-    unit_sums = jnp.broadcast_to(unit_sums[:, None], (8, 128))
+        )
+    )
+    places = lax.broadcasted_iota(jnp.int32, (8, 128), 0)
+    unit_sums = jnp.zeros((8, 128), f32)
+    for place, value in enumerate(scalars):
+        unit_sums = jnp.where(places == place, value, unit_sums)
     unit_sums = add_over(unit_sums, "tensor", (1, 2))
     unit_sums, input_grad, output = step(unit_sums, input_grad, output)
     input_far = swap(input_grad, "tensor", 2)

time: 484 us -> 497 us (1.027)
  starting transfers between devices: 66.8 us -> 50.7 us
  waiting for transfers between devices: 134 us -> 145 us
  other arithmetic: 84.5 us -> 95.3 us
  local copies, waits for them, and re-layouts: 71.9 us -> 79.2 us
    ppermute x68, starting transfers between devices: 66.8 us -> 50.7 us  [swap(): lax.ppermute(value, axis, [(place, place ^ bit) for place in range(size)])]
    ppermute x68, waiting for transfers between devices: 134 us -> 145 us  [swap(): lax.ppermute(value, axis, [(place, place ^ bit) for place in range(size)])]
    unnamed x302 -> x280, local copies, waits for them, and re-layouts: 45.8 us -> 52.8 us
  transfers between devices with their start and end apart: 68 -> 68, of which waited for: 29 -> 34; matrix products, arithmetic and copies ran while one was open for 31% -> 33% of each run, Pallas kernels for 13% -> 13%
where the time goes in v5:
time: 497 us; the launch traced here: 489 us
  waiting for transfers between devices  145 us (29%)
  other arithmetic  95.3 us (19%)
  local copies, waits for them, and re-layouts  79.2 us (16%)
  Pallas kernels  61.7 us (12%)
  starting transfers between devices  50.7 us (10%)
  matrix products  43.7 us (9%)
  between operations  13.5 us (3%)
    ppermute x68, waiting for transfers between devices, swap(): lax.ppermute(value, axis, [(place, place ^ bit) for place in range(size)])  145 us
    unnamed x280, local copies, waits for them, and re-layouts  52.8 us
    ppermute x68, starting transfers between devices, swap(): lax.ppermute(value, axis, [(place, place ^ bit) for place in range(size)])  50.7 us
    pallas_call x2, Pallas kernels, mixer_backward(): pl.pallas_call(body, grid=(1, pairs), in_specs=common_specs(slot, length)...  31 us
    dot_general x14, matrix products, tokens_out(): lax.dot_general(left, right, (((0,), (0,)), ((), ())), preferred_element_...  25.2 us
    pallas_call x1, Pallas kernels, mixer_forward(): pl.pallas_call(forward_body, grid=(slots, pairs), in_specs=common_specs(0...  16.4 us
    pallas_call x2, Pallas kernels, input_terms(): pl.pallas_call(input_body, grid_spec=pltpu.PrefetchScalarGridSpec(num_sca...  14.2 us
    select_n x18, other arithmetic, join_halves(): jnp.where(half == 0, mine, other)  12.8 us
  transfers between devices with their start and end apart: 68, of which 34 were waited for; matrix products, arithmetic and copies ran while one was open for 33% of the time, Pallas kernels for 13%

profile of v5, /device:TPU:0, one launch (start us, length us, event | category | flops | bytes accessed | tf_op | source)
XLA Modules:
  0.0 488.9 jit_solution(2420836929761986602)
XLA Ops:
  3.0 3.1 collective-permute-start
  12.2 3.2 collective-permute-done.1
  54.0 8.8 %collective-permute-done.6 = bf16[4,160,128]{2,1,0:T(8,128)(2,1)S(1)} collective-permute-done((bf16[4,160,128]{2,1,0:T(8,128)(2,1)S(1)}, bf16[4,160,128]{2,1,0:T(8,128)(2,1)S(1)}, u32[]{:S(2)}, u32[]{:S(2)}) %collective-permute-start.6) | collective-permute-done | bytes 163872 | tf_op jit(solution)/shard_map/ppermute | solution.py:551
  73.3 8.3 %collective-permute-done.11 = bf16[128,2048]{1,0:T(8,128)(2,1)S(1)} collective-permute-done((bf16[128,2048]{1,0:T(8,128)(2,1)}, bf16[128,2048]{1,0:T(8,128)(2,1)S(1)}, u32[]{:S(2)}, u32[]{:S(2)}) %collective-permute-start.11) | collective-permute-done | bytes 524320 | tf_op jit(solution)/shard_map/ppermute | solution.py:551
  83.8 12.4 %collective-permute-done.9 = bf16[512,512]{1,0:T(8,128)(2,1)S(1)} collective-permute-done((bf16[512,512]{1,0:T(8,128)(2,1)S(1)}, bf16[512,512]{1,0:T(8,128)(2,1)S(1)}, u32[]{:S(2)}, u32[]{:S(2)}) %collective-permute-start.9) | collective-permute-done | bytes 524320 | tf_op jit(solution)/shard_map/ppermute | solution.py:551
  106.7 5.0 %collective-permute-done.17 = bf16[8,128,256]{2,1,0:T(8,128)(2,1)} collective-permute-done((bf16[8,128,256]{2,1,0:T(8,128)(2,1)S(1)}, bf16[8,128,256]{2,1,0:T(8,128)(2,1)}, u32[]{:S(2)}, u32[]{:S(2)}) %collective-permute-start.17) | collective-permute-done | bytes 524320 | tf_op jit(solution)/shard_map/ppermute | solution.py:551
  124.4 3.6 fusion.13.x_ref.refs_6_
  128.1 3.6 fusion.11.z_ref.refs_7_
  137.5 6.7 %collective-permute-done.18 = bf16[128,2048]{1,0:T(8,128)(2,1)S(1)} collective-permute-done((bf16[128,2048]{1,0:T(8,128)(2,1)S(1)}, bf16[128,2048]{1,0:T(8,128)(2,1)S(1)}, u32[]{:S(2)}, u32[]{:S(2)}) %collective-permute-start.18) | collective-permute-done | bytes 524320 | tf_op jit(solution)/shard_map/ppermute | solution.py:551
  149.0 16.4 %mixer_forward.1 = (bf16[2,512,512]{2,1,0:T(8,128)(2,1)}, f32[2,512,512]{2,1,0:T(8,128)}, f32[2,512,128]{2,1,0:T(8,128)}) custom-call(f32[2,512,8]{2,1,0:T(8,128)} %copy.122.marks_ref.refs_0_, f32[2,8,512]{2,1,0:T(8,128)} %broadcast_in_dim.91.row_ref.refs_1_, f32[2,512,256]{2,1,0:T(8,128)} %fusion.150.bc_ref.refs_2_, f32[2,512,128]{2,1,0:T(8,128)} %fusion.64.dt_ref.refs_3_, ...), custom_call_target="tpu_custom_call" | custom-call | flops 16000000000 | bytes 1048576 | tf_op jit(solution)/shard_map/mixer_forward/pallas_call | solution.py:387
  190.0 2.9 multiply_convert_fusion
  198.7 3.8 fusion.2.refs_10_
  203.4 15.6 %mixer_backward.2 = (bf16[2,512,512]{2,1,0:T(8,128)(2,1)}, bf16[2,512,512]{2,1,0:T(8,128)(2,1)}, f32[2,512,256]{2,1,0:T(8,128)}, f32[2,512,128]{2,1,0:T(8,128)},...) custom-call(f32[2,512,8]{2,1,0:T(8,128)} %copy.122.marks_ref.refs_0_, ...), custom_call_target="tpu_custom_call" | custom-call | flops 16000000000 | bytes 1048576 | tf_op jit(solution)/shard_map/mixer_backward/pallas_call | solution.py:412
  221.8 3.4 convert_add_fusion
  229.1 15.4 %mixer_backward.3 = (bf16[2,512,512]{2,1,0:T(8,128)(2,1)}, bf16[2,512,512]{2,1,0:T(8,128)(2,1)}, f32[2,512,256]{2,1,0:T(8,128)}, f32[2,512,128]{2,1,0:T(8,128)},...) custom-call(f32[2,512,8]{2,1,0:T(8,128)} %copy.122.marks_ref.refs_0_, ...), custom_call_target="tpu_custom_call", output_to_operand_aliasing={{0}: (12, {}), {1}: (13, {}), {2}: (14, {}), {3}: (15, {}),... | custom-call | flops 16000000000 | bytes 1048576 | tf_op jit(solution)/shard_map/mixer_backward/pallas_call | solution.py:412
  248.5 3.0 convolution_bitcast_fusion
  253.8 3.1 convolution_convert_fusion.3
  256.9 12.3 %collective-permute-done.31 = bf16[512,512]{1,0:T(8,128)(2,1)} collective-permute-done((bf16[512,512]{1,0:T(8,128)(2,1)}, bf16[512,512]{1,0:T(8,128)(2,1)}, u32[]{:S(2)}, u32[]{:S(2)}) %collective-permute-start.31) | collective-permute-done | bytes 524320 | tf_op jit(solution)/shard_map/ppermute | solution.py:551
  285.6 7.0 %input_terms.2 = f32[2,256,2048]{2,1,0:T(8,128)} custom-call(s32[1]{0:T(128)} %bitcast.60.place_ref, bf16[2,2,256,512]{3,2,1,0:T(8,128)(2,1)} %bitcast.393, bf16[2,2,256,512]{3,2,1,0:T(8,128)(2,1)} %bitcast.400, bf16[2,2,256,128]{3,2,1,0:T(8,128)(2,1)} %bitcast.343, bf16[2048,512]{1,0:T(8,128)(2,1)} %copy-done.59, ...), custom_call_target="tpu_custom_call" | custom-call | flops 6000000000 | bytes 1048576 | tf_op jit(solution)/shard_map/input_terms/pallas_call | solution.py:480
  295.4 8.6 %collective-permute-done.36 = bf16[128,2048]{1,0:T(8,128)(2,1)S(1)} collective-permute-done((bf16[128,2048]{1,0:T(8,128)(2,1)}, bf16[128,2048]{1,0:T(8,128)(2,1)S(1)}, u32[]{:S(2)}, u32[]{:S(2)}) %collective-permute-start.36) | collective-permute-done | bytes 524320 | tf_op jit(solution)/shard_map/ppermute | solution.py:551
  309.5 2.9 fusion.19
  313.1 7.2 %input_terms.3 = f32[2,256,2048]{2,1,0:T(8,128)} custom-call(s32[1]{0:T(128)} %bitcast.66.place_ref, bf16[2,2,256,512]{3,2,1,0:T(8,128)(2,1)} %bitcast.394, bf16[2,2,256,512]{3,2,1,0:T(8,128)(2,1)} %bitcast.401, bf16[2,2,256,128]{3,2,1,0:T(8,128)(2,1)} %bitcast.344, bf16[2048,512]{1,0:T(8,128)(2,1)} %copy-done.59, ...), custom_call_target="tpu_custom_call" | custom-call | flops 6000000000 | bytes 1048576 | tf_op jit(solution)/shard_map/input_terms/pallas_call | solution.py:480
  320.7 4.2 add.832
  335.9 5.5 %collective-permute-done.42 = f32[4,72,256]{2,1,0:T(8,128)S(1)} collective-permute-done((f32[4,72,256]{2,1,0:T(8,128)S(1)}, f32[4,72,256]{2,1,0:T(8,128)S(1)}, u32[]{:S(2)}, u32[]{:S(2)}) %collective-permute-start.42) | collective-permute-done | bytes 294944 | tf_op jit(solution)/shard_map/ppermute | solution.py:551
  341.5 8.6 %collective-permute-done.44 = bf16[512,512]{1,0:T(8,128)(2,1)} collective-permute-done((bf16[512,512]{1,0:T(8,128)(2,1)}, bf16[512,512]{1,0:T(8,128)(2,1)}, u32[]{:S(2)}, u32[]{:S(2)}) %collective-permute-start.44) | collective-permute-done | bytes 524320 | tf_op jit(solution)/shard_map/ppermute | solution.py:551
  353.6 13.9 %collective-permute-done.47 = f32[2,72,256]{2,1,0:T(8,128)S(1)} collective-permute-done((f32[2,72,256]{2,1,0:T(8,128)S(1)}, f32[2,72,256]{2,1,0:T(8,128)S(1)}, u32[]{:S(2)}, u32[]{:S(2)}) %collective-permute-start.47) | collective-permute-done | bytes 147488 | tf_op jit(solution)/shard_map/ppermute | solution.py:551
  372.8 10.3 %collective-permute-done.49 = bf16[128,2048]{1,0:T(8,128)(2,1)S(1)} collective-permute-done((bf16[128,2048]{1,0:T(8,128)(2,1)S(1)}, bf16[128,2048]{1,0:T(8,128)(2,1)S(1)}, u32[]{:S(2)}, u32[]{:S(2)}) %collective-permute-start.49) | collective-permute-done | bytes 524320 | tf_op jit(solution)/shard_map/ppermute | solution.py:551
  392.4 4.3 collective-permute-done.53
  400.2 2.9 collective-permute-done.55
  414.5 3.8 collective-permute-done.57
  419.5 2.9 collective-permute-done.58
  438.6 3.3 select_select_fusion
  (672 shorter events, 259.0 us)
Async XLA Ops:
  17.0 28.4 %collective-permute-start.2 = (bf16[512,512]{1,0:T(8,128)(2,1)}, bf16[512,512]{1,0:T(8,128)(2,1)}, u32[]{:S(2)}, u32[]{:S(2)}) collective-permute-start(bf16[512,512]{1,0:T(8,128)(2,1)} %get-tuple-element.624), channel_id=1, source_target_pairs={{0,16},{4,20},{8,24},{12,28},{16,0},{20,4},{24,8},{28,12},{1,17},{... | collective-permute-start | bytes 1572872 | tf_op jit(solution)/shard_map/ppermute | solution.py:551
  19.6 25.8 %collective-permute-start.3 = (bf16[512,512]{1,0:T(8,128)(2,1)}, bf16[512,512]{1,0:T(8,128)(2,1)}, u32[]{:S(2)}, u32[]{:S(2)}) collective-permute-start(bf16[512,512]{1,0:T(8,128)(2,1)} %get-tuple-element.624), channel_id=1, source_target_pairs={{0,4},{4,0},{8,12},{12,8},{16,20},{20,16},{24,28},{28,24},{1,5},{5... | collective-permute-start | bytes 1572872 | tf_op jit(solution)/shard_map/ppermute | solution.py:551
  22.1 23.3 %collective-permute-start.4 = (bf16[2,160,128]{2,1,0:T(8,128)(2,1)S(1)}, bf16[2,160,128]{2,1,0:T(8,128)(2,1)S(1)}, u32[]{:S(2)}, u32[]{:S(2)}) collective-permute-start(bf16[2,160,128]{2,1,0:T(8,128)(2,1)S(1)} %pad_maximum_fusion.17), channel_id=1, source_target_pairs={{0,16},{4,20},{8,24},{12,28},{16,0},{20,4},{24,8},{28,12},{1,17},{... | collective-permute-start | bytes 245768 | tf_op jit(solution)/shard_map/ppermute | solution.py:551
  45.4 20.9 %collective-permute-start.5 = (bf16[512,512]{1,0:T(8,128)(2,1)}, bf16[512,512]{1,0:T(8,128)(2,1)}, u32[]{:S(2)}, u32[]{:S(2)}) collective-permute-start(bf16[512,512]{1,0:T(8,128)(2,1)} %collective-permute-done.2), channel_id=1, source_target_pairs={{0,4},{4,0},{8,12},{12,8},{16,20},{20,16},{24,28},{28,24},{1,5},{5... | collective-permute-start | bytes 1572872 | tf_op jit(solution)/shard_map/ppermute | solution.py:551
  46.8 19.5 %collective-permute-start.8 = (bf16[128,2048]{1,0:T(8,128)(2,1)}, bf16[128,2048]{1,0:T(8,128)(2,1)}, u32[]{:S(2)}, u32[]{:S(2)}) collective-permute-start(bf16[128,2048]{1,0:T(8,128)(2,1)} %get-tuple-element.200), channel_id=1, source_target_pairs={{0,8},{4,12},{8,0},{12,4},{16,24},{20,28},{24,16},{28,20},{1,9},{5... | collective-permute-start | bytes 1572872 | tf_op jit(solution)/shard_map/ppermute | solution.py:551
  48.2 18.1 %collective-permute-start.7 = (bf16[256,512]{1,0:T(8,128)(2,1)}, bf16[256,512]{1,0:T(8,128)(2,1)}, u32[]{:S(2)}, u32[]{:S(2)}) collective-permute-start(bf16[256,512]{1,0:T(8,128)(2,1)} %get-tuple-element.199), channel_id=1, source_target_pairs={{0,8},{4,12},{8,0},{12,4},{16,24},{20,28},{24,16},{28,20},{1,9},{5... | collective-permute-start | bytes 786440 | tf_op jit(solution)/shard_map/ppermute | solution.py:551
  70.3 25.9 %collective-permute-start.9 = (bf16[512,512]{1,0:T(8,128)(2,1)S(1)}, bf16[512,512]{1,0:T(8,128)(2,1)S(1)}, u32[]{:S(2)}, u32[]{:S(2)}) collective-permute-start(bf16[512,512]{1,0:T(8,128)(2,1)S(1)} %get-tuple-element.620), channel_id=1, source_target_pairs={{0,16},{4,20},{8,24},{12,28},{16,0},{20,4},{24,8},{28,12},{1,17},{... | collective-permute-start | bytes 1572872 | tf_op jit(solution)/shard_map/ppermute | solution.py:551
  70.8 25.4 %collective-permute-start.10 = (bf16[512,512]{1,0:T(8,128)(2,1)S(1)}, bf16[512,512]{1,0:T(8,128)(2,1)S(1)}, u32[]{:S(2)}, u32[]{:S(2)}) collective-permute-start(bf16[512,512]{1,0:T(8,128)(2,1)S(1)} %get-tuple-element.620), channel_id=1, source_target_pairs={{0,4},{4,0},{8,12},{12,8},{16,20},{20,16},{24,28},{28,24},{1,5},{5... | collective-permute-start | bytes 1572872 | tf_op jit(solution)/shard_map/ppermute | solution.py:551
  96.2 16.8 %collective-permute-start.16 = (bf16[256,2048]{1,0:T(8,128)(2,1)}, bf16[256,2048]{1,0:T(8,128)(2,1)}, u32[]{:S(2)}, u32[]{:S(2)}) collective-permute-start(bf16[256,2048]{1,0:T(8,128)(2,1)} %pad_maximum_fusion.2), channel_id=1, source_target_pairs={{0,1},{1,0},{2,3},{3,2},{4,5},{5,4},{6,7},{7,6},{8,9},{9,8},{10,11... | collective-permute-start | bytes 3145736 | tf_op jit(solution)/shard_map/ppermute | solution.py:551
  101.5 18.0 %collective-permute-start.13 = (bf16[512,512]{1,0:T(8,128)(2,1)}, bf16[512,512]{1,0:T(8,128)(2,1)S(1)}, u32[]{:S(2)}, u32[]{:S(2)}) collective-permute-start(bf16[512,512]{1,0:T(8,128)(2,1)} %copy-done.44), channel_id=1, source_target_pairs={{0,4},{4,0},{8,12},{12,8},{16,20},{20,16},{24,28},{28,24},{1,5},{5... | collective-permute-start | bytes 1572872 | tf_op jit(solution)/shard_map/ppermute | solution.py:551
  102.0 17.5 %collective-permute-start.14 = (bf16[256,512]{1,0:T(8,128)(2,1)}, bf16[256,512]{1,0:T(8,128)(2,1)S(1)}, u32[]{:S(2)}, u32[]{:S(2)}) collective-permute-start(bf16[256,512]{1,0:T(8,128)(2,1)} %get-tuple-element.213), channel_id=1, source_target_pairs={{0,8},{4,12},{8,0},{12,4},{16,24},{20,28},{24,16},{28,20},{1,9},{5... | collective-permute-start | bytes 786440 | tf_op jit(solution)/shard_map/ppermute | solution.py:551
  102.0 19.4 %collective-permute-start.15 = (bf16[128,2048]{1,0:T(8,128)(2,1)}, bf16[128,2048]{1,0:T(8,128)(2,1)S(1)}, u32[]{:S(2)}, u32[]{:S(2)}) collective-permute-start(bf16[128,2048]{1,0:T(8,128)(2,1)} %get-tuple-element.214), channel_id=1, source_target_pairs={{0,8},{4,12},{8,0},{12,4},{16,24},{20,28},{24,16},{28,20},{1,9},{5... | collective-permute-start | bytes 1572872 | tf_op jit(solution)/shard_map/ppermute | solution.py:551
  122.3 25.2 %collective-permute-start.20 = (bf16[512,512]{1,0:T(8,128)(2,1)}, bf16[512,512]{1,0:T(8,128)(2,1)}, u32[]{:S(2)}, u32[]{:S(2)}) collective-permute-start(bf16[512,512]{1,0:T(8,128)(2,1)} %get-tuple-element.615), channel_id=1, source_target_pairs={{0,16},{4,20},{8,24},{12,28},{16,0},{20,4},{24,8},{28,12},{1,17},{... | collective-permute-start | bytes 1572872 | tf_op jit(solution)/shard_map/ppermute | solution.py:551
  122.9 45.8 %collective-permute-start.21 = (bf16[512,512]{1,0:T(8,128)(2,1)}, bf16[512,512]{1,0:T(8,128)(2,1)}, u32[]{:S(2)}, u32[]{:S(2)}) collective-permute-start(bf16[512,512]{1,0:T(8,128)(2,1)} %get-tuple-element.615), channel_id=1, source_target_pairs={{0,4},{4,0},{8,12},{12,8},{16,20},{20,16},{24,28},{28,24},{1,5},{5... | collective-permute-start | bytes 1572872 | tf_op jit(solution)/shard_map/ppermute | solution.py:551
  146.1 26.3 %collective-permute-start.19 = (bf16[256,2048]{1,0:T(8,128)(2,1)}, bf16[256,2048]{1,0:T(8,128)(2,1)}, u32[]{:S(2)}, u32[]{:S(2)}) collective-permute-start(bf16[256,2048]{1,0:T(8,128)(2,1)} %pad_maximum_fusion.4), channel_id=1, source_target_pairs={{0,1},{1,0},{2,3},{3,2},{4,5},{5,4},{6,7},{7,6},{8,9},{9,8},{10,11... | collective-permute-start | bytes 3145736 | tf_op jit(solution)/shard_map/ppermute | solution.py:551
  147.5 23.1 %collective-permute-start.22 = (bf16[512,512]{1,0:T(8,128)(2,1)}, bf16[512,512]{1,0:T(8,128)(2,1)}, u32[]{:S(2)}, u32[]{:S(2)}) collective-permute-start(bf16[512,512]{1,0:T(8,128)(2,1)} %collective-permute-done.20), channel_id=1, source_target_pairs={{0,4},{4,0},{8,12},{12,8},{16,20},{20,16},{24,28},{28,24},{1,5},{5... | collective-permute-start | bytes 1572872 | tf_op jit(solution)/shard_map/ppermute | solution.py:551
  186.3 16.2 %collective-permute-start.26 = (bf16[2,256,2048]{2,1,0:T(8,128)(2,1)S(1)}, bf16[2,256,2048]{2,1,0:T(8,128)(2,1)}, u32[]{:S(2)}, u32[]{:S(2)}) collective-permute-start(bf16[2,256,2048]{2,1,0:T(8,128)(2,1)S(1)} %dynamic-slice_convert_fusion), channel_id=1, source_target_pairs={{0,1},{1,0},{2,3},{3,2},{4,5},{5,4},{6,7},{7,6},{8,9},{9,8},{10,11... | collective-permute-start | bytes 6291464 | tf_op jit(solution)/shard_map/ppermute | solution.py:551
  194.5 24.5 %collective-permute-start.27 = (bf16[512,512]{1,0:T(8,128)(2,1)}, bf16[512,512]{1,0:T(8,128)(2,1)S(1)}, u32[]{:S(2)}, u32[]{:S(2)}) collective-permute-start(bf16[512,512]{1,0:T(8,128)(2,1)} %convolution_convert_fusion.5), channel_id=1, source_target_pairs={{0,4},{4,0},{8,12},{12,8},{16,20},{20,16},{24,28},{28,24},{1,5},{5... | collective-permute-start | bytes 1572872 | tf_op jit(solution)/shard_map/ppermute | solution.py:551
  196.6 55.0 %collective-permute-start.28 = (bf16[512,512]{1,0:T(8,128)(2,1)}, bf16[512,512]{1,0:T(8,128)(2,1)}, u32[]{:S(2)}, u32[]{:S(2)}) collective-permute-start(bf16[512,512]{1,0:T(8,128)(2,1)} %convolution_convert_fusion.4), channel_id=1, source_target_pairs={{0,4},{4,0},{8,12},{12,8},{16,20},{20,16},{24,28},{28,24},{1,5},{5... | collective-permute-start | bytes 1572872 | tf_op jit(solution)/shard_map/ppermute | solution.py:551
  227.4 24.1 %collective-permute-start.29 = (bf16[2,128,2048]{2,1,0:T(8,128)(2,1)S(1)}, bf16[2,128,2048]{2,1,0:T(8,128)(2,1)}, u32[]{:S(2)}, u32[]{:S(2)}) collective-permute-start(bf16[2,128,2048]{2,1,0:T(8,128)(2,1)S(1)} %dynamic-slice_convert_fusion.2), channel_id=1, source_target_pairs={{0,2},{1,3},{2,0},{3,1},{4,6},{5,7},{6,4},{7,5},{8,10},{9,11},{10,... | collective-permute-start | bytes 3145736 | tf_op jit(solution)/shard_map/ppermute | solution.py:551
  245.9 23.3 %collective-permute-start.31 = (bf16[512,512]{1,0:T(8,128)(2,1)}, bf16[512,512]{1,0:T(8,128)(2,1)}, u32[]{:S(2)}, u32[]{:S(2)}) collective-permute-start(bf16[512,512]{1,0:T(8,128)(2,1)} %fusion.18), channel_id=1, source_target_pairs={{0,16},{4,20},{8,24},{12,28},{16,0},{20,4},{24,8},{28,12},{1,17},{... | collective-permute-start | bytes 1572872 | tf_op jit(solution)/shard_map/ppermute | solution.py:551
  251.6 17.5 %collective-permute-start.30 = (f32[2,256,256]{2,1,0:T(8,128)S(1)}, f32[2,256,256]{2,1,0:T(8,128)S(1)}, u32[]{:S(2)}, u32[]{:S(2)}) collective-permute-start(f32[2,256,256]{2,1,0:T(8,128)S(1)} %constant_dynamic-slice_fusion.3), channel_id=1, source_target_pairs={{0,1},{1,0},{2,3},{3,2},{4,5},{5,4},{6,7},{7,6},{8,9},{9,8},{10,11... | collective-permute-start | bytes 1572872 | tf_op jit(solution)/shard_map/ppermute | solution.py:551
  275.0 19.3 %collective-permute-start.33 = (bf16[512,512]{1,0:T(8,128)(2,1)}, bf16[512,512]{1,0:T(8,128)(2,1)}, u32[]{:S(2)}, u32[]{:S(2)}) collective-permute-start(bf16[512,512]{1,0:T(8,128)(2,1)} %convolution_convert_fusion.3), channel_id=1, source_target_pairs={{0,4},{4,0},{8,12},{12,8},{16,20},{20,16},{24,28},{28,24},{1,5},{5... | collective-permute-start | bytes 1572872 | tf_op jit(solution)/shard_map/ppermute | solution.py:551
  285.1 18.9 %collective-permute-start.36 = (bf16[128,2048]{1,0:T(8,128)(2,1)}, bf16[128,2048]{1,0:T(8,128)(2,1)S(1)}, u32[]{:S(2)}, u32[]{:S(2)}) collective-permute-start(bf16[128,2048]{1,0:T(8,128)(2,1)} %fusion.62), channel_id=1, source_target_pairs={{0,8},{4,12},{8,0},{12,4},{16,24},{20,28},{24,16},{28,20},{1,9},{5... | collective-permute-start | bytes 1572872 | tf_op jit(solution)/shard_map/ppermute | solution.py:551
  285.1 35.2 %collective-permute-start.38 = (bf16[512,512]{1,0:T(8,128)(2,1)}, bf16[512,512]{1,0:T(8,128)(2,1)}, u32[]{:S(2)}, u32[]{:S(2)}) collective-permute-start(bf16[512,512]{1,0:T(8,128)(2,1)} %convolution_convert_fusion.2), channel_id=1, source_target_pairs={{0,4},{4,0},{8,12},{12,8},{16,20},{20,16},{24,28},{28,24},{1,5},{5... | collective-permute-start | bytes 1572872 | tf_op jit(solution)/shard_map/ppermute | solution.py:551
  292.6 48.8 %collective-permute-start.43 = (bf16[1024,512]{1,0:T(8,128)(2,1)}, bf16[1024,512]{1,0:T(8,128)(2,1)}, u32[]{:S(2)}, u32[]{:S(2)}) collective-permute-start(bf16[1024,512]{1,0:T(8,128)(2,1)} %pad_maximum_fusion.5), channel_id=1, source_target_pairs={{0,4},{4,0},{8,12},{12,8},{16,20},{20,16},{24,28},{28,24},{1,5},{5... | collective-permute-start | bytes 3145736 | tf_op jit(solution)/shard_map/ppermute | solution.py:551
  305.4 15.3 %collective-permute-start.39 = (f32[2,256,2048]{2,1,0:T(8,128)}, f32[2,256,2048]{2,1,0:T(8,128)}, u32[]{:S(2)}, u32[]{:S(2)}) collective-permute-start(f32[2,256,2048]{2,1,0:T(8,128)} %input_terms.2), channel_id=1, source_target_pairs={{0,1},{1,0},{2,3},{3,2},{4,5},{5,4},{6,7},{7,6},{8,9},{9,8},{10,11... | collective-permute-start | bytes 12582920 | tf_op jit(solution)/shard_map/ppermute | solution.py:551
  312.5 37.6 %collective-permute-start.44 = (bf16[512,512]{1,0:T(8,128)(2,1)}, bf16[512,512]{1,0:T(8,128)(2,1)}, u32[]{:S(2)}, u32[]{:S(2)}) collective-permute-start(bf16[512,512]{1,0:T(8,128)(2,1)} %fusion.19), channel_id=1, source_target_pairs={{0,16},{4,20},{8,24},{12,28},{16,0},{20,4},{24,8},{28,12},{1,17},{... | collective-permute-start | bytes 1572872 | tf_op jit(solution)/shard_map/ppermute | solution.py:551
  329.3 38.7 %collective-permute-start.46 = (bf16[512,512]{1,0:T(8,128)(2,1)S(1)}, bf16[512,512]{1,0:T(8,128)(2,1)S(1)}, u32[]{:S(2)}, u32[]{:S(2)}) collective-permute-start(bf16[512,512]{1,0:T(8,128)(2,1)S(1)} %fusion.20), channel_id=1, source_target_pairs={{0,16},{4,20},{8,24},{12,28},{16,0},{20,4},{24,8},{28,12},{1,17},{... | collective-permute-start | bytes 1572872 | tf_op jit(solution)/shard_map/ppermute | solution.py:551
  333.9 33.7 %collective-permute-start.45 = (bf16[2,128,2048]{2,1,0:T(8,128)(2,1)S(1)}, bf16[2,128,2048]{2,1,0:T(8,128)(2,1)S(1)}, u32[]{:S(2)}, u32[]{:S(2)}) collective-permute-start(bf16[2,128,2048]{2,1,0:T(8,128)(2,1)S(1)} %dynamic-slice_convert_fusion.1), channel_id=1, source_target_pairs={{0,2},{1,3},{2,0},{3,1},{4,6},{5,7},{6,4},{7,5},{8,10},{9,11},{10,... | collective-permute-start | bytes 3145736 | tf_op jit(solution)/shard_map/ppermute | solution.py:551
  350.1 17.4 %collective-permute-start.47 = (f32[2,72,256]{2,1,0:T(8,128)S(1)}, f32[2,72,256]{2,1,0:T(8,128)S(1)}, u32[]{:S(2)}, u32[]{:S(2)}) collective-permute-start(f32[2,72,256]{2,1,0:T(8,128)S(1)} %slice.368), channel_id=1, source_target_pairs={{0,16},{4,20},{8,24},{12,28},{16,0},{20,4},{24,8},{28,12},{1,17},{... | collective-permute-start | bytes 442376 | tf_op jit(solution)/shard_map/ppermute | solution.py:551
  353.5 16.8 %collective-permute-start.51 = (bf16[256,2048]{1,0:T(8,128)(2,1)S(1)}, bf16[256,2048]{1,0:T(8,128)(2,1)S(1)}, u32[]{:S(2)}, u32[]{:S(2)}) collective-permute-start(bf16[256,2048]{1,0:T(8,128)(2,1)S(1)} %pad_maximum_fusion.7), channel_id=1, source_target_pairs={{0,1},{1,0},{2,3},{3,2},{4,5},{5,4},{6,7},{7,6},{8,9},{9,8},{10,11... | collective-permute-start | bytes 3145736 | tf_op jit(solution)/shard_map/ppermute | solution.py:551
  (138 other events, 1892.3 us)

commit v6 on v4

--- a/solution.py
+++ b/solution.py
@@ -959,20 +959,20 @@
     count = held.shape[0] // 2
     held = held[:count] + swap(held[count:], "dp", last_bit)
     output = join_halves(output, output_far, tensor_at // 2, 0)
+    held, both_kept, x_got, output = step(held, both_kept, x_got, output)
     output_far = swap(output, "tensor", 1)
-    held, both_kept, x_got, output_far = step(held, both_kept, x_got, output_far)
     for bit in reversed(dp_bits()[1:-1]):
         count = held.shape[0] // 2
         held = held[:count] + swap(held[count:], "dp", bit)
     x_terms = gradient_rows(normed_flat, x_low, 0, f32, both_kept[:part])
     z_terms = gradient_rows(normed_flat, z_low, 0, f32, both_kept[part:])
     x_mine, x_leaving = middle_sum(x_terms, x_got)
-    output = join_halves(output, output_far, core, 0)
     input_mine = input_kept + input_arriving.astype(f32)
     input_leaving = low_bits(input_mine[1])
-    held, z_terms, x_leaving, input_leaving = step(held, z_terms, x_leaving, input_leaving)
+    z_terms, x_leaving, input_leaving = step(z_terms, x_leaving, input_leaving)
 
     input_far = swap(input_leaving, "dp", PAIR)
+    output = join_halves(output, output_far, core, 0)
     small_far = swap(held[1], "dp", PAIR)
     z_mine, z_leaving = middle_sum(z_terms, z_got)
     z_leaving, small_far, input_far = step(z_leaving, small_far, input_far)

time: 484 us -> 477 us (0.986)
  starting transfers between devices: 66.8 us -> 56.4 us
    ppermute x68, starting transfers between devices: 66.8 us -> 56.4 us  [swap(): lax.ppermute(value, axis, [(place, place ^ bit) for place in range(size)])]
    unnamed x302 -> x298, local copies, waits for them, and re-layouts: 45.8 us -> 45.2 us
  transfers between devices with their start and end apart: 68 -> 68, of which waited for: 29 -> 32; matrix products, arithmetic and copies ran while one was open for 31% -> 31% of each run, Pallas kernels for 13% -> 13%
where the time goes in v6:
time: 477 us; the launch traced here: 468 us
  waiting for transfers between devices  137 us (29%)
  other arithmetic  84.1 us (18%)
  local copies, waits for them, and re-layouts  71.3 us (15%)
  Pallas kernels  61.7 us (13%)
  starting transfers between devices  56.4 us (12%)
  matrix products  43.7 us (9%)
  between operations  13.9 us (3%)
    ppermute x68, waiting for transfers between devices, swap(): lax.ppermute(value, axis, [(place, place ^ bit) for place in range(size)])  137 us
    ppermute x68, starting transfers between devices, swap(): lax.ppermute(value, axis, [(place, place ^ bit) for place in range(size)])  56.4 us
    unnamed x298, local copies, waits for them, and re-layouts  45.2 us
    pallas_call x2, Pallas kernels, mixer_backward(): pl.pallas_call(body, grid=(1, pairs), in_specs=common_specs(slot, length)...  31 us
    dot_general x14, matrix products, tokens_out(): lax.dot_general(left, right, (((0,), (0,)), ((), ())), preferred_element_...  25.2 us
    pallas_call x1, Pallas kernels, mixer_forward(): pl.pallas_call(forward_body, grid=(slots, pairs), in_specs=common_specs(0...  16.5 us
    pallas_call x2, Pallas kernels, input_terms(): pl.pallas_call(input_body, grid_spec=pltpu.PrefetchScalarGridSpec(num_sca...  14.2 us
    select_n x18, other arithmetic, join_halves(): jnp.where(half == 0, mine, other)  11.8 us
  transfers between devices with their start and end apart: 68, of which 32 were waited for; matrix products, arithmetic and copies ran while one was open for 31% of the time, Pallas kernels for 13%

profile of v6, /device:TPU:0, one launch (start us, length us, event | category | flops | bytes accessed | tf_op | source)
XLA Modules:
  0.0 468.3 jit_solution(14978277368281288892)
XLA Ops:
  3.0 3.1 collective-permute-start
  10.1 5.2 %collective-permute-done.1 = bf16[256,512]{1,0:T(8,128)(2,1)S(1)} collective-permute-done((bf16[256,512]{1,0:T(8,128)(2,1)S(1)}, bf16[256,512]{1,0:T(8,128)(2,1)S(1)}, u32[]{:S(2)}, u32[]{:S(2)}) %collective-permute-start.1) | collective-permute-done | bytes 262176 | tf_op jit(solution)/shard_map/ppermute | solution.py:551
  39.0 6.4 %collective-permute-done.4 = bf16[2,160,128]{2,1,0:T(8,128)(2,1)S(1)} collective-permute-done((bf16[2,160,128]{2,1,0:T(8,128)(2,1)S(1)}, bf16[2,160,128]{2,1,0:T(8,128)(2,1)S(1)}, u32[]{:S(2)}, u32[]{:S(2)}) %collective-permute-start.4) | collective-permute-done | bytes 81952 | tf_op jit(solution)/shard_map/ppermute | solution.py:551
  54.4 8.4 %collective-permute-done.6 = bf16[4,160,128]{2,1,0:T(8,128)(2,1)S(1)} collective-permute-done((bf16[4,160,128]{2,1,0:T(8,128)(2,1)S(1)}, bf16[4,160,128]{2,1,0:T(8,128)(2,1)S(1)}, u32[]{:S(2)}, u32[]{:S(2)}) %collective-permute-start.6) | collective-permute-done | bytes 163872 | tf_op jit(solution)/shard_map/ppermute | solution.py:551
  73.3 8.3 %collective-permute-done.11 = bf16[128,2048]{1,0:T(8,128)(2,1)S(1)} collective-permute-done((bf16[128,2048]{1,0:T(8,128)(2,1)}, bf16[128,2048]{1,0:T(8,128)(2,1)S(1)}, u32[]{:S(2)}, u32[]{:S(2)}) %collective-permute-start.11) | collective-permute-done | bytes 524320 | tf_op jit(solution)/shard_map/ppermute | solution.py:551
  83.8 12.4 %collective-permute-done.9 = bf16[512,512]{1,0:T(8,128)(2,1)S(1)} collective-permute-done((bf16[512,512]{1,0:T(8,128)(2,1)S(1)}, bf16[512,512]{1,0:T(8,128)(2,1)S(1)}, u32[]{:S(2)}, u32[]{:S(2)}) %collective-permute-start.9) | collective-permute-done | bytes 524320 | tf_op jit(solution)/shard_map/ppermute | solution.py:551
  107.0 4.8 %collective-permute-done.17 = bf16[8,128,256]{2,1,0:T(8,128)(2,1)} collective-permute-done((bf16[8,128,256]{2,1,0:T(8,128)(2,1)S(1)}, bf16[8,128,256]{2,1,0:T(8,128)(2,1)}, u32[]{:S(2)}, u32[]{:S(2)}) %collective-permute-start.17) | collective-permute-done | bytes 524320 | tf_op jit(solution)/shard_map/ppermute | solution.py:551
  124.7 3.6 fusion.13.x_ref.refs_6_
  128.4 3.7 fusion.11.z_ref.refs_7_
  137.8 6.7 %collective-permute-done.18 = bf16[128,2048]{1,0:T(8,128)(2,1)S(1)} collective-permute-done((bf16[128,2048]{1,0:T(8,128)(2,1)S(1)}, bf16[128,2048]{1,0:T(8,128)(2,1)S(1)}, u32[]{:S(2)}, u32[]{:S(2)}) %collective-permute-start.18) | collective-permute-done | bytes 524320 | tf_op jit(solution)/shard_map/ppermute | solution.py:551
  149.3 16.5 %mixer_forward.1 = (bf16[2,512,512]{2,1,0:T(8,128)(2,1)}, f32[2,512,512]{2,1,0:T(8,128)}, f32[2,512,128]{2,1,0:T(8,128)}) custom-call(f32[2,512,8]{2,1,0:T(8,128)} %copy.138.marks_ref.refs_0_, f32[2,8,512]{2,1,0:T(8,128)} %broadcast_in_dim.28.row_ref.refs_1_, f32[2,512,256]{2,1,0:T(8,128)} %fusion.146.bc_ref.refs_2_, f32[2,512,128]{2,1,0:T(8,128)} %fusion.64.dt_ref.refs_3_, ...), custom_call_target="tpu_custom_call" | custom-call | flops 16000000000 | bytes 1048576 | tf_op jit(solution)/shard_map/mixer_forward/pallas_call | solution.py:387
  190.3 2.9 multiply_convert_fusion
  198.9 3.7 fusion.2.refs_10_
  203.6 15.6 %mixer_backward.2 = (bf16[2,512,512]{2,1,0:T(8,128)(2,1)}, bf16[2,512,512]{2,1,0:T(8,128)(2,1)}, f32[2,512,256]{2,1,0:T(8,128)}, f32[2,512,128]{2,1,0:T(8,128)},...) custom-call(f32[2,512,8]{2,1,0:T(8,128)} %copy.138.marks_ref.refs_0_, ...), custom_call_target="tpu_custom_call" | custom-call | flops 16000000000 | bytes 1048576 | tf_op jit(solution)/shard_map/mixer_backward/pallas_call | solution.py:412
  219.3 2.8 fusion.18
  222.1 3.4 convert_add_fusion
  229.9 15.4 %mixer_backward.3 = (bf16[2,512,512]{2,1,0:T(8,128)(2,1)}, bf16[2,512,512]{2,1,0:T(8,128)(2,1)}, f32[2,512,256]{2,1,0:T(8,128)}, f32[2,512,128]{2,1,0:T(8,128)},...) custom-call(f32[2,512,8]{2,1,0:T(8,128)} %copy.138.marks_ref.refs_0_, ...), custom_call_target="tpu_custom_call", output_to_operand_aliasing={{0}: (12, {}), {1}: (13, {}), {2}: (14, {}), {3}: (15, {}),... | custom-call | flops 16000000000 | bytes 1048576 | tf_op jit(solution)/shard_map/mixer_backward/pallas_call | solution.py:412
  248.5 3.0 convolution_bitcast_fusion
  254.1 3.1 convolution_convert_fusion.3
  275.6 7.0 %input_terms.2 = f32[2,256,2048]{2,1,0:T(8,128)} custom-call(s32[1]{0:T(128)} %bitcast.60.place_ref, bf16[2,2,256,512]{3,2,1,0:T(8,128)(2,1)} %bitcast.380, bf16[2,2,256,512]{3,2,1,0:T(8,128)(2,1)} %bitcast.387, bf16[2,2,256,128]{3,2,1,0:T(8,128)(2,1)} %bitcast.327, bf16[2048,512]{1,0:T(8,128)(2,1)} %copy-done.61, ...), custom_call_target="tpu_custom_call" | custom-call | flops 6000000000 | bytes 1048576 | tf_op jit(solution)/shard_map/input_terms/pallas_call | solution.py:480
  284.2 8.7 %collective-permute-done.36 = bf16[128,2048]{1,0:T(8,128)(2,1)S(1)} collective-permute-done((bf16[128,2048]{1,0:T(8,128)(2,1)}, bf16[128,2048]{1,0:T(8,128)(2,1)S(1)}, u32[]{:S(2)}, u32[]{:S(2)}) %collective-permute-start.36) | collective-permute-done | bytes 524320 | tf_op jit(solution)/shard_map/ppermute | solution.py:551
  298.4 2.9 fusion.19
  303.7 7.2 %input_terms.3 = f32[2,256,2048]{2,1,0:T(8,128)} custom-call(s32[1]{0:T(128)} %bitcast.66.place_ref, bf16[2,2,256,512]{3,2,1,0:T(8,128)(2,1)} %bitcast.381, bf16[2,2,256,512]{3,2,1,0:T(8,128)(2,1)} %bitcast.388, bf16[2,2,256,128]{3,2,1,0:T(8,128)(2,1)} %bitcast.328, bf16[2048,512]{1,0:T(8,128)(2,1)} %copy-done.61, ...), custom_call_target="tpu_custom_call" | custom-call | flops 6000000000 | bytes 1048576 | tf_op jit(solution)/shard_map/input_terms/pallas_call | solution.py:480
  311.0 4.2 add.830
  326.3 4.0 collective-permute-done.42
  330.4 9.6 %collective-permute-done.44 = bf16[512,512]{1,0:T(8,128)(2,1)} collective-permute-done((bf16[512,512]{1,0:T(8,128)(2,1)}, bf16[512,512]{1,0:T(8,128)(2,1)}, u32[]{:S(2)}, u32[]{:S(2)}) %collective-permute-start.44) | collective-permute-done | bytes 524320 | tf_op jit(solution)/shard_map/ppermute | solution.py:551
  343.5 13.2 %collective-permute-done.47 = f32[2,72,256]{2,1,0:T(8,128)S(1)} collective-permute-done((f32[2,72,256]{2,1,0:T(8,128)S(1)}, f32[2,72,256]{2,1,0:T(8,128)S(1)}, u32[]{:S(2)}, u32[]{:S(2)}) %collective-permute-start.47) | collective-permute-done | bytes 147488 | tf_op jit(solution)/shard_map/ppermute | solution.py:551
  361.9 9.6 %collective-permute-done.49 = bf16[128,2048]{1,0:T(8,128)(2,1)S(1)} collective-permute-done((bf16[128,2048]{1,0:T(8,128)(2,1)S(1)}, bf16[128,2048]{1,0:T(8,128)(2,1)S(1)}, u32[]{:S(2)}, u32[]{:S(2)}) %collective-permute-start.49) | collective-permute-done | bytes 524320 | tf_op jit(solution)/shard_map/ppermute | solution.py:551
  375.7 4.8 %collective-permute-done.53 = f32[128,256]{1,0:T(8,128)S(1)} collective-permute-done((f32[128,256]{1,0:T(8,128)S(1)}, f32[128,256]{1,0:T(8,128)S(1)}, u32[]{:S(2)}, u32[]{:S(2)}) %collective-permute-start.53) | collective-permute-done | bytes 131104 | tf_op jit(solution)/shard_map/ppermute | solution.py:551
  380.6 3.5 collective-permute-done.50
  387.0 3.0 collective-permute-done.55
  404.6 2.9 collective-permute-done.60
  (680 shorter events, 244.8 us)
Async XLA Ops:
  17.0 28.4 %collective-permute-start.2 = (bf16[512,512]{1,0:T(8,128)(2,1)}, bf16[512,512]{1,0:T(8,128)(2,1)}, u32[]{:S(2)}, u32[]{:S(2)}) collective-permute-start(bf16[512,512]{1,0:T(8,128)(2,1)} %get-tuple-element.662), channel_id=1, source_target_pairs={{0,16},{4,20},{8,24},{12,28},{16,0},{20,4},{24,8},{28,12},{1,17},{... | collective-permute-start | bytes 1572872 | tf_op jit(solution)/shard_map/ppermute | solution.py:551
  19.6 25.8 %collective-permute-start.3 = (bf16[512,512]{1,0:T(8,128)(2,1)}, bf16[512,512]{1,0:T(8,128)(2,1)}, u32[]{:S(2)}, u32[]{:S(2)}) collective-permute-start(bf16[512,512]{1,0:T(8,128)(2,1)} %get-tuple-element.662), channel_id=1, source_target_pairs={{0,4},{4,0},{8,12},{12,8},{16,20},{20,16},{24,28},{28,24},{1,5},{5... | collective-permute-start | bytes 1572872 | tf_op jit(solution)/shard_map/ppermute | solution.py:551
  22.1 23.3 %collective-permute-start.4 = (bf16[2,160,128]{2,1,0:T(8,128)(2,1)S(1)}, bf16[2,160,128]{2,1,0:T(8,128)(2,1)S(1)}, u32[]{:S(2)}, u32[]{:S(2)}) collective-permute-start(bf16[2,160,128]{2,1,0:T(8,128)(2,1)S(1)} %pad_maximum_fusion.17), channel_id=1, source_target_pairs={{0,16},{4,20},{8,24},{12,28},{16,0},{20,4},{24,8},{28,12},{1,17},{... | collective-permute-start | bytes 245768 | tf_op jit(solution)/shard_map/ppermute | solution.py:551
  45.4 20.9 %collective-permute-start.5 = (bf16[512,512]{1,0:T(8,128)(2,1)}, bf16[512,512]{1,0:T(8,128)(2,1)}, u32[]{:S(2)}, u32[]{:S(2)}) collective-permute-start(bf16[512,512]{1,0:T(8,128)(2,1)} %collective-permute-done.2), channel_id=1, source_target_pairs={{0,4},{4,0},{8,12},{12,8},{16,20},{20,16},{24,28},{28,24},{1,5},{5... | collective-permute-start | bytes 1572872 | tf_op jit(solution)/shard_map/ppermute | solution.py:551
  46.8 19.5 %collective-permute-start.8 = (bf16[128,2048]{1,0:T(8,128)(2,1)}, bf16[128,2048]{1,0:T(8,128)(2,1)}, u32[]{:S(2)}, u32[]{:S(2)}) collective-permute-start(bf16[128,2048]{1,0:T(8,128)(2,1)} %get-tuple-element.200), channel_id=1, source_target_pairs={{0,8},{4,12},{8,0},{12,4},{16,24},{20,28},{24,16},{28,20},{1,9},{5... | collective-permute-start | bytes 1572872 | tf_op jit(solution)/shard_map/ppermute | solution.py:551
  48.6 17.7 %collective-permute-start.7 = (bf16[256,512]{1,0:T(8,128)(2,1)}, bf16[256,512]{1,0:T(8,128)(2,1)}, u32[]{:S(2)}, u32[]{:S(2)}) collective-permute-start(bf16[256,512]{1,0:T(8,128)(2,1)} %get-tuple-element.199), channel_id=1, source_target_pairs={{0,8},{4,12},{8,0},{12,4},{16,24},{20,28},{24,16},{28,20},{1,9},{5... | collective-permute-start | bytes 786440 | tf_op jit(solution)/shard_map/ppermute | solution.py:551
  70.3 25.9 %collective-permute-start.9 = (bf16[512,512]{1,0:T(8,128)(2,1)S(1)}, bf16[512,512]{1,0:T(8,128)(2,1)S(1)}, u32[]{:S(2)}, u32[]{:S(2)}) collective-permute-start(bf16[512,512]{1,0:T(8,128)(2,1)S(1)} %get-tuple-element.658), channel_id=1, source_target_pairs={{0,16},{4,20},{8,24},{12,28},{16,0},{20,4},{24,8},{28,12},{1,17},{... | collective-permute-start | bytes 1572872 | tf_op jit(solution)/shard_map/ppermute | solution.py:551
  70.8 25.4 %collective-permute-start.10 = (bf16[512,512]{1,0:T(8,128)(2,1)S(1)}, bf16[512,512]{1,0:T(8,128)(2,1)S(1)}, u32[]{:S(2)}, u32[]{:S(2)}) collective-permute-start(bf16[512,512]{1,0:T(8,128)(2,1)S(1)} %get-tuple-element.658), channel_id=1, source_target_pairs={{0,4},{4,0},{8,12},{12,8},{16,20},{20,16},{24,28},{28,24},{1,5},{5... | collective-permute-start | bytes 1572872 | tf_op jit(solution)/shard_map/ppermute | solution.py:551
  96.2 16.8 %collective-permute-start.16 = (bf16[256,2048]{1,0:T(8,128)(2,1)}, bf16[256,2048]{1,0:T(8,128)(2,1)}, u32[]{:S(2)}, u32[]{:S(2)}) collective-permute-start(bf16[256,2048]{1,0:T(8,128)(2,1)} %pad_maximum_fusion.2), channel_id=1, source_target_pairs={{0,1},{1,0},{2,3},{3,2},{4,5},{5,4},{6,7},{7,6},{8,9},{9,8},{10,11... | collective-permute-start | bytes 3145736 | tf_op jit(solution)/shard_map/ppermute | solution.py:551
  101.8 17.6 %collective-permute-start.13 = (bf16[512,512]{1,0:T(8,128)(2,1)}, bf16[512,512]{1,0:T(8,128)(2,1)S(1)}, u32[]{:S(2)}, u32[]{:S(2)}) collective-permute-start(bf16[512,512]{1,0:T(8,128)(2,1)} %copy-done.45), channel_id=1, source_target_pairs={{0,4},{4,0},{8,12},{12,8},{16,20},{20,16},{24,28},{28,24},{1,5},{5... | collective-permute-start | bytes 1572872 | tf_op jit(solution)/shard_map/ppermute | solution.py:551
  102.3 17.2 %collective-permute-start.14 = (bf16[256,512]{1,0:T(8,128)(2,1)}, bf16[256,512]{1,0:T(8,128)(2,1)S(1)}, u32[]{:S(2)}, u32[]{:S(2)}) collective-permute-start(bf16[256,512]{1,0:T(8,128)(2,1)} %get-tuple-element.213), channel_id=1, source_target_pairs={{0,8},{4,12},{8,0},{12,4},{16,24},{20,28},{24,16},{28,20},{1,9},{5... | collective-permute-start | bytes 786440 | tf_op jit(solution)/shard_map/ppermute | solution.py:551
  102.3 19.4 %collective-permute-start.15 = (bf16[128,2048]{1,0:T(8,128)(2,1)}, bf16[128,2048]{1,0:T(8,128)(2,1)S(1)}, u32[]{:S(2)}, u32[]{:S(2)}) collective-permute-start(bf16[128,2048]{1,0:T(8,128)(2,1)} %get-tuple-element.214), channel_id=1, source_target_pairs={{0,8},{4,12},{8,0},{12,4},{16,24},{20,28},{24,16},{28,20},{1,9},{5... | collective-permute-start | bytes 1572872 | tf_op jit(solution)/shard_map/ppermute | solution.py:551
  122.6 25.2 %collective-permute-start.20 = (bf16[512,512]{1,0:T(8,128)(2,1)}, bf16[512,512]{1,0:T(8,128)(2,1)}, u32[]{:S(2)}, u32[]{:S(2)}) collective-permute-start(bf16[512,512]{1,0:T(8,128)(2,1)} %get-tuple-element.653), channel_id=1, source_target_pairs={{0,16},{4,20},{8,24},{12,28},{16,0},{20,4},{24,8},{28,12},{1,17},{... | collective-permute-start | bytes 1572872 | tf_op jit(solution)/shard_map/ppermute | solution.py:551
  123.2 45.9 %collective-permute-start.21 = (bf16[512,512]{1,0:T(8,128)(2,1)}, bf16[512,512]{1,0:T(8,128)(2,1)}, u32[]{:S(2)}, u32[]{:S(2)}) collective-permute-start(bf16[512,512]{1,0:T(8,128)(2,1)} %get-tuple-element.653), channel_id=1, source_target_pairs={{0,4},{4,0},{8,12},{12,8},{16,20},{20,16},{24,28},{28,24},{1,5},{5... | collective-permute-start | bytes 1572872 | tf_op jit(solution)/shard_map/ppermute | solution.py:551
  146.4 26.3 %collective-permute-start.19 = (bf16[256,2048]{1,0:T(8,128)(2,1)}, bf16[256,2048]{1,0:T(8,128)(2,1)}, u32[]{:S(2)}, u32[]{:S(2)}) collective-permute-start(bf16[256,2048]{1,0:T(8,128)(2,1)} %pad_maximum_fusion.4), channel_id=1, source_target_pairs={{0,1},{1,0},{2,3},{3,2},{4,5},{5,4},{6,7},{7,6},{8,9},{9,8},{10,11... | collective-permute-start | bytes 3145736 | tf_op jit(solution)/shard_map/ppermute | solution.py:551
  147.8 23.1 %collective-permute-start.22 = (bf16[512,512]{1,0:T(8,128)(2,1)}, bf16[512,512]{1,0:T(8,128)(2,1)}, u32[]{:S(2)}, u32[]{:S(2)}) collective-permute-start(bf16[512,512]{1,0:T(8,128)(2,1)} %collective-permute-done.20), channel_id=1, source_target_pairs={{0,4},{4,0},{8,12},{12,8},{16,20},{20,16},{24,28},{28,24},{1,5},{5... | collective-permute-start | bytes 1572872 | tf_op jit(solution)/shard_map/ppermute | solution.py:551
  186.6 16.1 %collective-permute-start.26 = (bf16[2,256,2048]{2,1,0:T(8,128)(2,1)S(1)}, bf16[2,256,2048]{2,1,0:T(8,128)(2,1)}, u32[]{:S(2)}, u32[]{:S(2)}) collective-permute-start(bf16[2,256,2048]{2,1,0:T(8,128)(2,1)S(1)} %dynamic-slice_convert_fusion), channel_id=1, source_target_pairs={{0,1},{1,0},{2,3},{3,2},{4,5},{5,4},{6,7},{7,6},{8,9},{9,8},{10,11... | collective-permute-start | bytes 6291464 | tf_op jit(solution)/shard_map/ppermute | solution.py:551
  194.8 24.4 %collective-permute-start.27 = (bf16[512,512]{1,0:T(8,128)(2,1)}, bf16[512,512]{1,0:T(8,128)(2,1)S(1)}, u32[]{:S(2)}, u32[]{:S(2)}) collective-permute-start(bf16[512,512]{1,0:T(8,128)(2,1)} %convolution_convert_fusion.5), channel_id=1, source_target_pairs={{0,4},{4,0},{8,12},{12,8},{16,20},{20,16},{24,28},{28,24},{1,5},{5... | collective-permute-start | bytes 1572872 | tf_op jit(solution)/shard_map/ppermute | solution.py:551
  196.8 54.8 %collective-permute-start.28 = (bf16[512,512]{1,0:T(8,128)(2,1)}, bf16[512,512]{1,0:T(8,128)(2,1)}, u32[]{:S(2)}, u32[]{:S(2)}) collective-permute-start(bf16[512,512]{1,0:T(8,128)(2,1)} %convolution_convert_fusion.4), channel_id=1, source_target_pairs={{0,4},{4,0},{8,12},{12,8},{16,20},{20,16},{24,28},{28,24},{1,5},{5... | collective-permute-start | bytes 1572872 | tf_op jit(solution)/shard_map/ppermute | solution.py:551
  227.7 23.9 %collective-permute-start.29 = (bf16[2,128,2048]{2,1,0:T(8,128)(2,1)S(1)}, bf16[2,128,2048]{2,1,0:T(8,128)(2,1)}, u32[]{:S(2)}, u32[]{:S(2)}) collective-permute-start(bf16[2,128,2048]{2,1,0:T(8,128)(2,1)S(1)} %dynamic-slice_convert_fusion.2), channel_id=1, source_target_pairs={{0,2},{1,3},{2,0},{3,1},{4,6},{5,7},{6,4},{7,5},{8,10},{9,11},{10,... | collective-permute-start | bytes 3145736 | tf_op jit(solution)/shard_map/ppermute | solution.py:551
  229.2 28.0 %collective-permute-start.31 = (bf16[512,512]{1,0:T(8,128)(2,1)}, bf16[512,512]{1,0:T(8,128)(2,1)}, u32[]{:S(2)}, u32[]{:S(2)}) collective-permute-start(bf16[512,512]{1,0:T(8,128)(2,1)} %fusion.18), channel_id=1, source_target_pairs={{0,16},{4,20},{8,24},{12,28},{16,0},{20,4},{24,8},{28,12},{1,17},{... | collective-permute-start | bytes 1572872 | tf_op jit(solution)/shard_map/ppermute | solution.py:551
  263.0 21.3 %collective-permute-start.33 = (bf16[512,512]{1,0:T(8,128)(2,1)}, bf16[512,512]{1,0:T(8,128)(2,1)}, u32[]{:S(2)}, u32[]{:S(2)}) collective-permute-start(bf16[512,512]{1,0:T(8,128)(2,1)} %convolution_convert_fusion.3), channel_id=1, source_target_pairs={{0,4},{4,0},{8,12},{12,8},{16,20},{20,16},{24,28},{28,24},{1,5},{5... | collective-permute-start | bytes 1572872 | tf_op jit(solution)/shard_map/ppermute | solution.py:551
  273.5 19.4 %collective-permute-start.36 = (bf16[128,2048]{1,0:T(8,128)(2,1)}, bf16[128,2048]{1,0:T(8,128)(2,1)S(1)}, u32[]{:S(2)}, u32[]{:S(2)}) collective-permute-start(bf16[128,2048]{1,0:T(8,128)(2,1)} %fusion.62), channel_id=1, source_target_pairs={{0,8},{4,12},{8,0},{12,4},{16,24},{20,28},{24,16},{28,20},{1,9},{5... | collective-permute-start | bytes 1572872 | tf_op jit(solution)/shard_map/ppermute | solution.py:551
  275.1 35.8 %collective-permute-start.38 = (bf16[512,512]{1,0:T(8,128)(2,1)}, bf16[512,512]{1,0:T(8,128)(2,1)}, u32[]{:S(2)}, u32[]{:S(2)}) collective-permute-start(bf16[512,512]{1,0:T(8,128)(2,1)} %convolution_convert_fusion.2), channel_id=1, source_target_pairs={{0,4},{4,0},{8,12},{12,8},{16,20},{20,16},{24,28},{28,24},{1,5},{5... | collective-permute-start | bytes 1572872 | tf_op jit(solution)/shard_map/ppermute | solution.py:551
  282.6 47.8 %collective-permute-start.43 = (bf16[1024,512]{1,0:T(8,128)(2,1)}, bf16[1024,512]{1,0:T(8,128)(2,1)}, u32[]{:S(2)}, u32[]{:S(2)}) collective-permute-start(bf16[1024,512]{1,0:T(8,128)(2,1)} %pad_maximum_fusion.5), channel_id=1, source_target_pairs={{0,4},{4,0},{8,12},{12,8},{16,20},{20,16},{24,28},{28,24},{1,5},{5... | collective-permute-start | bytes 3145736 | tf_op jit(solution)/shard_map/ppermute | solution.py:551
  294.3 16.7 %collective-permute-start.39 = (f32[2,256,2048]{2,1,0:T(8,128)}, f32[2,256,2048]{2,1,0:T(8,128)}, u32[]{:S(2)}, u32[]{:S(2)}) collective-permute-start(f32[2,256,2048]{2,1,0:T(8,128)} %input_terms.2), channel_id=1, source_target_pairs={{0,1},{1,0},{2,3},{3,2},{4,5},{5,4},{6,7},{7,6},{8,9},{9,8},{10,11... | collective-permute-start | bytes 12582920 | tf_op jit(solution)/shard_map/ppermute | solution.py:551
  295.1 15.9 %collective-permute-start.40 = (bf16[128,2048]{1,0:T(8,128)(2,1)S(1)}, bf16[128,2048]{1,0:T(8,128)(2,1)}, u32[]{:S(2)}, u32[]{:S(2)}) collective-permute-start(bf16[128,2048]{1,0:T(8,128)(2,1)S(1)} %constant_dynamic-update-slice_fusion.56), channel_id=1, source_target_pairs={{0,2},{1,3},{2,0},{3,1},{4,6},{5,7},{6,4},{7,5},{8,10},{9,11},{10,... | collective-permute-start | bytes 1572872 | tf_op jit(solution)/shard_map/ppermute | solution.py:551
  301.4 38.5 %collective-permute-start.44 = (bf16[512,512]{1,0:T(8,128)(2,1)}, bf16[512,512]{1,0:T(8,128)(2,1)}, u32[]{:S(2)}, u32[]{:S(2)}) collective-permute-start(bf16[512,512]{1,0:T(8,128)(2,1)} %fusion.19), channel_id=1, source_target_pairs={{0,16},{4,20},{8,24},{12,28},{16,0},{20,4},{24,8},{28,12},{1,17},{... | collective-permute-start | bytes 1572872 | tf_op jit(solution)/shard_map/ppermute | solution.py:551
  319.6 37.5 %collective-permute-start.46 = (bf16[512,512]{1,0:T(8,128)(2,1)S(1)}, bf16[512,512]{1,0:T(8,128)(2,1)S(1)}, u32[]{:S(2)}, u32[]{:S(2)}) collective-permute-start(bf16[512,512]{1,0:T(8,128)(2,1)S(1)} %fusion.20), channel_id=1, source_target_pairs={{0,16},{4,20},{8,24},{12,28},{16,0},{20,4},{24,8},{28,12},{1,17},{... | collective-permute-start | bytes 1572872 | tf_op jit(solution)/shard_map/ppermute | solution.py:551
  322.9 33.9 %collective-permute-start.45 = (bf16[2,128,2048]{2,1,0:T(8,128)(2,1)S(1)}, bf16[2,128,2048]{2,1,0:T(8,128)(2,1)S(1)}, u32[]{:S(2)}, u32[]{:S(2)}) collective-permute-start(bf16[2,128,2048]{2,1,0:T(8,128)(2,1)S(1)} %dynamic-slice_convert_fusion.1), channel_id=1, source_target_pairs={{0,2},{1,3},{2,0},{3,1},{4,6},{5,7},{6,4},{7,5},{8,10},{9,11},{10,... | collective-permute-start | bytes 3145736 | tf_op jit(solution)/shard_map/ppermute | solution.py:551
  340.0 16.7 %collective-permute-start.47 = (f32[2,72,256]{2,1,0:T(8,128)S(1)}, f32[2,72,256]{2,1,0:T(8,128)S(1)}, u32[]{:S(2)}, u32[]{:S(2)}) collective-permute-start(f32[2,72,256]{2,1,0:T(8,128)S(1)} %slice.379), channel_id=1, source_target_pairs={{0,16},{4,20},{8,24},{12,28},{16,0},{20,4},{24,8},{28,12},{1,17},{... | collective-permute-start | bytes 442376 | tf_op jit(solution)/shard_map/ppermute | solution.py:551
  343.4 16.1 %collective-permute-start.51 = (bf16[256,2048]{1,0:T(8,128)(2,1)S(1)}, bf16[256,2048]{1,0:T(8,128)(2,1)S(1)}, u32[]{:S(2)}, u32[]{:S(2)}) collective-permute-start(bf16[256,2048]{1,0:T(8,128)(2,1)S(1)} %pad_maximum_fusion.7), channel_id=1, source_target_pairs={{0,1},{1,0},{2,3},{3,2},{4,5},{5,4},{6,7},{7,6},{8,9},{9,8},{10,11... | collective-permute-start | bytes 3145736 | tf_op jit(solution)/shard_map/ppermute | solution.py:551
  (141 other events, 1777.7 us)
